TPU v7x, 32 devices: a whole 2x2x4 slice. The times are simulated.
32 devices in a mesh: dom: 16 (over z, y, x), col: 2 (over core).
Axes of the slice: x: 2, y: 2, z: 4, core: 2. Of those that a mesh axis runs over, the one named last changes fastest.
Arguments:
- diag_blocks: bfloat16 [3072, 128, 128], P(('dom', 'col')), may hold values from -0.375 to 0.375
- couplings: bfloat16 [3072, 6, 128], P(('dom', 'col')), may hold values from -1.1953125 to 1.1953125
- columns: int32 [3072, 6], P(('dom', 'col')), may hold values from 0 to 119, as said below
- send_rows: int32 [32, 24], P(('dom', 'col')), may hold values from 0 to 95
- shifts: float32 [6], replicated, may hold values from -0.5 to 0.5
- start_vector: float32 [3072, 128], P(('dom', 'col')), may hold values from -30 to 30
- sketch: bfloat16 [32, 3072, 128], P(None, ('dom', 'col')), may hold values from -0.0017089844 to 0.0017089844
Outputs:
- orthonormal: float32 [7, 3072, 128], P(None, ('dom', 'col'))
- factor: float32 [7, 7], replicated
- sketch_factor: float32 [7, 7], replicated
Inputs may be any that keep to these rules, and one draw needn't show every extreme that they name: `columns`: each device's column indices point into its extended vector: its 96 own row blocks, then 4 blocks from the lower col neighbour, 4 from the upper one, then 4 from the dom partner of each bisection level, lowest level first. Every received position is read by some block row of the device. `send_rows`: per device: the first 4 entries go to the lower col neighbour, the next 4 to the upper one, then 4 to the dom partner of each level, lowest level first.
All inputs are finite; a program needn't handle non-finite values.
Results may differ from a plain program's by a relative error of at most 0.0003.
Values sent between devices are 32-bit elements; how exact they have to be, the bound alone decides.
No kernel may reach another device: no remote copies, remote signals or barrier semaphores. Data moves between devices by JAX's collectives and lax.ppermute only.
A program may use at most 64 MiB of HBM per device.

v0:
```python
import jax
import jax.numpy as jnp
from jax import lax
from jax.sharding import PartitionSpec as P

highest = lax.Precision.HIGHEST


def with_halo(value, sides, width):
    for axis, dim in sides:
        count, length = (lax.axis_size(axis), value.shape[dim])
        up = [(i, (i + 1) % count) for i in range(count - 1)]
        down = [(j, i) for i, j in up]
        last = lax.slice_in_dim(value, length - width, length, axis=dim)
        first = lax.slice_in_dim(value, 0, width, axis=dim)
        before = lax.ppermute(last, axis, up)
        after = lax.ppermute(first, axis, down)
        value = jnp.concatenate([before, value, after], axis=dim)
    return value


def from_partner(value, axis, apart):
    return lax.ppermute(value, axis, [(i, i ^ 1 << apart) for i in range(lax.axis_size(axis))])


def cholesky_upper(gram_matrix):
    order_size = gram_matrix.shape[0]
    zero_entry = jnp.zeros((), gram_matrix.dtype)
    upper = [[zero_entry for col_index in range(order_size)] for row_index in range(order_size)]
    for pivot in range(order_size):
        diag_value = gram_matrix[pivot, pivot]
        for inner in range(pivot):
            diag_value = diag_value - upper[inner][pivot] * upper[inner][pivot]
        root_value = jnp.sqrt(diag_value)
        upper[pivot][pivot] = root_value
        for later in range(pivot + 1, order_size):
            entry = gram_matrix[pivot, later]
            for inner in range(pivot):
                entry = entry - upper[inner][pivot] * upper[inner][later]
            upper[pivot][later] = entry / root_value
    return jnp.stack([jnp.stack(row_list) for row_list in upper])


def upper_inverse(triangle):
    order_size = triangle.shape[0]
    zero_entry = jnp.zeros((), triangle.dtype)
    inverse = [[zero_entry for col_index in range(order_size)] for row_index in range(order_size)]
    for target in range(order_size):
        inverse[target][target] = 1.0 / triangle[target, target]
        for row_index in range(target - 1, -1, -1):
            entry = zero_entry
            for inner in range(row_index + 1, target + 1):
                entry = entry + triangle[row_index, inner] * inverse[inner][target]
            inverse[row_index][target] = -entry / triangle[row_index, row_index]
    return jnp.stack([jnp.stack(row_list) for row_list in inverse])


def combine_vectors(krylov, mixing):
    return jnp.einsum("krj,kl->lrj", krylov, mixing, precision=highest)


def shards(diag_blocks, couplings, columns, send_rows, shifts, start_vector, sketch):
    levels = lax.axis_size("dom").bit_length() - 1
    row_blocks, block_width = start_vector.shape
    face_blocks = send_rows.shape[1] // (2 + levels)
    send_list = send_rows[0]
    wide_blocks = diag_blocks.astype(jnp.float32)
    wide_couplings = couplings.astype(jnp.float32)
    vectors = [start_vector]
    for power_index in range(shifts.shape[0]):
        vector_in = vectors[-1]
        own_term = jnp.einsum("rij,rj->ri", wide_blocks, vector_in, precision=highest)
        outgoing = vector_in[send_list]
        col_side = with_halo(outgoing[: 2 * face_blocks], (("col", 0),), face_blocks)
        from_lower = col_side[:face_blocks]
        from_upper = col_side[3 * face_blocks :]
        bisect_out = outgoing[2 * face_blocks :]
        received = []
        for level_index in range(levels):
            level_piece = bisect_out[level_index * face_blocks : (level_index + 1) * face_blocks]
            received.append(from_partner(level_piece, "dom", level_index))
        remote = jnp.concatenate(received, axis=0)
        extended = jnp.concatenate([vector_in, from_lower, from_upper, remote], axis=0)
        neighbour_blocks = extended[columns]
        vectors.append(
            own_term
            + jnp.sum(wide_couplings * neighbour_blocks, axis=1)
            - shifts[power_index] * vectors[-1]
        )
    krylov = jnp.stack(vectors)
    total_rows = row_blocks * block_width * lax.axis_size("dom") * lax.axis_size("col")
    sketch_part = jnp.einsum("krj,srj->ks", krylov, sketch.astype(jnp.float32), precision=highest)
    sketched = lax.psum(sketch_part, ("dom", "col"))
    sketch_factor = cholesky_upper(jnp.dot(sketched, sketched.T, precision=highest))
    whitened = combine_vectors(krylov, upper_inverse(sketch_factor))
    local_gram = jnp.einsum("krj,lrj->kl", whitened, whitened, precision=highest)
    gram_matrix = lax.psum(local_gram, ("dom", "col")) / total_rows
    gram_factor = cholesky_upper(gram_matrix)
    orthonormal = combine_vectors(whitened, upper_inverse(gram_factor))
    factor = jnp.dot(gram_factor, sketch_factor, precision=highest)
    return (orthonormal, factor, sketch_factor)


def solution(mesh):
    in_specs = (
        P(("dom", "col"), None, None),
        P(("dom", "col"), None, None),
        P(("dom", "col"), None),
        P(("dom", "col"), None),
        P(),
        P(("dom", "col"), None),
        P(None, ("dom", "col"), None),
    )
    out_specs = (P(None, ("dom", "col"), None), P(), P())
    return jax.shard_map(shards, mesh=mesh, in_specs=in_specs, out_specs=out_specs, check_vma=False)
```

profile of v0, /device:TPU:0, one launch (start us, length us, event | category | flops | bytes accessed | tf_op | source)
XLA Modules:
  0.0 390.0 jit_solution(2846807409633811433)
XLA Ops:
  3.0 2.4 collective-permute-start
  6.7 2.4 collective-permute-start.2
  12.9 5.8 %fusion.47 = f32[96,1,128]{2,1,0:T(1,128)S(1)} fusion(bf16[96,128,128]{2,1,0:T(8,128)(2,1)S(1)} %copy-done, f32[96,128,1]{1,2,0:T(1,128)} %bitcast.324), kind=kOutput, calls=%fused_computation.92 | convolution fusion | flops 18874368 | bytes 3244032 | tf_op jit(solution)/shard_map/rij,rj->ri/dot_general | solution.py:72
  19.6 2.7 collective-permute-start.5
  22.3 1.9 collective-permute-done.5
  24.2 2.2 gather_fusion.1
  26.5 1.8 reshape.309
  31.2 2.6 collective-permute-start.11
  37.5 4.9 %fusion.48 = f32[96,1,128]{2,1,0:T(1,128)S(1)} fusion(f32[96,128,1]{1,2,0:T(1,128)S(1)} %bitcast.314, bf16[96,128,128]{2,1,0:T(8,128)(2,1)S(1)} %copy-done), kind=kOutput, calls=%fused_computation.93 | convolution fusion | flops 18874368 | bytes 3244032 | tf_op jit(solution)/shard_map/rij,rj->ri/dot_general | solution.py:72
  42.6 2.2 gather_fusion.3
  44.8 1.8 reshape.325
  48.9 2.5 collective-permute-start.12
  57.7 4.9 %fusion.49 = f32[96,1,128]{2,1,0:T(1,128)S(1)} fusion(f32[96,128,1]{1,2,0:T(1,128)S(1)} %bitcast.316, bf16[96,128,128]{2,1,0:T(8,128)(2,1)S(1)} %copy-done), kind=kOutput, calls=%fused_computation.94 | convolution fusion | flops 18874368 | bytes 3244032 | tf_op jit(solution)/shard_map/rij,rj->ri/dot_general | solution.py:72
  62.7 2.2 gather_fusion.5
  65.0 1.8 reshape.341
  69.1 1.9 collective-permute-start.18
  74.0 2.6 collective-permute-start.23
  76.6 4.9 %fusion.50 = f32[96,1,128]{2,1,0:T(1,128)S(1)} fusion(f32[96,128,1]{1,2,0:T(1,128)S(1)} %bitcast.318, bf16[96,128,128]{2,1,0:T(8,128)(2,1)S(1)} %copy-done), kind=kOutput, calls=%fused_computation.95 | convolution fusion | flops 18874368 | bytes 3244032 | tf_op jit(solution)/shard_map/rij,rj->ri/dot_general | solution.py:72
  81.7 2.2 gather_fusion.7
  83.9 1.8 reshape.357
  88.1 1.9 collective-permute-start.24
  96.3 4.9 %fusion.51 = f32[96,1,128]{2,1,0:T(1,128)S(1)} fusion(f32[96,128,1]{1,2,0:T(1,128)S(1)} %bitcast.320, bf16[96,128,128]{2,1,0:T(8,128)(2,1)S(1)} %copy-done), kind=kOutput, calls=%fused_computation.96 | convolution fusion | flops 18874368 | bytes 3244032 | tf_op jit(solution)/shard_map/rij,rj->ri/dot_general | solution.py:72
  101.4 2.2 gather_fusion.9
  103.6 1.8 reshape.373
  107.7 1.9 collective-permute-start.30
  112.4 2.6 collective-permute-start.35
  115.1 4.9 %fusion.52 = f32[96,1,128]{2,1,0:T(1,128)S(1)} fusion(f32[96,128,1]{1,2,0:T(1,128)S(1)} %bitcast.322, bf16[96,128,128]{2,1,0:T(8,128)(2,1)S(1)} %copy-done), kind=kOutput, calls=%fused_computation.97 | convolution fusion | flops 18874368 | bytes 3244032 | tf_op jit(solution)/shard_map/rij,rj->ri/dot_general | solution.py:72
  120.1 2.2 gather_fusion.11
  122.4 1.8 reshape.389
  128.0 2.1 convolution_bitcast_fusion.1
  130.1 40.4 %psum.14 = f32[7,32]{1,0:T(8,128)S(1)} all-reduce(f32[7,32]{1,0:T(8,128)S(1)} %convolution_bitcast_fusion.1), channel_id=1, replica_groups=mesh['dom'=16,'col'=2] {'dom','col'}, use_global_device_ids=true, to_apply=%region_6.0 | all-reduce | flops 224 | bytes 1792 | tf_op jit(solution)/shard_map/psum | solution.py:93
  258.5 38.9 %psum.15 = f32[7,7]{1,0:T(8,128)S(1)} all-reduce(f32[7,7]{1,0:T(8,128)S(1)} %convolution_bitcast_fusion), channel_id=1, replica_groups=mesh['dom'=16,'col'=2] {'dom','col'}, use_global_device_ids=true, to_apply=%region_7.0 | all-reduce | flops 49 | bytes 392 | tf_op jit(solution)/shard_map/psum | solution.py:97
  (202 shorter events, 83.8 us)
Async XLA Ops:
  3.0 16.6 %collective-permute-start = (f32[4,128]{1,0:T(4,128)S(1)}, f32[4,128]{1,0:T(4,128)S(1)}, u32[]{:S(2)}, u32[]{:S(2)}) collective-permute-start(f32[4,128]{1,0:T(4,128)S(1)} %get-tuple-element.44), channel_id=1, source_target_pairs={{0,1},{2,3},{4,5},{6,7},{8,9},{10,11},{12,13},{14,15},{16,17},{18,... | collective-permute-start | bytes 6152 | tf_op jit(solution)/shard_map/ppermute | solution.py:16
  5.4 16.9 %collective-permute-start.1 = (f32[4,128]{1,0:T(4,128)S(1)}, f32[4,128]{1,0:T(4,128)S(1)}, u32[]{:S(2)}, u32[]{:S(2)}) collective-permute-start(f32[4,128]{1,0:T(4,128)S(1)} %get-tuple-element.43), channel_id=1, source_target_pairs={{1,0},{3,2},{5,4},{7,6},{9,8},{11,10},{13,12},{15,14},{17,16},{19,... | collective-permute-start | bytes 6152 | tf_op jit(solution)/shard_map/ppermute | solution.py:17
  6.7 15.6 %collective-permute-start.2 = (f32[4,128]{1,0:T(4,128)S(1)}, f32[4,128]{1,0:T(4,128)S(1)}, u32[]{:S(2)}, u32[]{:S(2)}) collective-permute-start(f32[4,128]{1,0:T(4,128)S(1)} %get-tuple-element.42), channel_id=1, source_target_pairs={{0,2},{2,0},{4,6},{6,4},{8,10},{10,8},{12,14},{14,12},{16,18},{18,... | collective-permute-start | bytes 6152 | tf_op jit(solution)/shard_map/ppermute | solution.py:23
  9.1 13.2 %collective-permute-start.3 = (f32[4,128]{1,0:T(4,128)S(1)}, f32[4,128]{1,0:T(4,128)S(1)}, u32[]{:S(2)}, u32[]{:S(2)}) collective-permute-start(f32[4,128]{1,0:T(4,128)S(1)} %get-tuple-element.41), channel_id=1, source_target_pairs={{0,4},{2,6},{4,0},{6,2},{8,12},{10,14},{12,8},{14,10},{16,20},{18,... | collective-permute-start | bytes 6152 | tf_op jit(solution)/shard_map/ppermute | solution.py:23
  10.6 11.7 %collective-permute-start.4 = (f32[4,128]{1,0:T(4,128)S(1)}, f32[4,128]{1,0:T(4,128)S(1)}, u32[]{:S(2)}, u32[]{:S(2)}) collective-permute-start(f32[4,128]{1,0:T(4,128)S(1)} %get-tuple-element.40), channel_id=1, source_target_pairs={{0,8},{2,10},{4,12},{6,14},{8,0},{10,2},{12,4},{14,6},{16,24},{18,... | collective-permute-start | bytes 6152 | tf_op jit(solution)/shard_map/ppermute | solution.py:23
  30.7 6.3 %collective-permute-start.10 = (f32[4,128]{1,0:T(4,128)S(1)}, f32[4,128]{1,0:T(4,128)S(1)}, u32[]{:S(2)}, u32[]{:S(2)}) collective-permute-start(f32[4,128]{1,0:T(4,128)S(1)} %get-tuple-element.34), channel_id=1, source_target_pairs={{0,8},{2,10},{4,12},{6,14},{8,0},{10,2},{12,4},{14,6},{16,24},{18,... | collective-permute-start | bytes 6152 | tf_op jit(solution)/shard_map/ppermute | solution.py:23
  31.2 11.2 %collective-permute-start.11 = (f32[4,128]{1,0:T(4,128)S(1)}, f32[4,128]{1,0:T(4,128)S(1)}, u32[]{:S(2)}, u32[]{:S(2)}) collective-permute-start(f32[4,128]{1,0:T(4,128)S(1)} %get-tuple-element.33), channel_id=1, source_target_pairs={{0,16},{2,18},{4,20},{6,22},{8,24},{10,26},{12,28},{14,30},{16,0},... | collective-permute-start | bytes 6152 | tf_op jit(solution)/shard_map/ppermute | solution.py:23
  33.8 8.7 %collective-permute-start.6 = (f32[4,128]{1,0:T(4,128)S(1)}, f32[4,128]{1,0:T(4,128)S(1)}, u32[]{:S(2)}, u32[]{:S(2)}) collective-permute-start(f32[4,128]{1,0:T(4,128)S(1)} %get-tuple-element.38), channel_id=1, source_target_pairs={{0,1},{2,3},{4,5},{6,7},{8,9},{10,11},{12,13},{14,15},{16,17},{18,... | collective-permute-start | bytes 6152 | tf_op jit(solution)/shard_map/ppermute | solution.py:16
  35.1 7.4 %collective-permute-start.7 = (f32[4,128]{1,0:T(4,128)S(1)}, f32[4,128]{1,0:T(4,128)S(1)}, u32[]{:S(2)}, u32[]{:S(2)}) collective-permute-start(f32[4,128]{1,0:T(4,128)S(1)} %get-tuple-element.37), channel_id=1, source_target_pairs={{1,0},{3,2},{5,4},{7,6},{9,8},{11,10},{13,12},{15,14},{17,16},{19,... | collective-permute-start | bytes 6152 | tf_op jit(solution)/shard_map/ppermute | solution.py:17
  36.4 6.1 %collective-permute-start.8 = (f32[4,128]{1,0:T(4,128)S(1)}, f32[4,128]{1,0:T(4,128)S(1)}, u32[]{:S(2)}, u32[]{:S(2)}) collective-permute-start(f32[4,128]{1,0:T(4,128)S(1)} %get-tuple-element.36), channel_id=1, source_target_pairs={{0,2},{2,0},{4,6},{6,4},{8,10},{10,8},{12,14},{14,12},{16,18},{18,... | collective-permute-start | bytes 6152 | tf_op jit(solution)/shard_map/ppermute | solution.py:23
  37.0 5.5 %collective-permute-start.9 = (f32[4,128]{1,0:T(4,128)S(1)}, f32[4,128]{1,0:T(4,128)S(1)}, u32[]{:S(2)}, u32[]{:S(2)}) collective-permute-start(f32[4,128]{1,0:T(4,128)S(1)} %get-tuple-element.35), channel_id=1, source_target_pairs={{0,4},{2,6},{4,0},{6,2},{8,12},{10,14},{12,8},{14,10},{16,20},{18,... | collective-permute-start | bytes 6152 | tf_op jit(solution)/shard_map/ppermute | solution.py:23
  48.9 8.4 %collective-permute-start.12 = (f32[4,128]{1,0:T(4,128)S(1)}, f32[4,128]{1,0:T(4,128)S(1)}, u32[]{:S(2)}, u32[]{:S(2)}) collective-permute-start(f32[4,128]{1,0:T(4,128)S(1)} %get-tuple-element.32), channel_id=1, source_target_pairs={{0,1},{2,3},{4,5},{6,7},{8,9},{10,11},{12,13},{14,15},{16,17},{18,... | collective-permute-start | bytes 6152 | tf_op jit(solution)/shard_map/ppermute | solution.py:16
  51.4 11.2 %collective-permute-start.13 = (f32[4,128]{1,0:T(4,128)S(1)}, f32[4,128]{1,0:T(4,128)S(1)}, u32[]{:S(2)}, u32[]{:S(2)}) collective-permute-start(f32[4,128]{1,0:T(4,128)S(1)} %get-tuple-element.31), channel_id=1, source_target_pairs={{1,0},{3,2},{5,4},{7,6},{9,8},{11,10},{13,12},{15,14},{17,16},{19,... | collective-permute-start | bytes 6152 | tf_op jit(solution)/shard_map/ppermute | solution.py:17
  52.7 9.9 %collective-permute-start.14 = (f32[4,128]{1,0:T(4,128)S(1)}, f32[4,128]{1,0:T(4,128)S(1)}, u32[]{:S(2)}, u32[]{:S(2)}) collective-permute-start(f32[4,128]{1,0:T(4,128)S(1)} %get-tuple-element.30), channel_id=1, source_target_pairs={{0,2},{2,0},{4,6},{6,4},{8,10},{10,8},{12,14},{14,12},{16,18},{18,... | collective-permute-start | bytes 6152 | tf_op jit(solution)/shard_map/ppermute | solution.py:23
  54.2 8.4 %collective-permute-start.15 = (f32[4,128]{1,0:T(4,128)S(1)}, f32[4,128]{1,0:T(4,128)S(1)}, u32[]{:S(2)}, u32[]{:S(2)}) collective-permute-start(f32[4,128]{1,0:T(4,128)S(1)} %get-tuple-element.29), channel_id=1, source_target_pairs={{0,4},{2,6},{4,0},{6,2},{8,12},{10,14},{12,8},{14,10},{16,20},{18,... | collective-permute-start | bytes 6152 | tf_op jit(solution)/shard_map/ppermute | solution.py:23
  55.7 6.9 %collective-permute-start.16 = (f32[4,128]{1,0:T(4,128)S(1)}, f32[4,128]{1,0:T(4,128)S(1)}, u32[]{:S(2)}, u32[]{:S(2)}) collective-permute-start(f32[4,128]{1,0:T(4,128)S(1)} %get-tuple-element.28), channel_id=1, source_target_pairs={{0,8},{2,10},{4,12},{6,14},{8,0},{10,2},{12,4},{14,6},{16,24},{18,... | collective-permute-start | bytes 6152 | tf_op jit(solution)/shard_map/ppermute | solution.py:23
  57.3 5.3 %collective-permute-start.17 = (f32[4,128]{1,0:T(4,128)S(1)}, f32[4,128]{1,0:T(4,128)S(1)}, u32[]{:S(2)}, u32[]{:S(2)}) collective-permute-start(f32[4,128]{1,0:T(4,128)S(1)} %get-tuple-element.27), channel_id=1, source_target_pairs={{0,16},{2,18},{4,20},{6,22},{8,24},{10,26},{12,28},{14,30},{16,0},... | collective-permute-start | bytes 6152 | tf_op jit(solution)/shard_map/ppermute | solution.py:23
  71.0 10.6 %collective-permute-start.19 = (f32[4,128]{1,0:T(4,128)S(1)}, f32[4,128]{1,0:T(4,128)S(1)}, u32[]{:S(2)}, u32[]{:S(2)}) collective-permute-start(f32[4,128]{1,0:T(4,128)S(1)} %get-tuple-element.25), channel_id=1, source_target_pairs={{1,0},{3,2},{5,4},{7,6},{9,8},{11,10},{13,12},{15,14},{17,16},{19,... | collective-permute-start | bytes 6152 | tf_op jit(solution)/shard_map/ppermute | solution.py:17
  72.5 9.1 %collective-permute-start.20 = (f32[4,128]{1,0:T(4,128)S(1)}, f32[4,128]{1,0:T(4,128)S(1)}, u32[]{:S(2)}, u32[]{:S(2)}) collective-permute-start(f32[4,128]{1,0:T(4,128)S(1)} %get-tuple-element.24), channel_id=1, source_target_pairs={{0,2},{2,0},{4,6},{6,4},{8,10},{10,8},{12,14},{14,12},{16,18},{18,... | collective-permute-start | bytes 6152 | tf_op jit(solution)/shard_map/ppermute | solution.py:23
  73.1 8.5 %collective-permute-start.21 = (f32[4,128]{1,0:T(4,128)S(1)}, f32[4,128]{1,0:T(4,128)S(1)}, u32[]{:S(2)}, u32[]{:S(2)}) collective-permute-start(f32[4,128]{1,0:T(4,128)S(1)} %get-tuple-element.23), channel_id=1, source_target_pairs={{0,4},{2,6},{4,0},{6,2},{8,12},{10,14},{12,8},{14,10},{16,20},{18,... | collective-permute-start | bytes 6152 | tf_op jit(solution)/shard_map/ppermute | solution.py:23
  73.6 8.0 %collective-permute-start.22 = (f32[4,128]{1,0:T(4,128)S(1)}, f32[4,128]{1,0:T(4,128)S(1)}, u32[]{:S(2)}, u32[]{:S(2)}) collective-permute-start(f32[4,128]{1,0:T(4,128)S(1)} %get-tuple-element.22), channel_id=1, source_target_pairs={{0,8},{2,10},{4,12},{6,14},{8,0},{10,2},{12,4},{14,6},{16,24},{18,... | collective-permute-start | bytes 6152 | tf_op jit(solution)/shard_map/ppermute | solution.py:23
  74.0 7.6 %collective-permute-start.23 = (f32[4,128]{1,0:T(4,128)S(1)}, f32[4,128]{1,0:T(4,128)S(1)}, u32[]{:S(2)}, u32[]{:S(2)}) collective-permute-start(f32[4,128]{1,0:T(4,128)S(1)} %get-tuple-element.21), channel_id=1, source_target_pairs={{0,16},{2,18},{4,20},{6,22},{8,24},{10,26},{12,28},{14,30},{16,0},... | collective-permute-start | bytes 6152 | tf_op jit(solution)/shard_map/ppermute | solution.py:23
  88.1 7.9 %collective-permute-start.24 = (f32[4,128]{1,0:T(4,128)S(1)}, f32[4,128]{1,0:T(4,128)S(1)}, u32[]{:S(2)}, u32[]{:S(2)}) collective-permute-start(f32[4,128]{1,0:T(4,128)S(1)} %get-tuple-element.20), channel_id=1, source_target_pairs={{0,1},{2,3},{4,5},{6,7},{8,9},{10,11},{12,13},{14,15},{16,17},{18,... | collective-permute-start | bytes 6152 | tf_op jit(solution)/shard_map/ppermute | solution.py:16
  90.0 11.2 %collective-permute-start.25 = (f32[4,128]{1,0:T(4,128)S(1)}, f32[4,128]{1,0:T(4,128)S(1)}, u32[]{:S(2)}, u32[]{:S(2)}) collective-permute-start(f32[4,128]{1,0:T(4,128)S(1)} %get-tuple-element.19), channel_id=1, source_target_pairs={{1,0},{3,2},{5,4},{7,6},{9,8},{11,10},{13,12},{15,14},{17,16},{19,... | collective-permute-start | bytes 6152 | tf_op jit(solution)/shard_map/ppermute | solution.py:17
  91.3 9.9 %collective-permute-start.26 = (f32[4,128]{1,0:T(4,128)S(1)}, f32[4,128]{1,0:T(4,128)S(1)}, u32[]{:S(2)}, u32[]{:S(2)}) collective-permute-start(f32[4,128]{1,0:T(4,128)S(1)} %get-tuple-element.18), channel_id=1, source_target_pairs={{0,2},{2,0},{4,6},{6,4},{8,10},{10,8},{12,14},{14,12},{16,18},{18,... | collective-permute-start | bytes 6152 | tf_op jit(solution)/shard_map/ppermute | solution.py:23
  92.9 8.4 %collective-permute-start.27 = (f32[4,128]{1,0:T(4,128)S(1)}, f32[4,128]{1,0:T(4,128)S(1)}, u32[]{:S(2)}, u32[]{:S(2)}) collective-permute-start(f32[4,128]{1,0:T(4,128)S(1)} %get-tuple-element.17), channel_id=1, source_target_pairs={{0,4},{2,6},{4,0},{6,2},{8,12},{10,14},{12,8},{14,10},{16,20},{18,... | collective-permute-start | bytes 6152 | tf_op jit(solution)/shard_map/ppermute | solution.py:23
  94.4 6.9 %collective-permute-start.28 = (f32[4,128]{1,0:T(4,128)S(1)}, f32[4,128]{1,0:T(4,128)S(1)}, u32[]{:S(2)}, u32[]{:S(2)}) collective-permute-start(f32[4,128]{1,0:T(4,128)S(1)} %get-tuple-element.16), channel_id=1, source_target_pairs={{0,8},{2,10},{4,12},{6,14},{8,0},{10,2},{12,4},{14,6},{16,24},{18,... | collective-permute-start | bytes 6152 | tf_op jit(solution)/shard_map/ppermute | solution.py:23
  109.6 10.4 %collective-permute-start.31 = (f32[4,128]{1,0:T(4,128)S(1)}, f32[4,128]{1,0:T(4,128)S(1)}, u32[]{:S(2)}, u32[]{:S(2)}) collective-permute-start(f32[4,128]{1,0:T(4,128)S(1)} %get-tuple-element.13), channel_id=1, source_target_pairs={{1,0},{3,2},{5,4},{7,6},{9,8},{11,10},{13,12},{15,14},{17,16},{19,... | collective-permute-start | bytes 6152 | tf_op jit(solution)/shard_map/ppermute | solution.py:17
  110.9 9.1 %collective-permute-start.32 = (f32[4,128]{1,0:T(4,128)S(1)}, f32[4,128]{1,0:T(4,128)S(1)}, u32[]{:S(2)}, u32[]{:S(2)}) collective-permute-start(f32[4,128]{1,0:T(4,128)S(1)} %get-tuple-element.12), channel_id=1, source_target_pairs={{0,2},{2,0},{4,6},{6,4},{8,10},{10,8},{12,14},{14,12},{16,18},{18,... | collective-permute-start | bytes 6152 | tf_op jit(solution)/shard_map/ppermute | solution.py:23
  111.5 8.5 %collective-permute-start.33 = (f32[4,128]{1,0:T(4,128)S(1)}, f32[4,128]{1,0:T(4,128)S(1)}, u32[]{:S(2)}, u32[]{:S(2)}) collective-permute-start(f32[4,128]{1,0:T(4,128)S(1)} %get-tuple-element.11), channel_id=1, source_target_pairs={{0,4},{2,6},{4,0},{6,2},{8,12},{10,14},{12,8},{14,10},{16,20},{18,... | collective-permute-start | bytes 6152 | tf_op jit(solution)/shard_map/ppermute | solution.py:23
  112.0 8.0 %collective-permute-start.34 = (f32[4,128]{1,0:T(4,128)S(1)}, f32[4,128]{1,0:T(4,128)S(1)}, u32[]{:S(2)}, u32[]{:S(2)}) collective-permute-start(f32[4,128]{1,0:T(4,128)S(1)} %get-tuple-element.10), channel_id=1, source_target_pairs={{0,8},{2,10},{4,12},{6,14},{8,0},{10,2},{12,4},{14,6},{16,24},{18,... | collective-permute-start | bytes 6152 | tf_op jit(solution)/shard_map/ppermute | solution.py:23
  112.4 7.6 %collective-permute-start.35 = (f32[4,128]{1,0:T(4,128)S(1)}, f32[4,128]{1,0:T(4,128)S(1)}, u32[]{:S(2)}, u32[]{:S(2)}) collective-permute-start(f32[4,128]{1,0:T(4,128)S(1)} %get-tuple-element.9), channel_id=1, source_target_pairs={{0,16},{2,18},{4,20},{6,22},{8,24},{10,26},{12,28},{14,30},{16,0},... | collective-permute-start | bytes 6152 | tf_op jit(solution)/shard_map/ppermute | solution.py:23
  (23 other events, 384.0 us)
where the time goes:
time: 393 us; the launch traced here: 390 us
  between operations  145 us (37%)
  blocking collectives  79.3 us (20%)
  local copies, waits for them, and re-layouts  59 us (15%)
  starting transfers between devices  50.4 us (13%)
  matrix products  37.1 us (9%)
  other arithmetic  17.2 us (4%)
    psum x1, blocking collectives, shards(): sketched = lax.psum(sketch_part, ('dom', 'col'))  40.4 us
    psum x1, blocking collectives, shards(): gram_matrix = lax.psum(local_gram, ('dom', 'col')) / total_rows  38.9 us
    ppermute x24, starting transfers between devices, from_partner(): lax.ppermute(value, axis, [(i, i ^ 1 << apart) for i in range(lax.axis_si...  30.6 us
    dot_general x6, matrix products, shards(): jnp.einsum('rij,rj->ri', wide_blocks, vector_in, precision=highest)  30.5 us
    gather x12, local copies, waits for them, and re-layouts, shards(): neighbour_blocks = extended[columns]  24 us
    another operation x24, local copies, waits for them, and re-layouts, upper_inverse(): return jnp.stack([jnp.stack(row_list) for row_list in inverse])  12.5 us
    ppermute x6, starting transfers between devices, with_halo(): before = lax.ppermute(last, axis, up)  11.9 us
    ppermute x6, starting transfers between devices, with_halo(): after = lax.ppermute(first, axis, down)  7.93 us
  transfers between devices with their start and end apart: 36, of which 1 were waited for; matrix products, arithmetic and copies ran while one was open for 8% of the time, Pallas kernels for 0%

commit v1 on v0

v1 whole, which is shorter than its diff:
```python
import functools

import jax
import jax.numpy as jnp
from jax import lax
from jax.experimental import pallas as pl
from jax.experimental.pallas import tpu as pltpu
from jax.sharding import PartitionSpec as P

f32, bf16, i32 = jnp.float32, jnp.bfloat16, jnp.int32
VMEM = pl.BlockSpec(memory_space=pltpu.VMEM)
SUB, LANE = 8, 128
HI_LANE, LO_LANE = 32, 64


def params():
    return pltpu.CompilerParams(vmem_limit_bytes=16 << 20)


def run(body, outs, args, name, cost=(0, 0), scratch=()):
    return pl.pallas_call(
        body,
        out_shape=[jax.ShapeDtypeStruct(shape, dtype) for shape, dtype in outs],
        in_specs=[VMEM] * len(args),
        out_specs=[VMEM] * len(outs),
        scratch_shapes=list(scratch),
        compiler_params=params(),
        cost_estimate=pl.CostEstimate(flops=cost[0], bytes_accessed=cost[1], transcendentals=0),
        name=name,
    )(*args)


def lanes(shape=(SUB, LANE)):
    return lax.broadcasted_iota(i32, shape, len(shape) - 1)


def subs(shape=(SUB, LANE)):
    return lax.broadcasted_iota(i32, shape, len(shape) - 2)


def two_parts(value):
    high = value.astype(bf16)
    return high, (value - high.astype(f32)).astype(bf16)


def three_parts(value):
    high = value.astype(bf16)
    rest = value - high.astype(f32)
    middle = rest.astype(bf16)
    return high, middle, (rest - middle.astype(f32)).astype(bf16)


def dot(left, right):
    return lax.dot_general(left, right, (((1,), (0,)), ((), ())), preferred_element_type=f32)


def dot_nt(left, right):
    return lax.dot_general(left, right, (((1,), (1,)), ((), ())), preferred_element_type=f32)


def two_sum(a, b):
    total = a + b
    part = total - a
    return total, (a - (total - part)) + (b - part)


def split(a):
    scaled = a * 4097.0
    high = scaled - (scaled - a)
    return high, a - high


def two_product(a, a_split, b, b_split):
    product = a * b
    (ah, al), (bh, bl) = a_split, b_split
    return product, ((ah * bh - product) + ah * bl + al * bh) + al * bl


def pair_add(a, b):
    total, error = two_sum(a[0], b[0])
    return total, error + (a[1] + b[1])


def take_rows(send_hot, value):
    high, middle, low = three_parts(value)
    return dot(send_hot, high) + dot(send_hot, middle) + dot(send_hot, low)


def write_pieces(picked, out_refs):
    start = 0
    for ref in out_refs:
        ref[...] = picked[start : start + ref.shape[0]]
        start += ref.shape[0]


def first_body(send_ref, start_ref, hot_ref, *rest):
    out_refs, row_ref = rest[:-1], rest[-1]
    sends = send_ref.shape[1]
    row_ref[...] = jnp.full((SUB, LANE), -1, i32)
    row_ref[0:1, 0:sends] = send_ref[...]
    wanted = jnp.broadcast_to(row_ref[0:1, :], (LANE, LANE))
    hot = jnp.where(wanted == subs((LANE, LANE)), 1.0, 0.0).astype(f32).T
    hot = hot[: hot_ref.shape[0], : hot_ref.shape[1]].astype(bf16)
    hot_ref[...] = hot
    write_pieces(take_rows(hot, start_ref[...]), out_refs)


def prepare_body(own_rows, face, swap, columns_ref, couplings_ref, shifts_ref, place_ref, hot_ref, wide_ref, shift_ref):
    neighbours = columns_ref.shape[1]
    columns = columns_ref[...]
    if swap:
        place = place_ref[0]
        lower = (columns >= own_rows) & (columns < own_rows + face)
        upper = (columns >= own_rows + face) & (columns < own_rows + 2 * face)
        columns = jnp.where(
            lower,
            jnp.where(place == 1, columns + face, -1),
            jnp.where(upper, jnp.where(place == 0, columns - face, -1), columns),
        )
    width = lanes((own_rows, LANE))
    couplings = couplings_ref[...].astype(f32)
    for k in range(neighbours):
        hot = jnp.where(columns[:, k : k + 1] == width, 1.0, 0.0).astype(bf16)
        hot_ref[k * own_rows : (k + 1) * own_rows, 0:LANE] = hot
        hot_ref[k * own_rows : (k + 1) * own_rows, LANE : 2 * LANE] = hot
        wide_ref[k] = couplings[:, k, :]
    for k in range(shift_ref.shape[0]):
        shift_ref[k] = jnp.broadcast_to(shifts_ref[0:1, k : k + 1], (SUB, LANE))


def matvec(blocks_ref, vector_ref, own_ref):
    groups = vector_ref.shape[0] // SUB

    def group(g, carry):
        base = pl.multiple_of(g * SUB, SUB)
        high, low = two_parts(vector_ref[pl.ds(base, SUB), :])
        left = jnp.concatenate([high.astype(f32), low.astype(f32)], axis=0).astype(bf16)
        sub = subs()
        total = jnp.zeros((SUB, LANE), f32)
        for b in range(0, SUB, 2):
            start = pl.multiple_of((g * SUB + b) * LANE, 2 * LANE)
            out = dot_nt(left, blocks_ref[pl.ds(start, 2 * LANE), :])
            both = out[:SUB] + out[SUB:]
            total = jnp.where(sub == b, both[:, :LANE], total)
            total = jnp.where(sub == b + 1, both[:, LANE:], total)
        own_ref[pl.ds(base, SUB), :] = total
        return carry

    lax.fori_loop(0, groups, group, 0)


def statistics(k, vectors, sketch_ref, packet_in, packet_ref, scratch_ref):
    rows = vectors[0].shape[0]
    groups = rows // SUB
    sketches = sketch_ref.shape[0]
    lane, sub = lanes(), subs()
    newest = [vectors[k][g * SUB : (g + 1) * SUB, :] for g in range(groups)]
    new_split = [split(x) for x in newest]

    def one(i, carry):
        row = sketch_ref[i].astype(f32)
        parts = [newest[g] * row[g * SUB : (g + 1) * SUB, :] for g in range(groups)]
        while len(parts) > 1:
            parts = [a + b for a, b in zip(parts[::2], parts[1::2])] + parts[len(parts) // 2 * 2 :]
        scratch_ref[pl.ds(pl.multiple_of(i * SUB, SUB), SUB), :] = parts[0]
        return carry

    lax.fori_loop(0, sketches, one, 0, unroll=4)
    partial = scratch_ref[...]
    ones = jnp.ones((SUB, LANE), bf16)
    high, middle, low = three_parts(partial)
    across = dot_nt(ones, high) + dot_nt(ones, middle) + dot_nt(ones, low)
    width = sketches * SUB
    pick = jnp.where(
        lax.broadcasted_iota(i32, (width, LANE), 0) // SUB == lax.broadcasted_iota(i32, (width, LANE), 1), 1.0, 0.0
    ).astype(bf16)
    high, middle, low = three_parts(across)
    sketch_row = dot(high, pick) + dot(middle, pick) + dot(low, pick)

    wide = (jnp.zeros((SUB, LANE), f32), jnp.zeros((SUB, LANE), f32))
    for l in range(k + 1):
        total = None
        for g in range(groups):
            other = vectors[l][g * SUB : (g + 1) * SUB, :] if l < k else newest[g]
            other_split = split(other) if l < k else new_split[g]
            product = two_product(newest[g], new_split[g], other, other_split)
            total = product if total is None else pair_add(total, product)
        for step in (4, 2, 1):
            total = pair_add(total, tuple(pltpu.roll(x, step, 0) for x in total))
        wide = tuple(jnp.where(sub == l, t, w) for t, w in zip(total, wide))
    for step in (64, 32, 16, 8, 4, 2, 1):
        wide = pair_add(wide, tuple(pltpu.roll(x, step, 1) for x in wide))
    wide = two_sum(*wide)

    packet = packet_in
    row_k = sub == k
    packet = jnp.where(row_k & (lane < sketches), sketch_row, packet)
    for part, first in zip(wide, (HI_LANE, LO_LANE)):
        column = lane == first + k
        packet = jnp.where(column & (sub <= k), part, packet)
        turned = jnp.where(lane == first + sub, part, 0.0)
        for step in (4, 2, 1):
            turned = turned + pltpu.roll(turned, step, 0)
        packet = jnp.where(row_k & (lane >= first) & (lane <= first + k), turned, packet)
    packet_ref[...] = packet


def middle_body(k, first, last, *refs):
    refs = list(refs)
    vectors = [refs.pop(0) for _ in range(k + 1)]
    sketch_ref = refs.pop(0)
    packet_in = jnp.zeros((SUB, LANE), f32) if first else refs.pop(0)[...]
    if not last:
        blocks_ref = refs.pop(0)
    packet_ref = refs.pop(0)
    own_ref = None if last else refs.pop(0)
    scratch_ref = refs.pop(0)
    if not last:
        matvec(blocks_ref, vectors[k], own_ref)
    statistics(k, vectors, sketch_ref, packet_in, packet_ref, scratch_ref)


def next_body(k, received, last, *refs):
    own_ref, vector_ref, hot_ref, wide_ref, shift_ref = refs[:5]
    refs = refs[5:]
    if not last:
        send_ref, refs = refs[0], refs[1:]
    halo_refs, refs = refs[:received], refs[received:]
    next_ref, refs = refs[0], refs[1:]
    out_refs, extended_ref = refs[:-1], refs[-1]
    rows = vector_ref.shape[0]
    extended_ref[0:rows, :] = vector_ref[...]
    start = rows
    for ref in halo_refs:
        extended_ref[start : start + ref.shape[0], :] = ref[...]
        start += ref.shape[0]
    if start < LANE:
        extended_ref[start:LANE, :] = jnp.zeros((LANE - start, LANE), f32)
    parts = jnp.concatenate(two_parts(extended_ref[...]), axis=0)
    gathered = dot(hot_ref[...], parts)
    shift = shift_ref[k]
    for g in range(rows // SUB):
        at = slice(g * SUB, (g + 1) * SUB)
        total = own_ref[at, :] - shift * vector_ref[at, :]
        for n in range(wide_ref.shape[0]):
            total = total + wide_ref[n, at, :] * gathered[n * rows + g * SUB : n * rows + (g + 1) * SUB]
        next_ref[at, :] = total
    if not last:
        write_pieces(take_rows(send_ref[...], next_ref[...]), out_refs)


def splat(value, row, column):
    return jnp.broadcast_to(value[row : row + 1, column : column + 1], (SUB, LANE))


def cholesky(entries, n):
    work = {(i, j): entries[i, j] for i in range(n) for j in range(i, n)}
    upper, reciprocal = {}, []
    for p in range(n):
        root = jnp.sqrt(work[p, p])
        inverse = 1.0 / root
        reciprocal.append(inverse)
        upper[p, p] = root
        for j in range(p + 1, n):
            upper[p, j] = work[p, j] * inverse
        for i in range(p + 1, n):
            for j in range(i, n):
                work[i, j] = work[i, j] - upper[p, i] * upper[p, j]
    return upper, reciprocal


def upper_inverse(upper, reciprocal, n):
    result = {}
    for j in range(n):
        result[j, j] = reciprocal[j]
        for i in range(j - 1, -1, -1):
            total = upper[i, j] * result[j, j]
            for m in range(i + 1, j):
                total = total + upper[i, m] * result[m, j]
            result[i, j] = -(total * reciprocal[i])
    return result


def upper_product(left, right, n):
    result = {}
    for i in range(n):
        for j in range(i, n):
            total = left[i, i] * right[i, j]
            for m in range(i + 1, j + 1):
                total = total + left[i, m] * right[m, j]
            result[i, j] = total
    return result


def laid_out(entries, n, by_row=True):
    lane, sub = lanes(), subs()
    rows = jnp.zeros((SUB, LANE), f32)
    for i in range(n):
        row = jnp.zeros((SUB, LANE), f32)
        for j in range(i, n):
            row = jnp.where(lane == j, entries[i, j], row)
        rows = jnp.where(sub == i, row, rows)
    return rows


def times_pair(pair, factor, factor_split):
    product, error = two_product(pair[0], split(pair[0]), factor, factor_split)
    return product, error + pair[1] * factor


def last_body(n, sketches, total_rows, packets_ref, *refs):
    vector_refs, (orthonormal_ref, factor_ref, sketch_factor_ref) = refs[:n], refs[n:]
    lane, sub = lanes(), subs()
    devices = packets_ref.shape[0] // SUB
    sums = [(packets_ref[i * SUB : (i + 1) * SUB, :], jnp.zeros((SUB, LANE), f32)) for i in range(devices)]
    while len(sums) > 1:
        sums = [pair_add(a, b) for a, b in zip(sums[::2], sums[1::2])] + sums[len(sums) // 2 * 2 :]
    total, error = sums[0]
    low_parts = pltpu.roll(total + error, LANE - (LO_LANE - HI_LANE), 1)
    gram = two_sum(total, error + low_parts)

    sketched = jnp.where(lane < sketches, total + error, 0.0)
    entries = {}
    for j in range(n):
        products = jnp.sum(sketched * jnp.broadcast_to(sketched[j : j + 1, :], (SUB, LANE)), axis=1, keepdims=True)
        column = jnp.broadcast_to(products, (SUB, LANE))
        for i in range(j + 1):
            entries[i, j] = jnp.broadcast_to(column[i : i + 1, :], (SUB, LANE))
    sketch_upper, sketch_reciprocal = cholesky(entries, n)
    mixing = upper_inverse(sketch_upper, sketch_reciprocal, n)

    half = None
    for k in range(n):
        row = jnp.zeros((SUB, LANE), f32)
        for j in range(k, n):
            row = jnp.where(lane == j, mixing[k, j], row)
        column = tuple(jnp.broadcast_to(x[:, HI_LANE + k : HI_LANE + k + 1], (SUB, LANE)) for x in gram)
        term = times_pair(column, row, split(row))
        half = term if half is None else pair_add(half, term)
    half = two_sum(*half)
    white = None
    for i in range(n):
        column = jnp.zeros((SUB, LANE), f32)
        for j in range(i, n):
            column = jnp.where(sub == j, mixing[i, j], column)
        row = tuple(jnp.broadcast_to(x[i : i + 1, :], (SUB, LANE)) for x in half)
        term = times_pair(row, column, split(column))
        white = term if white is None else pair_add(white, term)
    white = (white[0] + white[1]) / total_rows
    entries = {(i, j): splat(white, i, j) for i in range(n) for j in range(i, n)}
    gram_upper, gram_reciprocal = cholesky(entries, n)
    weights = upper_product(mixing, upper_inverse(gram_upper, gram_reciprocal, n), n)

    for g in range(vector_refs[0].shape[0] // SUB):
        at = slice(g * SUB, (g + 1) * SUB)
        basis = [ref[at, :] for ref in vector_refs]
        for j in range(n):
            value = basis[0] * weights[0, j]
            for i in range(1, j + 1):
                value = value + basis[i] * weights[i, j]
            orthonormal_ref[j, at, :] = value
    factor_ref[...] = laid_out(upper_product(gram_upper, sketch_upper, n), n)[:n, :n]
    sketch_factor_ref[...] = laid_out(sketch_upper, n)[:n, :n]


def shards(diag_blocks, couplings, columns, send_rows, shifts, start_vector, sketch):
    dom, col = lax.axis_size("dom"), lax.axis_size("col")
    levels = dom.bit_length() - 1
    rows, width = start_vector.shape
    neighbours = couplings.shape[1]
    sends = send_rows.shape[1]
    face = sends // (2 + levels)
    powers = shifts.shape[0]
    n = powers + 1
    sketches = sketch.shape[0]
    swap = col == 2
    blocks = diag_blocks.reshape(rows * width, width)
    pieces = [2 * face] if swap else [face, face]
    pieces = pieces + [face] * levels
    piece_outs = [((size, width), f32) for size in pieces]
    send_pad = -(-sends // 16) * 16

    def exchange(outgoing):
        outgoing = list(outgoing)
        if swap:
            side = [lax.ppermute(outgoing[0], "col", [(0, 1), (1, 0)])]
            outgoing = outgoing[1:]
        else:
            up = [(i, i + 1) for i in range(col - 1)]
            side = [
                lax.ppermute(outgoing[1], "col", up),
                lax.ppermute(outgoing[0], "col", [(j, i) for i, j in up]),
            ]
            outgoing = outgoing[2:]
        far = [
            lax.ppermute(piece, "dom", [(i, i ^ (1 << level)) for i in range(dom)])
            for level, piece in enumerate(outgoing)
        ]
        return side + far

    send_hot, *outgoing = run(
        first_body,
        [((send_pad, rows), bf16)] + piece_outs,
        (send_rows, start_vector),
        "first",
        scratch=[pltpu.VMEM((SUB, LANE), i32)],
    )
    place = jnp.full((1, neighbours), lax.axis_index("col"), i32).reshape(1, 1, neighbours)
    neighbour_hot, wide, shift = run(
        functools.partial(prepare_body, rows, face, swap),
        [
            ((neighbours * rows, 2 * LANE), bf16),
            ((neighbours, rows, width), f32),
            ((powers, SUB, LANE), f32),
        ],
        (columns, couplings, shifts.reshape(1, powers), place),
        "prepare",
        cost=(4_000_000, 1_000_000),
    )
    vectors = [start_vector]
    packet = None
    for k in range(n):
        last = k == powers
        received = None if last else exchange(outgoing)
        args = (*vectors, sketch, *(() if packet is None else (packet,)), *(() if last else (blocks,)))
        result = run(
            functools.partial(middle_body, k, packet is None, last),
            [((SUB, LANE), f32)] + ([] if last else [((rows, width), f32)]),
            args,
            f"middle_{k}",
            cost=(20_000_000, 4_000_000),
            scratch=[pltpu.VMEM((sketches * SUB, LANE), f32)],
        )
        packet = result[0]
        if last:
            break
        final = k + 1 == powers
        args = (result[1], vectors[-1], neighbour_hot, wide, shift, *(() if final else (send_hot,)), *received)
        vector, *outgoing = run(
            functools.partial(next_body, k, len(received), final),
            [((rows, width), f32)] + ([] if final else piece_outs),
            args,
            f"next_{k}",
            cost=(1_000_000, 1_000_000),
            scratch=[pltpu.VMEM((LANE, LANE), f32)],
        )
        vectors.append(vector)

    everyone = ("dom", "col")
    packets = lax.all_to_all(jnp.tile(packet, (dom * col, 1)), everyone, 0, 0, tiled=True)
    orthonormal, factor, sketch_factor = run(
        functools.partial(last_body, n, sketches, float(rows * width * dom * col)),
        [((n, rows, width), f32), ((n, n), f32), ((n, n), f32)],
        (packets, *vectors),
        "last",
        cost=(5_000_000, 1_000_000),
    )
    return orthonormal, factor, sketch_factor


def solution(mesh):
    both = ("dom", "col")
    in_specs = (
        P(both, None, None),
        P(both, None, None),
        P(both, None),
        P(both, None),
        P(),
        P(both, None),
        P(None, both, None),
    )
    out_specs = (P(None, both, None), P(), P())
    return jax.shard_map(shards, mesh=mesh, in_specs=in_specs, out_specs=out_specs, check_vma=False)
```

time: 393 us -> 75.1 us (0.19)
  between operations: 145 us -> 0.98 us
  blocking collectives: 79.3 us -> 12.8 us
  local copies, waits for them, and re-layouts: 59 us -> 7.69 us
  matrix products: 37.1 us -> 0 us
  Pallas kernels: 0 us -> 23.4 us
  starting transfers between devices: 50.4 us -> 28.4 us
  other arithmetic: 17.2 us -> 0 us
    psum x2 -> x0, blocking collectives: 79.3 us -> none  [the longest x1 40.4 us: shards(): sketched = lax.psum(sketch_part, ('dom', 'col'))]
    dot_general x12 -> x0, matrix products: 37.1 us -> none  [the longest x6 30.5 us: shards(): jnp.einsum('rij,rj->ri', wide_blocks, vector_in, precision=highest)]
    gather x18 -> x0, local copies, waits for them, and re-layouts: 28.3 us -> none  [the longest x12 24 us: shards(): neighbour_blocks = extended[columns]]
    pallas_call x0 -> x16, Pallas kernels: none -> 23.4 us  [run(): pl.pallas_call(body, out_shape=[jax.ShapeDtypeStruct(shape, dtype) for sh...]
    ppermute x36 -> x30, starting transfers between devices: 50.4 us -> 28.4 us  [the longest x24 27.9 us: exchange(): lax.ppermute(piece, 'dom', [(i, i ^ 1 << level) for i in range(dom)])]
    another operation x37 -> x1, local copies, waits for them, and re-layouts: 17.1 us -> 0.01 us  [shards(): jnp.tile(packet, (dom * col, 1))]
    all_to_all x0 -> x1, blocking collectives: none -> 12.8 us  [shards(): lax.all_to_all(jnp.tile(packet, (dom * col, 1)), everyone, 0, 0, tiled=True)]
    slice x24 -> x0, local copies, waits for them, and re-layouts: 12.1 us -> none  [the longest x11 7.31 us: upper_inverse(): entry = entry + triangle[row_index, inner] * inverse[inner][target]]
  transfers between devices with their start and end apart: 36 -> 30, of which waited for: 1 -> 2; matrix products, arithmetic and copies ran while one was open for 8% -> 2% of each run, Pallas kernels for 0% -> 25%
where the time goes in v1:
time: 75.1 us; the launch traced here: 74.7 us
  starting transfers between devices  28.4 us (38%)
  Pallas kernels  23.4 us (31%)
  blocking collectives  12.8 us (17%)
  local copies, waits for them, and re-layouts  7.69 us (10%)
  waiting for transfers between devices  1.52 us (2%)
  between operations  0.98 us (1%)
    ppermute x24, starting transfers between devices, exchange(): lax.ppermute(piece, 'dom', [(i, i ^ 1 << level) for i in range(dom)])  27.9 us
    pallas_call x16, Pallas kernels, run(): pl.pallas_call(body, out_shape=[jax.ShapeDtypeStruct(shape, dtype) for sh...  23.4 us
    all_to_all x1, blocking collectives, shards(): lax.all_to_all(jnp.tile(packet, (dom * col, 1)), everyone, 0, 0, tiled=True)  12.8 us
    unnamed x16, local copies, waits for them, and re-layouts  7.68 us
  transfers between devices with their start and end apart: 30, of which 2 were waited for; matrix products, arithmetic and copies ran while one was open for 2% of the time, Pallas kernels for 25%

profile of v1, /device:TPU:0, one launch (start us, length us, event | category | flops | bytes accessed | tf_op | source)
XLA Modules:
  0.0 74.7 jit_solution(16421509272022249327)
XLA Ops:
  0.6 0.8 %copy-done.3 = f32[96,128]{1,0:T(8,128)S(1)} copy-done((f32[96,128]{1,0:T(8,128)S(1)}, f32[96,128]{1,0:T(8,128)}, u32[]{:S(2)}) %copy-start.3) | copy-done | bytes 49176
  1.4 0.7 copy-done.5
  2.8 2.5 %collective-permute-start.1 = (f32[4,128]{1,0:T(4,128)S(1)}, f32[4,128]{1,0:T(4,128)S(1)}, u32[]{:S(2)}, u32[]{:S(2)}) collective-permute-start(f32[4,128]{1,0:T(4,128)S(1)} %get-tuple-element.60), channel_id=1, source_target_pairs={{0,2},{2,0},{4,6},{6,4},{8,10},{10,8},{12,14},{14,12},{16,18},{18,... | collective-permute-start | bytes 6152 | tf_op jit(solution)/shard_map/ppermute | solution.py:396
  5.3 1.5 %collective-permute-start.2 = (f32[4,128]{1,0:T(4,128)S(1)}, f32[4,128]{1,0:T(4,128)S(1)}, u32[]{:S(2)}, u32[]{:S(2)}) collective-permute-start(f32[4,128]{1,0:T(4,128)S(1)} %get-tuple-element.61), channel_id=1, source_target_pairs={{0,4},{2,6},{4,0},{6,2},{8,12},{10,14},{12,8},{14,10},{16,20},{18,... | collective-permute-start | bytes 6152 | tf_op jit(solution)/shard_map/ppermute | solution.py:396
  6.8 1.6 %collective-permute-start.3 = (f32[4,128]{1,0:T(4,128)S(1)}, f32[4,128]{1,0:T(4,128)S(1)}, u32[]{:S(2)}, u32[]{:S(2)}) collective-permute-start(f32[4,128]{1,0:T(4,128)S(1)} %get-tuple-element.62), channel_id=1, source_target_pairs={{0,8},{2,10},{4,12},{6,14},{8,0},{10,2},{12,4},{14,6},{16,24},{18,... | collective-permute-start | bytes 6152 | tf_op jit(solution)/shard_map/ppermute | solution.py:396
  8.4 2.6 %collective-permute-start.4 = (f32[4,128]{1,0:T(4,128)S(1)}, f32[4,128]{1,0:T(4,128)S(1)}, u32[]{:S(2)}, u32[]{:S(2)}) collective-permute-start(f32[4,128]{1,0:T(4,128)S(1)} %get-tuple-element.63), channel_id=1, source_target_pairs={{0,16},{2,18},{4,20},{6,22},{8,24},{10,26},{12,28},{14,30},{16,0},... | collective-permute-start | bytes 6152 | tf_op jit(solution)/shard_map/ppermute | solution.py:396
  11.0 0.8 %copy.10.columns_ref = s32[96,6]{1,0:T(8,128)S(1)} copy(s32[96,6]{0,1:T(8,128)} %param.9) | data formatting | bytes 4608 | tf_op args[2]
  11.8 1.0 %copy.11.couplings_ref = bf16[96,6,128]{2,1,0:T(8,128)(2,1)S(1)} copy(bf16[96,6,128]{2,0,1:T(8,128)(2,1)} %param.8) | data formatting | bytes 294912 | tf_op args[1]
  12.8 0.6 copy-done.6
  13.7 1.9 %copy-done = bf16[96,128,128]{2,1,0:T(8,128)(2,1)S(1)} copy-done((bf16[96,128,128]{2,1,0:T(8,128)(2,1)S(1)}, bf16[96,128,128]{2,1,0:T(8,128)(2,1)}, u32[]{:S(2)}) %copy-start) | copy-done | bytes 3145752
  15.6 1.1 %copy-done.1 = bf16[32,96,128]{2,1,0:T(8,128)(2,1)S(1)} copy-done((bf16[32,96,128]{2,1,0:T(8,128)(2,1)S(1)}, bf16[32,96,128]{2,1,0:T(8,128)(2,1)}, u32[]{:S(2)}) %copy-start.1) | copy-done | bytes 786456
  16.7 0.8 %copy-done.4 = f32[96,128]{1,0:T(8,128)S(1)} copy-done((f32[96,128]{1,0:T(8,128)S(1)}, f32[96,128]{1,0:T(8,128)}, u32[]{:S(2)}) %copy-start.4) | copy-done | bytes 49176
  17.5 3.0 %middle_0.1 = (f32[8,128]{1,0:T(8,128)S(1)}, f32[96,128]{1,0:T(8,128)S(1)}) custom-call(f32[96,128]{1,0:T(8,128)S(1)} %copy-done.4, bf16[32,96,128]{2,1,0:T(8,128)(2,1)S(1)} %copy-done.1, bf16[12288,128]{1,0:T(8,128)(2,1)S(1)} %bitcast.3), custom_call_target="tpu_custom_call" | custom-call | flops 20000000 | bytes 4000000 | tf_op jit(solution)/shard_map/middle_0/pallas_call | solution.py:21
  22.5 3.0 %middle_1.1 = (f32[8,128]{1,0:T(8,128)S(1)}, f32[96,128]{1,0:T(8,128)S(1)}) custom-call(f32[96,128]{1,0:T(8,128)S(1)} %copy-done.4, f32[96,128]{1,0:T(8,128)S(1)} %get-tuple-element.64.refs_1_, bf16[32,96,128]{2,1,0:T(8,128)(2,1)S(1)} %copy-done.2, f32[8,128]{1,0:T(8,128)S(1)} %get-tuple-element.65.refs_3_, bf16[12288,128]{1,0:T(8,128)(2,1)S(1)} %bitcast.4), custom_call_target="tpu_custom_call" | custom-call | flops 20000000 | bytes 4000000 | tf_op jit(solution)/shard_map/middle_1/pallas_call | solution.py:21
  25.6 1.3 %collective-permute-done.9.refs_10_ = f32[4,128]{1,0:T(4,128)S(1)} collective-permute-done((f32[4,128]{1,0:T(4,128)S(1)}, f32[4,128]{1,0:T(4,128)S(1)}, u32[]{:S(2)}, u32[]{:S(2)}) %collective-permute-start.9) | collective-permute-done | bytes 2080 | tf_op jit(solution)/shard_map/ppermute | solution.py:396
  27.3 1.5 %collective-permute-start.11 = (f32[4,128]{1,0:T(4,128)S(1)}, f32[4,128]{1,0:T(4,128)S(1)}, u32[]{:S(2)}, u32[]{:S(2)}) collective-permute-start(f32[4,128]{1,0:T(4,128)S(1)} %get-tuple-element.76), channel_id=1, source_target_pairs={{0,2},{2,0},{4,6},{6,4},{8,10},{10,8},{12,14},{14,12},{16,18},{18,... | collective-permute-start | bytes 6152 | tf_op jit(solution)/shard_map/ppermute | solution.py:396
  28.9 1.5 %collective-permute-start.12 = (f32[4,128]{1,0:T(4,128)S(1)}, f32[4,128]{1,0:T(4,128)S(1)}, u32[]{:S(2)}, u32[]{:S(2)}) collective-permute-start(f32[4,128]{1,0:T(4,128)S(1)} %get-tuple-element.77), channel_id=1, source_target_pairs={{0,4},{2,6},{4,0},{6,2},{8,12},{10,14},{12,8},{14,10},{16,20},{18,... | collective-permute-start | bytes 6152 | tf_op jit(solution)/shard_map/ppermute | solution.py:396
  30.4 1.6 %collective-permute-start.13 = (f32[4,128]{1,0:T(4,128)S(1)}, f32[4,128]{1,0:T(4,128)S(1)}, u32[]{:S(2)}, u32[]{:S(2)}) collective-permute-start(f32[4,128]{1,0:T(4,128)S(1)} %get-tuple-element.78), channel_id=1, source_target_pairs={{0,8},{2,10},{4,12},{6,14},{8,0},{10,2},{12,4},{14,6},{16,24},{18,... | collective-permute-start | bytes 6152 | tf_op jit(solution)/shard_map/ppermute | solution.py:396
  32.0 1.5 %collective-permute-start.14 = (f32[4,128]{1,0:T(4,128)S(1)}, f32[4,128]{1,0:T(4,128)S(1)}, u32[]{:S(2)}, u32[]{:S(2)}) collective-permute-start(f32[4,128]{1,0:T(4,128)S(1)} %get-tuple-element.79), channel_id=1, source_target_pairs={{0,16},{2,18},{4,20},{6,22},{8,24},{10,26},{12,28},{14,30},{16,0},... | collective-permute-start | bytes 6152 | tf_op jit(solution)/shard_map/ppermute | solution.py:396
  33.5 3.0 %middle_2.1 = (f32[8,128]{1,0:T(8,128)S(1)}, f32[96,128]{1,0:T(8,128)S(1)}) custom-call(f32[96,128]{1,0:T(8,128)S(1)} %copy-done.4, f32[96,128]{1,0:T(8,128)S(1)} %get-tuple-element.64.refs_1_, f32[96,128]{1,0:T(8,128)S(1)} %get-tuple-element.72.refs_2_.refs_1_, bf16[32,96,128]{2,1,0:T(8,128)(2,1)S(1)} %copy-done.2, f32[8,128]{1,0:T(8,128)S(1)} %get-tuple-element.73.refs_4_, ...), custom_call_target="tpu_custom_call" | custom-call | flops 20000000 | bytes 4000000 | tf_op jit(solution)/shard_map/middle_2/pallas_call | solution.py:21
  38.5 1.4 %collective-permute-start.19 = (f32[4,128]{1,0:T(4,128)S(1)}, f32[4,128]{1,0:T(4,128)S(1)}, u32[]{:S(2)}, u32[]{:S(2)}) collective-permute-start(f32[4,128]{1,0:T(4,128)S(1)} %get-tuple-element.87), channel_id=1, source_target_pairs={{0,16},{2,18},{4,20},{6,22},{8,24},{10,26},{12,28},{14,30},{16,0},... | collective-permute-start | bytes 6152 | tf_op jit(solution)/shard_map/ppermute | solution.py:396
  39.9 3.1 %middle_3.1 = (f32[8,128]{1,0:T(8,128)S(1)}, f32[96,128]{1,0:T(8,128)S(1)}) custom-call(f32[96,128]{1,0:T(8,128)S(1)} %copy-done.4, f32[96,128]{1,0:T(8,128)S(1)} %get-tuple-element.64.refs_1_, f32[96,128]{1,0:T(8,128)S(1)} %get-tuple-element.72.refs_2_.refs_1_, f32[96,128]{1,0:T(8,128)S(1)} %get-tuple-element.80.refs_3_.refs_1_, ...), custom_call_target="tpu_custom_call" | custom-call | flops 20000000 | bytes 4000000 | tf_op jit(solution)/shard_map/middle_3/pallas_call | solution.py:21
  43.5 1.6 %collective-permute-start.21 = (f32[4,128]{1,0:T(4,128)S(1)}, f32[4,128]{1,0:T(4,128)S(1)}, u32[]{:S(2)}, u32[]{:S(2)}) collective-permute-start(f32[4,128]{1,0:T(4,128)S(1)} %get-tuple-element.92), channel_id=1, source_target_pairs={{0,2},{2,0},{4,6},{6,4},{8,10},{10,8},{12,14},{14,12},{16,18},{18,... | collective-permute-start | bytes 6152 | tf_op jit(solution)/shard_map/ppermute | solution.py:396
  45.0 1.5 %collective-permute-start.22 = (f32[4,128]{1,0:T(4,128)S(1)}, f32[4,128]{1,0:T(4,128)S(1)}, u32[]{:S(2)}, u32[]{:S(2)}) collective-permute-start(f32[4,128]{1,0:T(4,128)S(1)} %get-tuple-element.93), channel_id=1, source_target_pairs={{0,4},{2,6},{4,0},{6,2},{8,12},{10,14},{12,8},{14,10},{16,20},{18,... | collective-permute-start | bytes 6152 | tf_op jit(solution)/shard_map/ppermute | solution.py:396
  46.5 1.6 %collective-permute-start.23 = (f32[4,128]{1,0:T(4,128)S(1)}, f32[4,128]{1,0:T(4,128)S(1)}, u32[]{:S(2)}, u32[]{:S(2)}) collective-permute-start(f32[4,128]{1,0:T(4,128)S(1)} %get-tuple-element.94), channel_id=1, source_target_pairs={{0,8},{2,10},{4,12},{6,14},{8,0},{10,2},{12,4},{14,6},{16,24},{18,... | collective-permute-start | bytes 6152 | tf_op jit(solution)/shard_map/ppermute | solution.py:396
  48.1 1.5 %collective-permute-start.24 = (f32[4,128]{1,0:T(4,128)S(1)}, f32[4,128]{1,0:T(4,128)S(1)}, u32[]{:S(2)}, u32[]{:S(2)}) collective-permute-start(f32[4,128]{1,0:T(4,128)S(1)} %get-tuple-element.95), channel_id=1, source_target_pairs={{0,16},{2,18},{4,20},{6,22},{8,24},{10,26},{12,28},{14,30},{16,0},... | collective-permute-start | bytes 6152 | tf_op jit(solution)/shard_map/ppermute | solution.py:396
  49.6 3.1 %middle_4.1 = (f32[8,128]{1,0:T(8,128)S(1)}, f32[96,128]{1,0:T(8,128)S(1)}) custom-call(f32[96,128]{1,0:T(8,128)S(1)} %copy-done.4, f32[96,128]{1,0:T(8,128)S(1)} %get-tuple-element.64.refs_1_, f32[96,128]{1,0:T(8,128)S(1)} %get-tuple-element.72.refs_2_.refs_1_, f32[96,128]{1,0:T(8,128)S(1)} %get-tuple-element.80.refs_3_.refs_1_, ...), custom_call_target="tpu_custom_call" | custom-call | flops 20000000 | bytes 4000000 | tf_op jit(solution)/shard_map/middle_4/pallas_call | solution.py:21
  54.7 1.4 %collective-permute-start.29 = (f32[4,128]{1,0:T(4,128)S(1)}, f32[4,128]{1,0:T(4,128)S(1)}, u32[]{:S(2)}, u32[]{:S(2)}) collective-permute-start(f32[4,128]{1,0:T(4,128)S(1)} %get-tuple-element.103), channel_id=1, source_target_pairs={{0,16},{2,18},{4,20},{6,22},{8,24},{10,26},{12,28},{14,30},{16,0},... | collective-permute-start | bytes 6152 | tf_op jit(solution)/shard_map/ppermute | solution.py:396
  56.1 3.2 %middle_5.1 = (f32[8,128]{1,0:T(8,128)S(1)}, f32[96,128]{1,0:T(8,128)S(1)}) custom-call(f32[96,128]{1,0:T(8,128)S(1)} %copy-done.4, f32[96,128]{1,0:T(8,128)S(1)} %get-tuple-element.64.refs_1_, f32[96,128]{1,0:T(8,128)S(1)} %get-tuple-element.72.refs_2_.refs_1_, f32[96,128]{1,0:T(8,128)S(1)} %get-tuple-element.80.refs_3_.refs_1_, ...), custom_call_target="tpu_custom_call" | custom-call | flops 20000000 | bytes 4000000 | tf_op jit(solution)/shard_map/middle_5/pallas_call | solution.py:21
  59.6 1.0 %middle_6.1 = f32[8,128]{1,0:T(8,128)S(1)} custom-call(f32[96,128]{1,0:T(8,128)S(1)} %copy-done.4, f32[96,128]{1,0:T(8,128)S(1)} %get-tuple-element.64.refs_1_, f32[96,128]{1,0:T(8,128)S(1)} %get-tuple-element.72.refs_2_.refs_1_, f32[96,128]{1,0:T(8,128)S(1)} %get-tuple-element.80.refs_3_.refs_1_, f32[96,128]{1,0:T(8,128)S(1)} %get-tuple-element.88.refs_4_.refs_1_, ...), custom_call_target="tpu_custom_call" | custom-call | flops 20000000 | bytes 4000000 | tf_op jit(solution)/shard_map/middle_6/pallas_call | solution.py:21
  60.6 12.8 %all_to_all.8 = f32[32,8,128]{2,1,0:T(8,128)S(1)} all-to-all(f32[32,8,128]{2,1,0:T(8,128)S(1)} %tile.2), channel_id=1, replica_groups=mesh['dom'=16,'col'=2] {'dom','col'}, dimensions={0} | all-to-all | bytes 262144 | tf_op jit(solution)/shard_map/all_to_all | solution.py:450
  73.4 1.4 %last.1 = (f32[7,96,128]{2,1,0:T(8,128)}, f32[7,7]{1,0:T(8,128)}, f32[7,7]{1,0:T(8,128)}) custom-call(f32[256,128]{1,0:T(8,128)S(1)} %bitcast.9, f32[96,128]{1,0:T(8,128)S(1)} %copy-done.4, f32[96,128]{1,0:T(8,128)S(1)} %get-tuple-element.64.refs_1_, f32[96,128]{1,0:T(8,128)S(1)} %get-tuple-element.72.refs_2_.refs_1_, ...), custom_call_target="tpu_custom_call" | custom-call | flops 5000000 | bytes 1000000 | tf_op jit(solution)/shard_map/last/pallas_call | solution.py:21
  (63 shorter events, 8.0 us)
Async XLA Ops:
  2.3 18.2 %collective-permute-start = (f32[8,128]{1,0:T(8,128)S(1)}, f32[8,128]{1,0:T(8,128)S(1)}, u32[]{:S(2)}, u32[]{:S(2)}) collective-permute-start(f32[8,128]{1,0:T(8,128)S(1)} %get-tuple-element.59), channel_id=1, source_target_pairs={{0,1},{1,0},{2,3},{3,2},{4,5},{5,4},{6,7},{7,6},{8,9},{9,8},{10,11... | collective-permute-start | bytes 12296 | tf_op jit(solution)/shard_map/ppermute | solution.py:386
  2.8 17.7 %collective-permute-start.1 = (f32[4,128]{1,0:T(4,128)S(1)}, f32[4,128]{1,0:T(4,128)S(1)}, u32[]{:S(2)}, u32[]{:S(2)}) collective-permute-start(f32[4,128]{1,0:T(4,128)S(1)} %get-tuple-element.60), channel_id=1, source_target_pairs={{0,2},{2,0},{4,6},{6,4},{8,10},{10,8},{12,14},{14,12},{16,18},{18,... | collective-permute-start | bytes 6152 | tf_op jit(solution)/shard_map/ppermute | solution.py:396
  5.3 15.2 %collective-permute-start.2 = (f32[4,128]{1,0:T(4,128)S(1)}, f32[4,128]{1,0:T(4,128)S(1)}, u32[]{:S(2)}, u32[]{:S(2)}) collective-permute-start(f32[4,128]{1,0:T(4,128)S(1)} %get-tuple-element.61), channel_id=1, source_target_pairs={{0,4},{2,6},{4,0},{6,2},{8,12},{10,14},{12,8},{14,10},{16,20},{18,... | collective-permute-start | bytes 6152 | tf_op jit(solution)/shard_map/ppermute | solution.py:396
  6.8 13.7 %collective-permute-start.3 = (f32[4,128]{1,0:T(4,128)S(1)}, f32[4,128]{1,0:T(4,128)S(1)}, u32[]{:S(2)}, u32[]{:S(2)}) collective-permute-start(f32[4,128]{1,0:T(4,128)S(1)} %get-tuple-element.62), channel_id=1, source_target_pairs={{0,8},{2,10},{4,12},{6,14},{8,0},{10,2},{12,4},{14,6},{16,24},{18,... | collective-permute-start | bytes 6152 | tf_op jit(solution)/shard_map/ppermute | solution.py:396
  8.4 12.1 %collective-permute-start.4 = (f32[4,128]{1,0:T(4,128)S(1)}, f32[4,128]{1,0:T(4,128)S(1)}, u32[]{:S(2)}, u32[]{:S(2)}) collective-permute-start(f32[4,128]{1,0:T(4,128)S(1)} %get-tuple-element.63), channel_id=1, source_target_pairs={{0,16},{2,18},{4,20},{6,22},{8,24},{10,26},{12,28},{14,30},{16,0},... | collective-permute-start | bytes 6152 | tf_op jit(solution)/shard_map/ppermute | solution.py:396
  13.7 1.9 %copy-start = (bf16[96,128,128]{2,1,0:T(8,128)(2,1)S(1)}, bf16[96,128,128]{2,1,0:T(8,128)(2,1)}, u32[]{:S(2)}) copy-start(bf16[96,128,128]{2,1,0:T(8,128)(2,1)} %param.7) | copy-start | bytes 9437188
  17.5 5.0 %copy-start.2 = (bf16[32,96,128]{2,1,0:T(8,128)(2,1)S(1)}, bf16[32,96,128]{2,1,0:T(8,128)(2,1)}, u32[]{:S(2)}) copy-start(bf16[32,96,128]{2,1,0:T(8,128)(2,1)} %refs_7_.1) | copy-start | bytes 2359300
  20.9 6.0 %collective-permute-start.5 = (f32[8,128]{1,0:T(8,128)S(1)}, f32[8,128]{1,0:T(8,128)S(1)}, u32[]{:S(2)}, u32[]{:S(2)}) collective-permute-start(f32[8,128]{1,0:T(8,128)S(1)} %get-tuple-element.67), channel_id=1, source_target_pairs={{0,1},{1,0},{2,3},{3,2},{4,5},{5,4},{6,7},{7,6},{8,9},{9,8},{10,11... | collective-permute-start | bytes 12296 | tf_op jit(solution)/shard_map/ppermute | solution.py:386
  20.9 4.5 %collective-permute-start.6 = (f32[4,128]{1,0:T(4,128)S(1)}, f32[4,128]{1,0:T(4,128)S(1)}, u32[]{:S(2)}, u32[]{:S(2)}) collective-permute-start(f32[4,128]{1,0:T(4,128)S(1)} %get-tuple-element.68), channel_id=1, source_target_pairs={{0,2},{2,0},{4,6},{6,4},{8,10},{10,8},{12,14},{14,12},{16,18},{18,... | collective-permute-start | bytes 6152 | tf_op jit(solution)/shard_map/ppermute | solution.py:396
  21.5 4.0 %collective-permute-start.7 = (f32[4,128]{1,0:T(4,128)S(1)}, f32[4,128]{1,0:T(4,128)S(1)}, u32[]{:S(2)}, u32[]{:S(2)}) collective-permute-start(f32[4,128]{1,0:T(4,128)S(1)} %get-tuple-element.69), channel_id=1, source_target_pairs={{0,4},{2,6},{4,0},{6,2},{8,12},{10,14},{12,8},{14,10},{16,20},{18,... | collective-permute-start | bytes 6152 | tf_op jit(solution)/shard_map/ppermute | solution.py:396
  22.0 3.6 %collective-permute-start.8 = (f32[4,128]{1,0:T(4,128)S(1)}, f32[4,128]{1,0:T(4,128)S(1)}, u32[]{:S(2)}, u32[]{:S(2)}) collective-permute-start(f32[4,128]{1,0:T(4,128)S(1)} %get-tuple-element.70), channel_id=1, source_target_pairs={{0,8},{2,10},{4,12},{6,14},{8,0},{10,2},{12,4},{14,6},{16,24},{18,... | collective-permute-start | bytes 6152 | tf_op jit(solution)/shard_map/ppermute | solution.py:396
  22.4 4.5 %collective-permute-start.9 = (f32[4,128]{1,0:T(4,128)S(1)}, f32[4,128]{1,0:T(4,128)S(1)}, u32[]{:S(2)}, u32[]{:S(2)}) collective-permute-start(f32[4,128]{1,0:T(4,128)S(1)} %get-tuple-element.71), channel_id=1, source_target_pairs={{0,16},{2,18},{4,20},{6,22},{8,24},{10,26},{12,28},{14,30},{16,0},... | collective-permute-start | bytes 6152 | tf_op jit(solution)/shard_map/ppermute | solution.py:396
  27.3 9.2 %collective-permute-start.10 = (f32[8,128]{1,0:T(8,128)S(1)}, f32[8,128]{1,0:T(8,128)S(1)}, u32[]{:S(2)}, u32[]{:S(2)}) collective-permute-start(f32[8,128]{1,0:T(8,128)S(1)} %get-tuple-element.75), channel_id=1, source_target_pairs={{0,1},{1,0},{2,3},{3,2},{4,5},{5,4},{6,7},{7,6},{8,9},{9,8},{10,11... | collective-permute-start | bytes 12296 | tf_op jit(solution)/shard_map/ppermute | solution.py:386
  27.3 9.2 %collective-permute-start.11 = (f32[4,128]{1,0:T(4,128)S(1)}, f32[4,128]{1,0:T(4,128)S(1)}, u32[]{:S(2)}, u32[]{:S(2)}) collective-permute-start(f32[4,128]{1,0:T(4,128)S(1)} %get-tuple-element.76), channel_id=1, source_target_pairs={{0,2},{2,0},{4,6},{6,4},{8,10},{10,8},{12,14},{14,12},{16,18},{18,... | collective-permute-start | bytes 6152 | tf_op jit(solution)/shard_map/ppermute | solution.py:396
  28.9 7.7 %collective-permute-start.12 = (f32[4,128]{1,0:T(4,128)S(1)}, f32[4,128]{1,0:T(4,128)S(1)}, u32[]{:S(2)}, u32[]{:S(2)}) collective-permute-start(f32[4,128]{1,0:T(4,128)S(1)} %get-tuple-element.77), channel_id=1, source_target_pairs={{0,4},{2,6},{4,0},{6,2},{8,12},{10,14},{12,8},{14,10},{16,20},{18,... | collective-permute-start | bytes 6152 | tf_op jit(solution)/shard_map/ppermute | solution.py:396
  30.4 6.1 %collective-permute-start.13 = (f32[4,128]{1,0:T(4,128)S(1)}, f32[4,128]{1,0:T(4,128)S(1)}, u32[]{:S(2)}, u32[]{:S(2)}) collective-permute-start(f32[4,128]{1,0:T(4,128)S(1)} %get-tuple-element.78), channel_id=1, source_target_pairs={{0,8},{2,10},{4,12},{6,14},{8,0},{10,2},{12,4},{14,6},{16,24},{18,... | collective-permute-start | bytes 6152 | tf_op jit(solution)/shard_map/ppermute | solution.py:396
  32.0 4.6 %collective-permute-start.14 = (f32[4,128]{1,0:T(4,128)S(1)}, f32[4,128]{1,0:T(4,128)S(1)}, u32[]{:S(2)}, u32[]{:S(2)}) collective-permute-start(f32[4,128]{1,0:T(4,128)S(1)} %get-tuple-element.79), channel_id=1, source_target_pairs={{0,16},{2,18},{4,20},{6,22},{8,24},{10,26},{12,28},{14,30},{16,0},... | collective-permute-start | bytes 6152 | tf_op jit(solution)/shard_map/ppermute | solution.py:396
  37.0 6.1 %collective-permute-start.15 = (f32[8,128]{1,0:T(8,128)S(1)}, f32[8,128]{1,0:T(8,128)S(1)}, u32[]{:S(2)}, u32[]{:S(2)}) collective-permute-start(f32[8,128]{1,0:T(8,128)S(1)} %get-tuple-element.83), channel_id=1, source_target_pairs={{0,1},{1,0},{2,3},{3,2},{4,5},{5,4},{6,7},{7,6},{8,9},{9,8},{10,11... | collective-permute-start | bytes 12296 | tf_op jit(solution)/shard_map/ppermute | solution.py:386
  37.0 6.0 %collective-permute-start.16 = (f32[4,128]{1,0:T(4,128)S(1)}, f32[4,128]{1,0:T(4,128)S(1)}, u32[]{:S(2)}, u32[]{:S(2)}) collective-permute-start(f32[4,128]{1,0:T(4,128)S(1)} %get-tuple-element.84), channel_id=1, source_target_pairs={{0,2},{2,0},{4,6},{6,4},{8,10},{10,8},{12,14},{14,12},{16,18},{18,... | collective-permute-start | bytes 6152 | tf_op jit(solution)/shard_map/ppermute | solution.py:396
  37.6 5.5 %collective-permute-start.17 = (f32[4,128]{1,0:T(4,128)S(1)}, f32[4,128]{1,0:T(4,128)S(1)}, u32[]{:S(2)}, u32[]{:S(2)}) collective-permute-start(f32[4,128]{1,0:T(4,128)S(1)} %get-tuple-element.85), channel_id=1, source_target_pairs={{0,4},{2,6},{4,0},{6,2},{8,12},{10,14},{12,8},{14,10},{16,20},{18,... | collective-permute-start | bytes 6152 | tf_op jit(solution)/shard_map/ppermute | solution.py:396
  38.1 5.0 %collective-permute-start.18 = (f32[4,128]{1,0:T(4,128)S(1)}, f32[4,128]{1,0:T(4,128)S(1)}, u32[]{:S(2)}, u32[]{:S(2)}) collective-permute-start(f32[4,128]{1,0:T(4,128)S(1)} %get-tuple-element.86), channel_id=1, source_target_pairs={{0,8},{2,10},{4,12},{6,14},{8,0},{10,2},{12,4},{14,6},{16,24},{18,... | collective-permute-start | bytes 6152 | tf_op jit(solution)/shard_map/ppermute | solution.py:396
  38.5 4.5 %collective-permute-start.19 = (f32[4,128]{1,0:T(4,128)S(1)}, f32[4,128]{1,0:T(4,128)S(1)}, u32[]{:S(2)}, u32[]{:S(2)}) collective-permute-start(f32[4,128]{1,0:T(4,128)S(1)} %get-tuple-element.87), channel_id=1, source_target_pairs={{0,16},{2,18},{4,20},{6,22},{8,24},{10,26},{12,28},{14,30},{16,0},... | collective-permute-start | bytes 6152 | tf_op jit(solution)/shard_map/ppermute | solution.py:396
  43.5 9.3 %collective-permute-start.20 = (f32[8,128]{1,0:T(8,128)S(1)}, f32[8,128]{1,0:T(8,128)S(1)}, u32[]{:S(2)}, u32[]{:S(2)}) collective-permute-start(f32[8,128]{1,0:T(8,128)S(1)} %get-tuple-element.91), channel_id=1, source_target_pairs={{0,1},{1,0},{2,3},{3,2},{4,5},{5,4},{6,7},{7,6},{8,9},{9,8},{10,11... | collective-permute-start | bytes 12296 | tf_op jit(solution)/shard_map/ppermute | solution.py:386
  43.5 9.3 %collective-permute-start.21 = (f32[4,128]{1,0:T(4,128)S(1)}, f32[4,128]{1,0:T(4,128)S(1)}, u32[]{:S(2)}, u32[]{:S(2)}) collective-permute-start(f32[4,128]{1,0:T(4,128)S(1)} %get-tuple-element.92), channel_id=1, source_target_pairs={{0,2},{2,0},{4,6},{6,4},{8,10},{10,8},{12,14},{14,12},{16,18},{18,... | collective-permute-start | bytes 6152 | tf_op jit(solution)/shard_map/ppermute | solution.py:396
  45.0 7.7 %collective-permute-start.22 = (f32[4,128]{1,0:T(4,128)S(1)}, f32[4,128]{1,0:T(4,128)S(1)}, u32[]{:S(2)}, u32[]{:S(2)}) collective-permute-start(f32[4,128]{1,0:T(4,128)S(1)} %get-tuple-element.93), channel_id=1, source_target_pairs={{0,4},{2,6},{4,0},{6,2},{8,12},{10,14},{12,8},{14,10},{16,20},{18,... | collective-permute-start | bytes 6152 | tf_op jit(solution)/shard_map/ppermute | solution.py:396
  46.5 6.2 %collective-permute-start.23 = (f32[4,128]{1,0:T(4,128)S(1)}, f32[4,128]{1,0:T(4,128)S(1)}, u32[]{:S(2)}, u32[]{:S(2)}) collective-permute-start(f32[4,128]{1,0:T(4,128)S(1)} %get-tuple-element.94), channel_id=1, source_target_pairs={{0,8},{2,10},{4,12},{6,14},{8,0},{10,2},{12,4},{14,6},{16,24},{18,... | collective-permute-start | bytes 6152 | tf_op jit(solution)/shard_map/ppermute | solution.py:396
  48.1 4.7 %collective-permute-start.24 = (f32[4,128]{1,0:T(4,128)S(1)}, f32[4,128]{1,0:T(4,128)S(1)}, u32[]{:S(2)}, u32[]{:S(2)}) collective-permute-start(f32[4,128]{1,0:T(4,128)S(1)} %get-tuple-element.95), channel_id=1, source_target_pairs={{0,16},{2,18},{4,20},{6,22},{8,24},{10,26},{12,28},{14,30},{16,0},... | collective-permute-start | bytes 6152 | tf_op jit(solution)/shard_map/ppermute | solution.py:396
  53.2 6.1 %collective-permute-start.25 = (f32[8,128]{1,0:T(8,128)S(1)}, f32[8,128]{1,0:T(8,128)S(1)}, u32[]{:S(2)}, u32[]{:S(2)}) collective-permute-start(f32[8,128]{1,0:T(8,128)S(1)} %get-tuple-element.99), channel_id=1, source_target_pairs={{0,1},{1,0},{2,3},{3,2},{4,5},{5,4},{6,7},{7,6},{8,9},{9,8},{10,11... | collective-permute-start | bytes 12296 | tf_op jit(solution)/shard_map/ppermute | solution.py:386
  53.2 6.1 %collective-permute-start.26 = (f32[4,128]{1,0:T(4,128)S(1)}, f32[4,128]{1,0:T(4,128)S(1)}, u32[]{:S(2)}, u32[]{:S(2)}) collective-permute-start(f32[4,128]{1,0:T(4,128)S(1)} %get-tuple-element.100), channel_id=1, source_target_pairs={{0,2},{2,0},{4,6},{6,4},{8,10},{10,8},{12,14},{14,12},{16,18},{18,... | collective-permute-start | bytes 6152 | tf_op jit(solution)/shard_map/ppermute | solution.py:396
  53.8 5.5 %collective-permute-start.27 = (f32[4,128]{1,0:T(4,128)S(1)}, f32[4,128]{1,0:T(4,128)S(1)}, u32[]{:S(2)}, u32[]{:S(2)}) collective-permute-start(f32[4,128]{1,0:T(4,128)S(1)} %get-tuple-element.101), channel_id=1, source_target_pairs={{0,4},{2,6},{4,0},{6,2},{8,12},{10,14},{12,8},{14,10},{16,20},{18,... | collective-permute-start | bytes 6152 | tf_op jit(solution)/shard_map/ppermute | solution.py:396
  54.3 5.0 %collective-permute-start.28 = (f32[4,128]{1,0:T(4,128)S(1)}, f32[4,128]{1,0:T(4,128)S(1)}, u32[]{:S(2)}, u32[]{:S(2)}) collective-permute-start(f32[4,128]{1,0:T(4,128)S(1)} %get-tuple-element.102), channel_id=1, source_target_pairs={{0,8},{2,10},{4,12},{6,14},{8,0},{10,2},{12,4},{14,6},{16,24},{18,... | collective-permute-start | bytes 6152 | tf_op jit(solution)/shard_map/ppermute | solution.py:396
  54.7 4.6 %collective-permute-start.29 = (f32[4,128]{1,0:T(4,128)S(1)}, f32[4,128]{1,0:T(4,128)S(1)}, u32[]{:S(2)}, u32[]{:S(2)}) collective-permute-start(f32[4,128]{1,0:T(4,128)S(1)} %get-tuple-element.103), channel_id=1, source_target_pairs={{0,16},{2,18},{4,20},{6,22},{8,24},{10,26},{12,28},{14,30},{16,0},... | collective-permute-start | bytes 6152 | tf_op jit(solution)/shard_map/ppermute | solution.py:396
  (5 other events, 4.0 us)

commit v2 on v1

--- a/solution.py
+++ b/solution.py
@@ -93,23 +93,27 @@
         start += ref.shape[0]
 
 
-def first_body(send_ref, start_ref, hot_ref, *rest):
+def one_hot(row, rows):
+    wanted = jnp.broadcast_to(row, (LANE, LANE))
+    return jnp.where(wanted == subs((LANE, LANE)), 1.0, 0.0).astype(f32).T[:rows]
+
+
+def first_body(sends_ref, vector_ref, hot_ref, *rest):
     out_refs, row_ref = rest[:-1], rest[-1]
-    sends = send_ref.shape[1]
     row_ref[...] = jnp.full((SUB, LANE), -1, i32)
-    row_ref[0:1, 0:sends] = send_ref[...]
-    wanted = jnp.broadcast_to(row_ref[0:1, :], (LANE, LANE))
-    hot = jnp.where(wanted == subs((LANE, LANE)), 1.0, 0.0).astype(f32).T
-    hot = hot[: hot_ref.shape[0], : hot_ref.shape[1]].astype(bf16)
+    row_ref[0:1, 0 : sends_ref.shape[1]] = sends_ref[...]
+    hot = one_hot(row_ref[0:1, :], hot_ref.shape[0])[:, : hot_ref.shape[1]].astype(bf16)
     hot_ref[...] = hot
-    write_pieces(take_rows(hot, start_ref[...]), out_refs)
-
-
-def prepare_body(own_rows, face, swap, columns_ref, couplings_ref, shifts_ref, place_ref, hot_ref, wide_ref, shift_ref):
-    neighbours = columns_ref.shape[1]
-    columns = columns_ref[...]
+    write_pieces(take_rows(hot, vector_ref[...]), out_refs)
+
+
+def prepare(face, swap, columns_ref, couplings_ref, shifts_ref, place_ref, row_ref, hot_ref, wide_ref, shift_ref):
+    neighbours, own_rows = columns_ref.shape
+    row_ref[...] = jnp.full((SUB, LANE), -1, i32)
+    row_ref[0:neighbours, 0:own_rows] = columns_ref[...]
+    columns = row_ref[...]
     if swap:
-        place = place_ref[0]
+        place = jnp.broadcast_to(place_ref[...], (SUB, LANE))
         lower = (columns >= own_rows) & (columns < own_rows + face)
         upper = (columns >= own_rows + face) & (columns < own_rows + 2 * face)
         columns = jnp.where(
@@ -117,39 +121,31 @@
             jnp.where(place == 1, columns + face, -1),
             jnp.where(upper, jnp.where(place == 0, columns - face, -1), columns),
         )
-    width = lanes((own_rows, LANE))
-    couplings = couplings_ref[...].astype(f32)
     for k in range(neighbours):
-        hot = jnp.where(columns[:, k : k + 1] == width, 1.0, 0.0).astype(bf16)
+        hot = one_hot(columns[k : k + 1, :], own_rows).astype(bf16)
         hot_ref[k * own_rows : (k + 1) * own_rows, 0:LANE] = hot
         hot_ref[k * own_rows : (k + 1) * own_rows, LANE : 2 * LANE] = hot
-        wide_ref[k] = couplings[:, k, :]
+        wide_ref[k] = couplings_ref[k].astype(f32)
     for k in range(shift_ref.shape[0]):
         shift_ref[k] = jnp.broadcast_to(shifts_ref[0:1, k : k + 1], (SUB, LANE))
 
 
 def matvec(blocks_ref, vector_ref, own_ref):
-    groups = vector_ref.shape[0] // SUB
-
-    def group(g, carry):
-        base = pl.multiple_of(g * SUB, SUB)
-        high, low = two_parts(vector_ref[pl.ds(base, SUB), :])
+    sub = subs()
+    for g in range(vector_ref.shape[0] // SUB):
+        high, low = two_parts(vector_ref[g * SUB : (g + 1) * SUB, :])
         left = jnp.concatenate([high.astype(f32), low.astype(f32)], axis=0).astype(bf16)
-        sub = subs()
-        total = jnp.zeros((SUB, LANE), f32)
+        total = None
         for b in range(0, SUB, 2):
-            start = pl.multiple_of((g * SUB + b) * LANE, 2 * LANE)
-            out = dot_nt(left, blocks_ref[pl.ds(start, 2 * LANE), :])
+            start = (g * SUB + b) * LANE
+            out = dot_nt(left, blocks_ref[start : start + 2 * LANE, :])
             both = out[:SUB] + out[SUB:]
-            total = jnp.where(sub == b, both[:, :LANE], total)
+            total = both[:, :LANE] if total is None else jnp.where(sub == b, both[:, :LANE], total)
             total = jnp.where(sub == b + 1, both[:, LANE:], total)
-        own_ref[pl.ds(base, SUB), :] = total
-        return carry
-
-    lax.fori_loop(0, groups, group, 0)
-
-
-def statistics(k, vectors, sketch_ref, packet_in, packet_ref, scratch_ref):
+        own_ref[g * SUB : (g + 1) * SUB, :] = total
+
+
+def statistics(k, vectors, sketch_ref, packet):
     rows = vectors[0].shape[0]
     groups = rows // SUB
     sketches = sketch_ref.shape[0]
@@ -157,25 +153,22 @@
     newest = [vectors[k][g * SUB : (g + 1) * SUB, :] for g in range(groups)]
     new_split = [split(x) for x in newest]
 
-    def one(i, carry):
+    sums = []
+    for i in range(sketches):
         row = sketch_ref[i].astype(f32)
         parts = [newest[g] * row[g * SUB : (g + 1) * SUB, :] for g in range(groups)]
         while len(parts) > 1:
             parts = [a + b for a, b in zip(parts[::2], parts[1::2])] + parts[len(parts) // 2 * 2 :]
-        scratch_ref[pl.ds(pl.multiple_of(i * SUB, SUB), SUB), :] = parts[0]
-        return carry
-
-    lax.fori_loop(0, sketches, one, 0, unroll=4)
-    partial = scratch_ref[...]
-    ones = jnp.ones((SUB, LANE), bf16)
-    high, middle, low = three_parts(partial)
-    across = dot_nt(ones, high) + dot_nt(ones, middle) + dot_nt(ones, low)
-    width = sketches * SUB
-    pick = jnp.where(
-        lax.broadcasted_iota(i32, (width, LANE), 0) // SUB == lax.broadcasted_iota(i32, (width, LANE), 1), 1.0, 0.0
-    ).astype(bf16)
-    high, middle, low = three_parts(across)
-    sketch_row = dot(high, pick) + dot(middle, pick) + dot(low, pick)
+        sums.append(parts[0])
+    high, middle, low = three_parts(jnp.concatenate(sums, axis=0))
+    ones = jnp.ones((LANE, LANE), bf16)
+    across = dot(high, ones) + dot(middle, ones) + dot(low, ones)
+    picked = [jnp.where(lane == i, across[i * SUB : (i + 1) * SUB, :], 0.0) for i in range(sketches)]
+    while len(picked) > 1:
+        picked = [a + b for a, b in zip(picked[::2], picked[1::2])] + picked[len(picked) // 2 * 2 :]
+    sketch_row = picked[0]
+    for step in (4, 2, 1):
+        sketch_row = sketch_row + pltpu.roll(sketch_row, step, 0)
 
     wide = (jnp.zeros((SUB, LANE), f32), jnp.zeros((SUB, LANE), f32))
     for l in range(k + 1):
@@ -192,7 +185,6 @@
         wide = pair_add(wide, tuple(pltpu.roll(x, step, 1) for x in wide))
     wide = two_sum(*wide)
 
-    packet = packet_in
     row_k = sub == k
     packet = jnp.where(row_k & (lane < sketches), sketch_row, packet)
     for part, first in zip(wide, (HI_LANE, LO_LANE)):
@@ -202,40 +194,46 @@
         for step in (4, 2, 1):
             turned = turned + pltpu.roll(turned, step, 0)
         packet = jnp.where(row_k & (lane >= first) & (lane <= first + k), turned, packet)
+    return packet
+
+
+def setup_body(face, swap, *refs):
+    columns_ref, couplings_ref, shifts_ref, place_ref, blocks_ref, vector_ref = refs[:6]
+    own_ref, hot_ref, wide_ref, shift_ref, row_ref = refs[6:]
+    prepare(face, swap, columns_ref, couplings_ref, shifts_ref, place_ref, row_ref, hot_ref, wide_ref, shift_ref)
+    matvec(blocks_ref, vector_ref, own_ref)
+
+
+def middle_body(k, last, *refs):
+    vectors, refs = refs[: k + 1], list(refs[k + 1 :])
+    sketch_ref = refs.pop(0)
+    packet = jnp.zeros((SUB, LANE), f32) if k == 1 else refs.pop(0)[...]
+    if last:
+        (packet_ref,) = refs
+    else:
+        blocks_ref, packet_ref, own_ref = refs
+        matvec(blocks_ref, vectors[k], own_ref)
+    for newest in range(0 if k == 1 else k, k + 1):
+        packet = statistics(newest, vectors, sketch_ref, packet)
     packet_ref[...] = packet
 
 
-def middle_body(k, first, last, *refs):
-    refs = list(refs)
-    vectors = [refs.pop(0) for _ in range(k + 1)]
-    sketch_ref = refs.pop(0)
-    packet_in = jnp.zeros((SUB, LANE), f32) if first else refs.pop(0)[...]
-    if not last:
-        blocks_ref = refs.pop(0)
-    packet_ref = refs.pop(0)
-    own_ref = None if last else refs.pop(0)
-    scratch_ref = refs.pop(0)
-    if not last:
-        matvec(blocks_ref, vectors[k], own_ref)
-    statistics(k, vectors, sketch_ref, packet_in, packet_ref, scratch_ref)
-
-
-def next_body(k, received, last, *refs):
+def next_body(k, starts, last, *refs):
     own_ref, vector_ref, hot_ref, wide_ref, shift_ref = refs[:5]
     refs = refs[5:]
     if not last:
         send_ref, refs = refs[0], refs[1:]
-    halo_refs, refs = refs[:received], refs[received:]
+    halo_refs, refs = refs[: len(starts)], refs[len(starts) :]
     next_ref, refs = refs[0], refs[1:]
     out_refs, extended_ref = refs[:-1], refs[-1]
     rows = vector_ref.shape[0]
     extended_ref[0:rows, :] = vector_ref[...]
-    start = rows
-    for ref in halo_refs:
+    end = rows
+    for start, ref in zip(starts, halo_refs):
         extended_ref[start : start + ref.shape[0], :] = ref[...]
-        start += ref.shape[0]
-    if start < LANE:
-        extended_ref[start:LANE, :] = jnp.zeros((LANE - start, LANE), f32)
+        end += ref.shape[0]
+    if end < LANE:
+        extended_ref[end:LANE, :] = jnp.zeros((LANE - end, LANE), f32)
     parts = jnp.concatenate(two_parts(extended_ref[...]), axis=0)
     gathered = dot(hot_ref[...], parts)
     shift = shift_ref[k]
@@ -378,73 +376,69 @@
     pieces = [2 * face] if swap else [face, face]
     pieces = pieces + [face] * levels
     piece_outs = [((size, width), f32) for size in pieces]
+    starts = [rows + (2 + level) * face for level in reversed(range(levels))] + ([rows] if swap else [rows, rows + face])
     send_pad = -(-sends // 16) * 16
 
     def exchange(outgoing):
-        outgoing = list(outgoing)
+        side, far = list(outgoing[:-levels]), list(outgoing[-levels:])
+        for level in reversed(range(levels)):
+            far[level] = lax.ppermute(far[level], "dom", [(i, i ^ (1 << level)) for i in range(dom)])
         if swap:
-            side = [lax.ppermute(outgoing[0], "col", [(0, 1), (1, 0)])]
-            outgoing = outgoing[1:]
+            side = [lax.ppermute(side[0], "col", [(0, 1), (1, 0)])]
         else:
             up = [(i, i + 1) for i in range(col - 1)]
-            side = [
-                lax.ppermute(outgoing[1], "col", up),
-                lax.ppermute(outgoing[0], "col", [(j, i) for i, j in up]),
-            ]
-            outgoing = outgoing[2:]
-        far = [
-            lax.ppermute(piece, "dom", [(i, i ^ (1 << level)) for i in range(dom)])
-            for level, piece in enumerate(outgoing)
-        ]
-        return side + far
+            down = [(j, i) for i, j in up]
+            side = [lax.ppermute(side[1], "col", up), lax.ppermute(side[0], "col", down)]
+        return far[::-1] + side
 
     send_hot, *outgoing = run(
         first_body,
         [((send_pad, rows), bf16)] + piece_outs,
         (send_rows, start_vector),
         "first",
+        cost=(100_000_000_000, 1_000_000_000),
         scratch=[pltpu.VMEM((SUB, LANE), i32)],
     )
-    place = jnp.full((1, neighbours), lax.axis_index("col"), i32).reshape(1, 1, neighbours)
-    neighbour_hot, wide, shift = run(
-        functools.partial(prepare_body, rows, face, swap),
+    vectors = [start_vector]
+    place = jnp.full((1, LANE), lax.axis_index("col"), i32)
+    received = exchange(outgoing)
+    own, neighbour_hot, wide, shift = run(
+        functools.partial(setup_body, face, swap),
         [
+            ((rows, width), f32),
             ((neighbours * rows, 2 * LANE), bf16),
             ((neighbours, rows, width), f32),
             ((powers, SUB, LANE), f32),
         ],
-        (columns, couplings, shifts.reshape(1, powers), place),
-        "prepare",
-        cost=(4_000_000, 1_000_000),
+        (columns.T, couplings.transpose(1, 0, 2), shifts.reshape(1, powers), place, blocks, start_vector),
+        "setup",
+        cost=(20_000_000, 4_000_000),
+        scratch=[pltpu.VMEM((SUB, LANE), i32)],
     )
-    vectors = [start_vector]
-    packet = None
-    for k in range(n):
-        last = k == powers
-        received = None if last else exchange(outgoing)
-        args = (*vectors, sketch, *(() if packet is None else (packet,)), *(() if last else (blocks,)))
-        result = run(
-            functools.partial(middle_body, k, packet is None, last),
-            [((SUB, LANE), f32)] + ([] if last else [((rows, width), f32)]),
-            args,
-            f"middle_{k}",
-            cost=(20_000_000, 4_000_000),
-            scratch=[pltpu.VMEM((sketches * SUB, LANE), f32)],
-        )
-        packet = result[0]
-        if last:
-            break
+    packet = ()
+    for k in range(powers):
+        if k:
+            received = exchange(outgoing)
+            *packet, own = run(
+                functools.partial(middle_body, k, False),
+                [((SUB, LANE), f32), ((rows, width), f32)],
+                (*vectors, sketch, *packet, blocks),
+                f"middle_{k}",
+                cost=(20_000_000, 4_000_000),
+            )
         final = k + 1 == powers
-        args = (result[1], vectors[-1], neighbour_hot, wide, shift, *(() if final else (send_hot,)), *received)
         vector, *outgoing = run(
-            functools.partial(next_body, k, len(received), final),
+            functools.partial(next_body, k, starts, final),
             [((rows, width), f32)] + ([] if final else piece_outs),
-            args,
+            (own, vectors[-1], neighbour_hot, wide, shift, *(() if final else (send_hot,)), *received),
             f"next_{k}",
             cost=(1_000_000, 1_000_000),
             scratch=[pltpu.VMEM((LANE, LANE), f32)],
         )
         vectors.append(vector)
+    (packet,) = run(
+        functools.partial(middle_body, powers, True), [((SUB, LANE), f32)], (*vectors, sketch, *packet), "middle_last"
+    )
 
     everyone = ("dom", "col")
     packets = lax.all_to_all(jnp.tile(packet, (dom * col, 1)), everyone, 0, 0, tiled=True)

time: 75.1 us -> 65.1 us (0.87)
  Pallas kernels: 23.4 us -> 11.4 us
  local copies, waits for them, and re-layouts: 7.69 us -> 1.64 us
  starting transfers between devices: 28.4 us -> 32.1 us
  waiting for transfers between devices: 1.52 us -> 4.91 us
  blocking collectives: 12.8 us -> 14.1 us
    pallas_call x16 -> x15, Pallas kernels: 23.4 us -> 11.4 us  [run(): pl.pallas_call(body, out_shape=[jax.ShapeDtypeStruct(shape, dtype) for sh...]
    unnamed x16, local copies, waits for them, and re-layouts: 7.68 us -> 1.63 us
    ppermute x30, starting transfers between devices: 28.4 us -> 32.1 us  [the longest x24 31.6 us: exchange(): lax.ppermute(far[level], 'dom', [(i, i ^ 1 << level) for i in range(dom)])]
    ppermute x30, waiting for transfers between devices: 1.52 us -> 4.91 us  [the longest x24 4.9 us: exchange(): lax.ppermute(far[level], 'dom', [(i, i ^ 1 << level) for i in range(dom)])]
    all_to_all x1, blocking collectives: 12.8 us -> 14.1 us  [shards(): lax.all_to_all(jnp.tile(packet, (dom * col, 1)), everyone, 0, 0, tiled=True)]
  transfers between devices with their start and end apart: 30 -> 30, of which waited for: 2 -> 9; matrix products, arithmetic and copies ran while one was open for 2% -> 0% of each run, Pallas kernels for 25% -> 10%
where the time goes in v2:
time: 65.1 us; the launch traced here: 65 us
  starting transfers between devices  32.1 us (49%)
  blocking collectives  14.1 us (22%)
  Pallas kernels  11.4 us (18%)
  waiting for transfers between devices  4.91 us (8%)
  local copies, waits for them, and re-layouts  1.64 us (3%)
  between operations  0.82 us (1%)
    ppermute x24, starting transfers between devices, exchange(): lax.ppermute(far[level], 'dom', [(i, i ^ 1 << level) for i in range(dom)])  31.6 us
    all_to_all x1, blocking collectives, shards(): lax.all_to_all(jnp.tile(packet, (dom * col, 1)), everyone, 0, 0, tiled=True)  14.1 us
    pallas_call x15, Pallas kernels, run(): pl.pallas_call(body, out_shape=[jax.ShapeDtypeStruct(shape, dtype) for sh...  11.4 us
    ppermute x24, waiting for transfers between devices, exchange(): lax.ppermute(far[level], 'dom', [(i, i ^ 1 << level) for i in range(dom)])  4.9 us
    unnamed x16, local copies, waits for them, and re-layouts  1.63 us
  transfers between devices with their start and end apart: 30, of which 9 were waited for; matrix products, arithmetic and copies ran while one was open for 0% of the time, Pallas kernels for 10%

profile of v2, /device:TPU:0, one launch (start us, length us, event | category | flops | bytes accessed | tf_op | source)
XLA Modules:
  0.0 65.0 jit_solution(10375026647751326317)
XLA Ops:
  0.7 0.9 %copy-done.2 = f32[96,128]{1,0:T(8,128)S(1)} copy-done((f32[96,128]{1,0:T(8,128)S(1)}, f32[96,128]{1,0:T(8,128)}, u32[]{:S(2)}) %copy-start.2) | copy-done | bytes 49176
  1.6 0.7 %copy-done.7 = s32[1,24]{1,0:T(1,128)S(1)} copy-done((s32[1,24]{1,0:T(1,128)S(1)}, s32[1,24]{1,0:T(1,128)}, u32[]{:S(2)}) %copy-start.7) | copy-done | bytes 120
  2.5 0.5 collective-permute-start.4
  3.0 3.6 %collective-permute-start = (f32[4,128]{1,0:T(4,128)S(1)}, f32[4,128]{1,0:T(4,128)S(1)}, u32[]{:S(2)}, u32[]{:S(2)}) collective-permute-start(f32[4,128]{1,0:T(4,128)S(1)} %get-tuple-element.58), channel_id=1, source_target_pairs={{0,16},{2,18},{4,20},{6,22},{8,24},{10,26},{12,28},{14,30},{16,0},... | collective-permute-start | bytes 6152 | tf_op jit(solution)/shard_map/ppermute | solution.py:385
  6.6 1.6 %collective-permute-start.1 = (f32[4,128]{1,0:T(4,128)S(1)}, f32[4,128]{1,0:T(4,128)S(1)}, u32[]{:S(2)}, u32[]{:S(2)}) collective-permute-start(f32[4,128]{1,0:T(4,128)S(1)} %get-tuple-element.59), channel_id=1, source_target_pairs={{0,8},{2,10},{4,12},{6,14},{8,0},{10,2},{12,4},{14,6},{16,24},{18,... | collective-permute-start | bytes 6152 | tf_op jit(solution)/shard_map/ppermute | solution.py:385
  8.2 1.5 %collective-permute-start.2 = (f32[4,128]{1,0:T(4,128)S(1)}, f32[4,128]{1,0:T(4,128)S(1)}, u32[]{:S(2)}, u32[]{:S(2)}) collective-permute-start(f32[4,128]{1,0:T(4,128)S(1)} %get-tuple-element.60), channel_id=1, source_target_pairs={{0,4},{2,6},{4,0},{6,2},{8,12},{10,14},{12,8},{14,10},{16,20},{18,... | collective-permute-start | bytes 6152 | tf_op jit(solution)/shard_map/ppermute | solution.py:385
  9.7 1.5 %collective-permute-start.3 = (f32[4,128]{1,0:T(4,128)S(1)}, f32[4,128]{1,0:T(4,128)S(1)}, u32[]{:S(2)}, u32[]{:S(2)}) collective-permute-start(f32[4,128]{1,0:T(4,128)S(1)} %get-tuple-element.61), channel_id=1, source_target_pairs={{0,2},{2,0},{4,6},{6,4},{8,10},{10,8},{12,14},{14,12},{16,18},{18,... | collective-permute-start | bytes 6152 | tf_op jit(solution)/shard_map/ppermute | solution.py:385
  11.2 0.9 %setup.1 = (f32[96,128]{1,0:T(8,128)S(1)}, bf16[576,256]{1,0:T(8,128)(2,1)S(1)}, f32[6,96,128]{2,1,0:T(8,128)S(1)}, f32[6,8,128]{2,1,0:T(8,128)S(1)}) custom-call(s32[6,96]{1,0:T(8,128)S(1)} %bitcast.13, bf16[6,96,128]{2,1,0:T(8,128)(2,1)S(1)} %bitcast.12, f32[1,6]{1,0:T(1,128)S(1)} %bitcast.14, s32[1,128]{1,0:T(1,128)S(1)} %broadcast_in_dim.3.refs_3_, ...), custom_call_target="tpu_custom_call" | custom-call | flops 20000000 | bytes 4000000 | tf_op jit(solution)/shard_map/setup/pallas_call | solution.py:21
  12.2 1.1 %collective-permute-done.3.refs_9_ = f32[4,128]{1,0:T(4,128)S(1)} collective-permute-done((f32[4,128]{1,0:T(4,128)S(1)}, f32[4,128]{1,0:T(4,128)S(1)}, u32[]{:S(2)}, u32[]{:S(2)}) %collective-permute-start.3) | collective-permute-done | bytes 2080 | tf_op jit(solution)/shard_map/ppermute | solution.py:385
  14.8 1.7 %collective-permute-start.8 = (f32[4,128]{1,0:T(4,128)S(1)}, f32[4,128]{1,0:T(4,128)S(1)}, u32[]{:S(2)}, u32[]{:S(2)}) collective-permute-start(f32[4,128]{1,0:T(4,128)S(1)} %get-tuple-element.68), channel_id=1, source_target_pairs={{0,2},{2,0},{4,6},{6,4},{8,10},{10,8},{12,14},{14,12},{16,18},{18,... | collective-permute-start | bytes 6152 | tf_op jit(solution)/shard_map/ppermute | solution.py:385
  16.5 1.3 %middle_1.1 = (f32[8,128]{1,0:T(8,128)S(1)}, f32[96,128]{1,0:T(8,128)S(1)}) custom-call(f32[96,128]{1,0:T(8,128)S(1)} %copy-done.3, f32[96,128]{1,0:T(8,128)S(1)} %get-tuple-element.63.refs_1_, bf16[32,96,128]{2,1,0:T(8,128)(2,1)S(1)} %copy-done.1, bf16[12288,128]{1,0:T(8,128)(2,1)S(1)} %bitcast.6), custom_call_target="tpu_custom_call" | custom-call | flops 20000000 | bytes 4000000 | tf_op jit(solution)/shard_map/middle_1/pallas_call | solution.py:21
  18.8 2.9 %collective-permute-start.10 = (f32[4,128]{1,0:T(4,128)S(1)}, f32[4,128]{1,0:T(4,128)S(1)}, u32[]{:S(2)}, u32[]{:S(2)}) collective-permute-start(f32[4,128]{1,0:T(4,128)S(1)} %get-tuple-element.73), channel_id=1, source_target_pairs={{0,16},{2,18},{4,20},{6,22},{8,24},{10,26},{12,28},{14,30},{16,0},... | collective-permute-start | bytes 6152 | tf_op jit(solution)/shard_map/ppermute | solution.py:385
  21.6 1.6 %collective-permute-start.11 = (f32[4,128]{1,0:T(4,128)S(1)}, f32[4,128]{1,0:T(4,128)S(1)}, u32[]{:S(2)}, u32[]{:S(2)}) collective-permute-start(f32[4,128]{1,0:T(4,128)S(1)} %get-tuple-element.74), channel_id=1, source_target_pairs={{0,8},{2,10},{4,12},{6,14},{8,0},{10,2},{12,4},{14,6},{16,24},{18,... | collective-permute-start | bytes 6152 | tf_op jit(solution)/shard_map/ppermute | solution.py:385
  23.2 1.5 %collective-permute-start.12 = (f32[4,128]{1,0:T(4,128)S(1)}, f32[4,128]{1,0:T(4,128)S(1)}, u32[]{:S(2)}, u32[]{:S(2)}) collective-permute-start(f32[4,128]{1,0:T(4,128)S(1)} %get-tuple-element.75), channel_id=1, source_target_pairs={{0,4},{2,6},{4,0},{6,2},{8,12},{10,14},{12,8},{14,10},{16,20},{18,... | collective-permute-start | bytes 6152 | tf_op jit(solution)/shard_map/ppermute | solution.py:385
  24.7 1.5 %collective-permute-start.13 = (f32[4,128]{1,0:T(4,128)S(1)}, f32[4,128]{1,0:T(4,128)S(1)}, u32[]{:S(2)}, u32[]{:S(2)}) collective-permute-start(f32[4,128]{1,0:T(4,128)S(1)} %get-tuple-element.76), channel_id=1, source_target_pairs={{0,2},{2,0},{4,6},{6,4},{8,10},{10,8},{12,14},{14,12},{16,18},{18,... | collective-permute-start | bytes 6152 | tf_op jit(solution)/shard_map/ppermute | solution.py:385
  26.2 1.1 %middle_2.1 = (f32[8,128]{1,0:T(8,128)S(1)}, f32[96,128]{1,0:T(8,128)S(1)}) custom-call(f32[96,128]{1,0:T(8,128)S(1)} %copy-done.3, f32[96,128]{1,0:T(8,128)S(1)} %get-tuple-element.63.refs_1_, f32[96,128]{1,0:T(8,128)S(1)} %get-tuple-element.70.refs_2_.refs_1_, bf16[32,96,128]{2,1,0:T(8,128)(2,1)S(1)} %copy-done.1, f32[8,128]{1,0:T(8,128)S(1)} %get-tuple-element.71.refs_4_, ...), custom_call_target="tpu_custom_call" | custom-call | flops 20000000 | bytes 4000000 | tf_op jit(solution)/shard_map/middle_2/pallas_call | solution.py:21
  27.3 1.0 %collective-permute-done.13.refs_9_ = f32[4,128]{1,0:T(4,128)S(1)} collective-permute-done((f32[4,128]{1,0:T(4,128)S(1)}, f32[4,128]{1,0:T(4,128)S(1)}, u32[]{:S(2)}, u32[]{:S(2)}) %collective-permute-start.13) | collective-permute-done | bytes 2080 | tf_op jit(solution)/shard_map/ppermute | solution.py:385
  29.8 1.7 %collective-permute-start.18 = (f32[4,128]{1,0:T(4,128)S(1)}, f32[4,128]{1,0:T(4,128)S(1)}, u32[]{:S(2)}, u32[]{:S(2)}) collective-permute-start(f32[4,128]{1,0:T(4,128)S(1)} %get-tuple-element.84), channel_id=1, source_target_pairs={{0,2},{2,0},{4,6},{6,4},{8,10},{10,8},{12,14},{14,12},{16,18},{18,... | collective-permute-start | bytes 6152 | tf_op jit(solution)/shard_map/ppermute | solution.py:385
  31.5 1.1 %middle_3.1 = (f32[8,128]{1,0:T(8,128)S(1)}, f32[96,128]{1,0:T(8,128)S(1)}) custom-call(f32[96,128]{1,0:T(8,128)S(1)} %copy-done.3, f32[96,128]{1,0:T(8,128)S(1)} %get-tuple-element.63.refs_1_, f32[96,128]{1,0:T(8,128)S(1)} %get-tuple-element.70.refs_2_.refs_1_, f32[96,128]{1,0:T(8,128)S(1)} %get-tuple-element.78.refs_3_.refs_1_, ...), custom_call_target="tpu_custom_call" | custom-call | flops 20000000 | bytes 4000000 | tf_op jit(solution)/shard_map/middle_3/pallas_call | solution.py:21
  32.7 0.6 collective-permute-done.15.refs_6_
  33.8 2.9 %collective-permute-start.20 = (f32[4,128]{1,0:T(4,128)S(1)}, f32[4,128]{1,0:T(4,128)S(1)}, u32[]{:S(2)}, u32[]{:S(2)}) collective-permute-start(f32[4,128]{1,0:T(4,128)S(1)} %get-tuple-element.89), channel_id=1, source_target_pairs={{0,16},{2,18},{4,20},{6,22},{8,24},{10,26},{12,28},{14,30},{16,0},... | collective-permute-start | bytes 6152 | tf_op jit(solution)/shard_map/ppermute | solution.py:385
  36.7 1.6 %collective-permute-start.21 = (f32[4,128]{1,0:T(4,128)S(1)}, f32[4,128]{1,0:T(4,128)S(1)}, u32[]{:S(2)}, u32[]{:S(2)}) collective-permute-start(f32[4,128]{1,0:T(4,128)S(1)} %get-tuple-element.90), channel_id=1, source_target_pairs={{0,8},{2,10},{4,12},{6,14},{8,0},{10,2},{12,4},{14,6},{16,24},{18,... | collective-permute-start | bytes 6152 | tf_op jit(solution)/shard_map/ppermute | solution.py:385
  38.3 1.5 %collective-permute-start.22 = (f32[4,128]{1,0:T(4,128)S(1)}, f32[4,128]{1,0:T(4,128)S(1)}, u32[]{:S(2)}, u32[]{:S(2)}) collective-permute-start(f32[4,128]{1,0:T(4,128)S(1)} %get-tuple-element.91), channel_id=1, source_target_pairs={{0,4},{2,6},{4,0},{6,2},{8,12},{10,14},{12,8},{14,10},{16,20},{18,... | collective-permute-start | bytes 6152 | tf_op jit(solution)/shard_map/ppermute | solution.py:385
  39.8 1.5 %collective-permute-start.23 = (f32[4,128]{1,0:T(4,128)S(1)}, f32[4,128]{1,0:T(4,128)S(1)}, u32[]{:S(2)}, u32[]{:S(2)}) collective-permute-start(f32[4,128]{1,0:T(4,128)S(1)} %get-tuple-element.92), channel_id=1, source_target_pairs={{0,2},{2,0},{4,6},{6,4},{8,10},{10,8},{12,14},{14,12},{16,18},{18,... | collective-permute-start | bytes 6152 | tf_op jit(solution)/shard_map/ppermute | solution.py:385
  41.3 1.2 %middle_4.1 = (f32[8,128]{1,0:T(8,128)S(1)}, f32[96,128]{1,0:T(8,128)S(1)}) custom-call(f32[96,128]{1,0:T(8,128)S(1)} %copy-done.3, f32[96,128]{1,0:T(8,128)S(1)} %get-tuple-element.63.refs_1_, f32[96,128]{1,0:T(8,128)S(1)} %get-tuple-element.70.refs_2_.refs_1_, f32[96,128]{1,0:T(8,128)S(1)} %get-tuple-element.78.refs_3_.refs_1_, ...), custom_call_target="tpu_custom_call" | custom-call | flops 20000000 | bytes 4000000 | tf_op jit(solution)/shard_map/middle_4/pallas_call | solution.py:21
  42.5 0.9 %collective-permute-done.23.refs_9_ = f32[4,128]{1,0:T(4,128)S(1)} collective-permute-done((f32[4,128]{1,0:T(4,128)S(1)}, f32[4,128]{1,0:T(4,128)S(1)}, u32[]{:S(2)}, u32[]{:S(2)}) %collective-permute-start.23) | collective-permute-done | bytes 2080 | tf_op jit(solution)/shard_map/ppermute | solution.py:385
  44.9 1.7 %collective-permute-start.28 = (f32[4,128]{1,0:T(4,128)S(1)}, f32[4,128]{1,0:T(4,128)S(1)}, u32[]{:S(2)}, u32[]{:S(2)}) collective-permute-start(f32[4,128]{1,0:T(4,128)S(1)} %get-tuple-element.100), channel_id=1, source_target_pairs={{0,2},{2,0},{4,6},{6,4},{8,10},{10,8},{12,14},{14,12},{16,18},{18,... | collective-permute-start | bytes 6152 | tf_op jit(solution)/shard_map/ppermute | solution.py:385
  46.6 1.2 %middle_5.1 = (f32[8,128]{1,0:T(8,128)S(1)}, f32[96,128]{1,0:T(8,128)S(1)}) custom-call(f32[96,128]{1,0:T(8,128)S(1)} %copy-done.3, f32[96,128]{1,0:T(8,128)S(1)} %get-tuple-element.63.refs_1_, f32[96,128]{1,0:T(8,128)S(1)} %get-tuple-element.70.refs_2_.refs_1_, f32[96,128]{1,0:T(8,128)S(1)} %get-tuple-element.78.refs_3_.refs_1_, ...), custom_call_target="tpu_custom_call" | custom-call | flops 20000000 | bytes 4000000 | tf_op jit(solution)/shard_map/middle_5/pallas_call | solution.py:21
  47.8 0.5 collective-permute-done.25.refs_5_
  48.7 0.8 %middle_last.1 = f32[8,128]{1,0:T(8,128)S(1)} custom-call(f32[96,128]{1,0:T(8,128)S(1)} %copy-done.3, f32[96,128]{1,0:T(8,128)S(1)} %get-tuple-element.63.refs_1_, f32[96,128]{1,0:T(8,128)S(1)} %get-tuple-element.70.refs_2_.refs_1_, f32[96,128]{1,0:T(8,128)S(1)} %get-tuple-element.78.refs_3_.refs_1_, f32[96,128]{1,0:T(8,128)S(1)} %get-tuple-element.86.refs_4_.refs_1_, ...), custom_call_target="tpu_custom_call" | custom-call | tf_op jit(solution)/shard_map/middle_last/pallas_call | solution.py:21
  49.5 14.1 %all_to_all.8 = f32[32,8,128]{2,1,0:T(8,128)S(1)} all-to-all(f32[32,8,128]{2,1,0:T(8,128)S(1)} %tile.2), channel_id=1, replica_groups=mesh['dom'=16,'col'=2] {'dom','col'}, dimensions={0} | all-to-all | bytes 262144 | tf_op jit(solution)/shard_map/all_to_all | solution.py:444
  63.6 1.4 %last.1 = (f32[7,96,128]{2,1,0:T(8,128)}, f32[7,7]{1,0:T(8,128)}, f32[7,7]{1,0:T(8,128)}) custom-call(f32[256,128]{1,0:T(8,128)S(1)} %bitcast.11, f32[96,128]{1,0:T(8,128)S(1)} %copy-done.3, f32[96,128]{1,0:T(8,128)S(1)} %get-tuple-element.63.refs_1_, f32[96,128]{1,0:T(8,128)S(1)} %get-tuple-element.70.refs_2_.refs_1_, ...), custom_call_target="tpu_custom_call" | custom-call | flops 5000000 | bytes 1000000 | tf_op jit(solution)/shard_map/last/pallas_call | solution.py:21
  (62 shorter events, 6.6 us)
Async XLA Ops:
  0.6 10.6 %copy-start = (bf16[96,128,128]{2,1,0:T(8,128)(2,1)S(1)}, bf16[96,128,128]{2,1,0:T(8,128)(2,1)}, u32[]{:S(2)}) copy-start(bf16[96,128,128]{2,1,0:T(8,128)(2,1)} %param.7) | copy-start | bytes 9437188
  2.3 8.9 %copy-start.6 = (f32[6]{0:T(128)S(1)}, f32[6]{0:T(128)}, u32[]{:S(2)}) copy-start(f32[6]{0:T(128)} %param.11) | copy-start | bytes 76
  2.5 10.8 %collective-permute-start.4 = (f32[8,128]{1,0:T(8,128)S(1)}, f32[8,128]{1,0:T(8,128)S(1)}, u32[]{:S(2)}, u32[]{:S(2)}) collective-permute-start(f32[8,128]{1,0:T(8,128)S(1)} %get-tuple-element.62), channel_id=1, source_target_pairs={{0,1},{1,0},{2,3},{3,2},{4,5},{5,4},{6,7},{7,6},{8,9},{9,8},{10,11... | collective-permute-start | bytes 12296 | tf_op jit(solution)/shard_map/ppermute | solution.py:387
  3.0 9.2 %collective-permute-start = (f32[4,128]{1,0:T(4,128)S(1)}, f32[4,128]{1,0:T(4,128)S(1)}, u32[]{:S(2)}, u32[]{:S(2)}) collective-permute-start(f32[4,128]{1,0:T(4,128)S(1)} %get-tuple-element.58), channel_id=1, source_target_pairs={{0,16},{2,18},{4,20},{6,22},{8,24},{10,26},{12,28},{14,30},{16,0},... | collective-permute-start | bytes 6152 | tf_op jit(solution)/shard_map/ppermute | solution.py:385
  6.6 5.6 %collective-permute-start.1 = (f32[4,128]{1,0:T(4,128)S(1)}, f32[4,128]{1,0:T(4,128)S(1)}, u32[]{:S(2)}, u32[]{:S(2)}) collective-permute-start(f32[4,128]{1,0:T(4,128)S(1)} %get-tuple-element.59), channel_id=1, source_target_pairs={{0,8},{2,10},{4,12},{6,14},{8,0},{10,2},{12,4},{14,6},{16,24},{18,... | collective-permute-start | bytes 6152 | tf_op jit(solution)/shard_map/ppermute | solution.py:385
  8.2 4.0 %collective-permute-start.2 = (f32[4,128]{1,0:T(4,128)S(1)}, f32[4,128]{1,0:T(4,128)S(1)}, u32[]{:S(2)}, u32[]{:S(2)}) collective-permute-start(f32[4,128]{1,0:T(4,128)S(1)} %get-tuple-element.60), channel_id=1, source_target_pairs={{0,4},{2,6},{4,0},{6,2},{8,12},{10,14},{12,8},{14,10},{16,20},{18,... | collective-permute-start | bytes 6152 | tf_op jit(solution)/shard_map/ppermute | solution.py:385
  9.7 3.6 %collective-permute-start.3 = (f32[4,128]{1,0:T(4,128)S(1)}, f32[4,128]{1,0:T(4,128)S(1)}, u32[]{:S(2)}, u32[]{:S(2)}) collective-permute-start(f32[4,128]{1,0:T(4,128)S(1)} %get-tuple-element.61), channel_id=1, source_target_pairs={{0,2},{2,0},{4,6},{6,4},{8,10},{10,8},{12,14},{14,12},{16,18},{18,... | collective-permute-start | bytes 6152 | tf_op jit(solution)/shard_map/ppermute | solution.py:385
  13.7 4.7 %collective-permute-start.9 = (f32[8,128]{1,0:T(8,128)S(1)}, f32[8,128]{1,0:T(8,128)S(1)}, u32[]{:S(2)}, u32[]{:S(2)}) collective-permute-start(f32[8,128]{1,0:T(8,128)S(1)} %get-tuple-element.69), channel_id=1, source_target_pairs={{0,1},{1,0},{2,3},{3,2},{4,5},{5,4},{6,7},{7,6},{8,9},{9,8},{10,11... | collective-permute-start | bytes 12296 | tf_op jit(solution)/shard_map/ppermute | solution.py:387
  13.7 4.5 %collective-permute-start.5 = (f32[4,128]{1,0:T(4,128)S(1)}, f32[4,128]{1,0:T(4,128)S(1)}, u32[]{:S(2)}, u32[]{:S(2)}) collective-permute-start(f32[4,128]{1,0:T(4,128)S(1)} %get-tuple-element.65), channel_id=1, source_target_pairs={{0,16},{2,18},{4,20},{6,22},{8,24},{10,26},{12,28},{14,30},{16,0},... | collective-permute-start | bytes 6152 | tf_op jit(solution)/shard_map/ppermute | solution.py:385
  14.1 4.2 %collective-permute-start.6 = (f32[4,128]{1,0:T(4,128)S(1)}, f32[4,128]{1,0:T(4,128)S(1)}, u32[]{:S(2)}, u32[]{:S(2)}) collective-permute-start(f32[4,128]{1,0:T(4,128)S(1)} %get-tuple-element.66), channel_id=1, source_target_pairs={{0,8},{2,10},{4,12},{6,14},{8,0},{10,2},{12,4},{14,6},{16,24},{18,... | collective-permute-start | bytes 6152 | tf_op jit(solution)/shard_map/ppermute | solution.py:385
  14.5 3.7 %collective-permute-start.7 = (f32[4,128]{1,0:T(4,128)S(1)}, f32[4,128]{1,0:T(4,128)S(1)}, u32[]{:S(2)}, u32[]{:S(2)}) collective-permute-start(f32[4,128]{1,0:T(4,128)S(1)} %get-tuple-element.67), channel_id=1, source_target_pairs={{0,4},{2,6},{4,0},{6,2},{8,12},{10,14},{12,8},{14,10},{16,20},{18,... | collective-permute-start | bytes 6152 | tf_op jit(solution)/shard_map/ppermute | solution.py:385
  14.8 3.6 %collective-permute-start.8 = (f32[4,128]{1,0:T(4,128)S(1)}, f32[4,128]{1,0:T(4,128)S(1)}, u32[]{:S(2)}, u32[]{:S(2)}) collective-permute-start(f32[4,128]{1,0:T(4,128)S(1)} %get-tuple-element.68), channel_id=1, source_target_pairs={{0,2},{2,0},{4,6},{6,4},{8,10},{10,8},{12,14},{14,12},{16,18},{18,... | collective-permute-start | bytes 6152 | tf_op jit(solution)/shard_map/ppermute | solution.py:385
  18.8 9.6 %collective-permute-start.14 = (f32[8,128]{1,0:T(8,128)S(1)}, f32[8,128]{1,0:T(8,128)S(1)}, u32[]{:S(2)}, u32[]{:S(2)}) collective-permute-start(f32[8,128]{1,0:T(8,128)S(1)} %get-tuple-element.77), channel_id=1, source_target_pairs={{0,1},{1,0},{2,3},{3,2},{4,5},{5,4},{6,7},{7,6},{8,9},{9,8},{10,11... | collective-permute-start | bytes 12296 | tf_op jit(solution)/shard_map/ppermute | solution.py:387
  18.8 8.6 %collective-permute-start.10 = (f32[4,128]{1,0:T(4,128)S(1)}, f32[4,128]{1,0:T(4,128)S(1)}, u32[]{:S(2)}, u32[]{:S(2)}) collective-permute-start(f32[4,128]{1,0:T(4,128)S(1)} %get-tuple-element.73), channel_id=1, source_target_pairs={{0,16},{2,18},{4,20},{6,22},{8,24},{10,26},{12,28},{14,30},{16,0},... | collective-permute-start | bytes 6152 | tf_op jit(solution)/shard_map/ppermute | solution.py:385
  21.6 5.7 %collective-permute-start.11 = (f32[4,128]{1,0:T(4,128)S(1)}, f32[4,128]{1,0:T(4,128)S(1)}, u32[]{:S(2)}, u32[]{:S(2)}) collective-permute-start(f32[4,128]{1,0:T(4,128)S(1)} %get-tuple-element.74), channel_id=1, source_target_pairs={{0,8},{2,10},{4,12},{6,14},{8,0},{10,2},{12,4},{14,6},{16,24},{18,... | collective-permute-start | bytes 6152 | tf_op jit(solution)/shard_map/ppermute | solution.py:385
  23.2 4.1 %collective-permute-start.12 = (f32[4,128]{1,0:T(4,128)S(1)}, f32[4,128]{1,0:T(4,128)S(1)}, u32[]{:S(2)}, u32[]{:S(2)}) collective-permute-start(f32[4,128]{1,0:T(4,128)S(1)} %get-tuple-element.75), channel_id=1, source_target_pairs={{0,4},{2,6},{4,0},{6,2},{8,12},{10,14},{12,8},{14,10},{16,20},{18,... | collective-permute-start | bytes 6152 | tf_op jit(solution)/shard_map/ppermute | solution.py:385
  24.7 3.6 %collective-permute-start.13 = (f32[4,128]{1,0:T(4,128)S(1)}, f32[4,128]{1,0:T(4,128)S(1)}, u32[]{:S(2)}, u32[]{:S(2)}) collective-permute-start(f32[4,128]{1,0:T(4,128)S(1)} %get-tuple-element.76), channel_id=1, source_target_pairs={{0,2},{2,0},{4,6},{6,4},{8,10},{10,8},{12,14},{14,12},{16,18},{18,... | collective-permute-start | bytes 6152 | tf_op jit(solution)/shard_map/ppermute | solution.py:385
  28.7 4.7 %collective-permute-start.19 = (f32[8,128]{1,0:T(8,128)S(1)}, f32[8,128]{1,0:T(8,128)S(1)}, u32[]{:S(2)}, u32[]{:S(2)}) collective-permute-start(f32[8,128]{1,0:T(8,128)S(1)} %get-tuple-element.85), channel_id=1, source_target_pairs={{0,1},{1,0},{2,3},{3,2},{4,5},{5,4},{6,7},{7,6},{8,9},{9,8},{10,11... | collective-permute-start | bytes 12296 | tf_op jit(solution)/shard_map/ppermute | solution.py:387
  28.7 4.5 %collective-permute-start.15 = (f32[4,128]{1,0:T(4,128)S(1)}, f32[4,128]{1,0:T(4,128)S(1)}, u32[]{:S(2)}, u32[]{:S(2)}) collective-permute-start(f32[4,128]{1,0:T(4,128)S(1)} %get-tuple-element.81), channel_id=1, source_target_pairs={{0,16},{2,18},{4,20},{6,22},{8,24},{10,26},{12,28},{14,30},{16,0},... | collective-permute-start | bytes 6152 | tf_op jit(solution)/shard_map/ppermute | solution.py:385
  29.1 4.1 %collective-permute-start.16 = (f32[4,128]{1,0:T(4,128)S(1)}, f32[4,128]{1,0:T(4,128)S(1)}, u32[]{:S(2)}, u32[]{:S(2)}) collective-permute-start(f32[4,128]{1,0:T(4,128)S(1)} %get-tuple-element.82), channel_id=1, source_target_pairs={{0,8},{2,10},{4,12},{6,14},{8,0},{10,2},{12,4},{14,6},{16,24},{18,... | collective-permute-start | bytes 6152 | tf_op jit(solution)/shard_map/ppermute | solution.py:385
  29.5 3.7 %collective-permute-start.17 = (f32[4,128]{1,0:T(4,128)S(1)}, f32[4,128]{1,0:T(4,128)S(1)}, u32[]{:S(2)}, u32[]{:S(2)}) collective-permute-start(f32[4,128]{1,0:T(4,128)S(1)} %get-tuple-element.83), channel_id=1, source_target_pairs={{0,4},{2,6},{4,0},{6,2},{8,12},{10,14},{12,8},{14,10},{16,20},{18,... | collective-permute-start | bytes 6152 | tf_op jit(solution)/shard_map/ppermute | solution.py:385
  29.8 3.6 %collective-permute-start.18 = (f32[4,128]{1,0:T(4,128)S(1)}, f32[4,128]{1,0:T(4,128)S(1)}, u32[]{:S(2)}, u32[]{:S(2)}) collective-permute-start(f32[4,128]{1,0:T(4,128)S(1)} %get-tuple-element.84), channel_id=1, source_target_pairs={{0,2},{2,0},{4,6},{6,4},{8,10},{10,8},{12,14},{14,12},{16,18},{18,... | collective-permute-start | bytes 6152 | tf_op jit(solution)/shard_map/ppermute | solution.py:385
  33.8 9.6 %collective-permute-start.24 = (f32[8,128]{1,0:T(8,128)S(1)}, f32[8,128]{1,0:T(8,128)S(1)}, u32[]{:S(2)}, u32[]{:S(2)}) collective-permute-start(f32[8,128]{1,0:T(8,128)S(1)} %get-tuple-element.93), channel_id=1, source_target_pairs={{0,1},{1,0},{2,3},{3,2},{4,5},{5,4},{6,7},{7,6},{8,9},{9,8},{10,11... | collective-permute-start | bytes 12296 | tf_op jit(solution)/shard_map/ppermute | solution.py:387
  33.8 8.6 %collective-permute-start.20 = (f32[4,128]{1,0:T(4,128)S(1)}, f32[4,128]{1,0:T(4,128)S(1)}, u32[]{:S(2)}, u32[]{:S(2)}) collective-permute-start(f32[4,128]{1,0:T(4,128)S(1)} %get-tuple-element.89), channel_id=1, source_target_pairs={{0,16},{2,18},{4,20},{6,22},{8,24},{10,26},{12,28},{14,30},{16,0},... | collective-permute-start | bytes 6152 | tf_op jit(solution)/shard_map/ppermute | solution.py:385
  36.7 5.7 %collective-permute-start.21 = (f32[4,128]{1,0:T(4,128)S(1)}, f32[4,128]{1,0:T(4,128)S(1)}, u32[]{:S(2)}, u32[]{:S(2)}) collective-permute-start(f32[4,128]{1,0:T(4,128)S(1)} %get-tuple-element.90), channel_id=1, source_target_pairs={{0,8},{2,10},{4,12},{6,14},{8,0},{10,2},{12,4},{14,6},{16,24},{18,... | collective-permute-start | bytes 6152 | tf_op jit(solution)/shard_map/ppermute | solution.py:385
  38.3 4.2 %collective-permute-start.22 = (f32[4,128]{1,0:T(4,128)S(1)}, f32[4,128]{1,0:T(4,128)S(1)}, u32[]{:S(2)}, u32[]{:S(2)}) collective-permute-start(f32[4,128]{1,0:T(4,128)S(1)} %get-tuple-element.91), channel_id=1, source_target_pairs={{0,4},{2,6},{4,0},{6,2},{8,12},{10,14},{12,8},{14,10},{16,20},{18,... | collective-permute-start | bytes 6152 | tf_op jit(solution)/shard_map/ppermute | solution.py:385
  39.8 3.6 %collective-permute-start.23 = (f32[4,128]{1,0:T(4,128)S(1)}, f32[4,128]{1,0:T(4,128)S(1)}, u32[]{:S(2)}, u32[]{:S(2)}) collective-permute-start(f32[4,128]{1,0:T(4,128)S(1)} %get-tuple-element.92), channel_id=1, source_target_pairs={{0,2},{2,0},{4,6},{6,4},{8,10},{10,8},{12,14},{14,12},{16,18},{18,... | collective-permute-start | bytes 6152 | tf_op jit(solution)/shard_map/ppermute | solution.py:385
  43.8 4.7 %collective-permute-start.29 = (f32[8,128]{1,0:T(8,128)S(1)}, f32[8,128]{1,0:T(8,128)S(1)}, u32[]{:S(2)}, u32[]{:S(2)}) collective-permute-start(f32[8,128]{1,0:T(8,128)S(1)} %get-tuple-element.101), channel_id=1, source_target_pairs={{0,1},{1,0},{2,3},{3,2},{4,5},{5,4},{6,7},{7,6},{8,9},{9,8},{10,11... | collective-permute-start | bytes 12296 | tf_op jit(solution)/shard_map/ppermute | solution.py:387
  43.8 4.5 %collective-permute-start.25 = (f32[4,128]{1,0:T(4,128)S(1)}, f32[4,128]{1,0:T(4,128)S(1)}, u32[]{:S(2)}, u32[]{:S(2)}) collective-permute-start(f32[4,128]{1,0:T(4,128)S(1)} %get-tuple-element.97), channel_id=1, source_target_pairs={{0,16},{2,18},{4,20},{6,22},{8,24},{10,26},{12,28},{14,30},{16,0},... | collective-permute-start | bytes 6152 | tf_op jit(solution)/shard_map/ppermute | solution.py:385
  44.2 4.1 %collective-permute-start.26 = (f32[4,128]{1,0:T(4,128)S(1)}, f32[4,128]{1,0:T(4,128)S(1)}, u32[]{:S(2)}, u32[]{:S(2)}) collective-permute-start(f32[4,128]{1,0:T(4,128)S(1)} %get-tuple-element.98), channel_id=1, source_target_pairs={{0,8},{2,10},{4,12},{6,14},{8,0},{10,2},{12,4},{14,6},{16,24},{18,... | collective-permute-start | bytes 6152 | tf_op jit(solution)/shard_map/ppermute | solution.py:385
  44.6 3.7 %collective-permute-start.27 = (f32[4,128]{1,0:T(4,128)S(1)}, f32[4,128]{1,0:T(4,128)S(1)}, u32[]{:S(2)}, u32[]{:S(2)}) collective-permute-start(f32[4,128]{1,0:T(4,128)S(1)} %get-tuple-element.99), channel_id=1, source_target_pairs={{0,4},{2,6},{4,0},{6,2},{8,12},{10,14},{12,8},{14,10},{16,20},{18,... | collective-permute-start | bytes 6152 | tf_op jit(solution)/shard_map/ppermute | solution.py:385
  44.9 3.6 %collective-permute-start.28 = (f32[4,128]{1,0:T(4,128)S(1)}, f32[4,128]{1,0:T(4,128)S(1)}, u32[]{:S(2)}, u32[]{:S(2)}) collective-permute-start(f32[4,128]{1,0:T(4,128)S(1)} %get-tuple-element.100), channel_id=1, source_target_pairs={{0,2},{2,0},{4,6},{6,4},{8,10},{10,8},{12,14},{14,12},{16,18},{18,... | collective-permute-start | bytes 6152 | tf_op jit(solution)/shard_map/ppermute | solution.py:385
  (6 other events, 33.7 us)

commit v3 on v2

--- a/solution.py
+++ b/solution.py
@@ -7,6 +7,7 @@
 from jax.experimental.pallas import tpu as pltpu
 from jax.sharding import PartitionSpec as P
 
+
 f32, bf16, i32 = jnp.float32, jnp.bfloat16, jnp.int32
 VMEM = pl.BlockSpec(memory_space=pltpu.VMEM)
 SUB, LANE = 8, 128
@@ -17,7 +18,7 @@
     return pltpu.CompilerParams(vmem_limit_bytes=16 << 20)
 
 
-def run(body, outs, args, name, cost=(0, 0), scratch=()):
+def run(body, outs, args, cost=(0, 0), scratch=()):
     return pl.pallas_call(
         body,
         out_shape=[jax.ShapeDtypeStruct(shape, dtype) for shape, dtype in outs],
@@ -26,7 +27,6 @@
         scratch_shapes=list(scratch),
         compiler_params=params(),
         cost_estimate=pl.CostEstimate(flops=cost[0], bytes_accessed=cost[1], transcendentals=0),
-        name=name,
     )(*args)
 
 
@@ -98,29 +98,35 @@
     return jnp.where(wanted == subs((LANE, LANE)), 1.0, 0.0).astype(f32).T[:rows]
 
 
-def first_body(sends_ref, vector_ref, hot_ref, *rest):
+def first_body(face, order, place_ref, sends_ref, vector_ref, hot_ref, *rest):
     out_refs, row_ref = rest[:-1], rest[-1]
     row_ref[...] = jnp.full((SUB, LANE), -1, i32)
-    row_ref[0:1, 0 : sends_ref.shape[1]] = sends_ref[...]
+    even = place_ref[0:1, 0:face] == 0
+    for to, (source, odd_source) in enumerate(order):
+        taken = sends_ref[:, source * face : (source + 1) * face]
+        if odd_source != source:
+            taken = jnp.where(even, taken, sends_ref[:, odd_source * face : (odd_source + 1) * face])
+        row_ref[0:1, to * face : (to + 1) * face] = taken
     hot = one_hot(row_ref[0:1, :], hot_ref.shape[0])[:, : hot_ref.shape[1]].astype(bf16)
     hot_ref[...] = hot
     write_pieces(take_rows(hot, vector_ref[...]), out_refs)
 
 
-def prepare(face, swap, columns_ref, couplings_ref, shifts_ref, place_ref, row_ref, hot_ref, wide_ref, shift_ref):
+def prepare(face, moves, columns_ref, couplings_ref, shifts_ref, place_ref, row_ref, hot_ref, wide_ref, shift_ref):
     neighbours, own_rows = columns_ref.shape
     row_ref[...] = jnp.full((SUB, LANE), -1, i32)
     row_ref[0:neighbours, 0:own_rows] = columns_ref[...]
     columns = row_ref[...]
-    if swap:
-        place = jnp.broadcast_to(place_ref[...], (SUB, LANE))
-        lower = (columns >= own_rows) & (columns < own_rows + face)
-        upper = (columns >= own_rows + face) & (columns < own_rows + 2 * face)
-        columns = jnp.where(
-            lower,
-            jnp.where(place == 1, columns + face, -1),
-            jnp.where(upper, jnp.where(place == 0, columns - face, -1), columns),
-        )
+    even = jnp.broadcast_to(place_ref[...], (SUB, LANE)) == 0
+    moved = columns
+    for source, targets in enumerate(moves):
+        if targets == (source, source):
+            continue
+        first = own_rows + source * face
+        to = [-1 if target is None else columns + (target - source) * face for target in targets]
+        inside = (columns >= first) & (columns < first + face)
+        moved = jnp.where(inside, jnp.where(even, to[0], to[1]), moved)
+    columns = moved
     for k in range(neighbours):
         hot = one_hot(columns[k : k + 1, :], own_rows).astype(bf16)
         hot_ref[k * own_rows : (k + 1) * own_rows, 0:LANE] = hot
@@ -197,10 +203,10 @@
     return packet
 
 
-def setup_body(face, swap, *refs):
+def setup_body(face, moves, *refs):
     columns_ref, couplings_ref, shifts_ref, place_ref, blocks_ref, vector_ref = refs[:6]
     own_ref, hot_ref, wide_ref, shift_ref, row_ref = refs[6:]
-    prepare(face, swap, columns_ref, couplings_ref, shifts_ref, place_ref, row_ref, hot_ref, wide_ref, shift_ref)
+    prepare(face, moves, columns_ref, couplings_ref, shifts_ref, place_ref, row_ref, hot_ref, wide_ref, shift_ref)
     matvec(blocks_ref, vector_ref, own_ref)
 
 
@@ -218,20 +224,19 @@
     packet_ref[...] = packet
 
 
-def next_body(k, starts, last, *refs):
+def next_body(k, places, last, *refs):
     own_ref, vector_ref, hot_ref, wide_ref, shift_ref = refs[:5]
     refs = refs[5:]
     if not last:
         send_ref, refs = refs[0], refs[1:]
-    halo_refs, refs = refs[: len(starts)], refs[len(starts) :]
+    halo_refs, refs = refs[: len(places)], refs[len(places) :]
     next_ref, refs = refs[0], refs[1:]
     out_refs, extended_ref = refs[:-1], refs[-1]
     rows = vector_ref.shape[0]
     extended_ref[0:rows, :] = vector_ref[...]
-    end = rows
-    for start, ref in zip(starts, halo_refs):
-        extended_ref[start : start + ref.shape[0], :] = ref[...]
-        end += ref.shape[0]
+    for (first, count, to), ref in zip(places, halo_refs):
+        extended_ref[to : to + count, :] = ref[first : first + count, :]
+    end = rows + sum(count for _, count, _ in places)
     if end < LANE:
         extended_ref[end:LANE, :] = jnp.zeros((LANE - end, LANE), f32)
     parts = jnp.concatenate(two_parts(extended_ref[...]), axis=0)
@@ -290,7 +295,7 @@
     return result
 
 
-def laid_out(entries, n, by_row=True):
+def laid_out(entries, n):
     lane, sub = lanes(), subs()
     rows = jnp.zeros((SUB, LANE), f32)
     for i in range(n):
@@ -361,6 +366,10 @@
     sketch_factor_ref[...] = laid_out(sketch_upper, n)[:n, :n]
 
 
+def with_relay(col, levels):
+    return col == 2 and levels >= 2
+
+
 def shards(diag_blocks, couplings, columns, send_rows, shifts, start_vector, sketch):
     dom, col = lax.axis_size("dom"), lax.axis_size("col")
     levels = dom.bit_length() - 1
@@ -371,74 +380,94 @@
     powers = shifts.shape[0]
     n = powers + 1
     sketches = sketch.shape[0]
-    swap = col == 2
     blocks = diag_blocks.reshape(rows * width, width)
-    pieces = [2 * face] if swap else [face, face]
-    pieces = pieces + [face] * levels
-    piece_outs = [((size, width), f32) for size in pieces]
-    starts = [rows + (2 + level) * face for level in reversed(range(levels))] + ([rows] if swap else [rows, rows + face])
-    send_pad = -(-sends // 16) * 16
-
-    def exchange(outgoing):
-        side, far = list(outgoing[:-levels]), list(outgoing[-levels:])
-        for level in reversed(range(levels)):
-            far[level] = lax.ppermute(far[level], "dom", [(i, i ^ (1 << level)) for i in range(dom)])
-        if swap:
-            side = [lax.ppermute(side[0], "col", [(0, 1), (1, 0)])]
-        else:
-            up = [(i, i + 1) for i in range(col - 1)]
-            down = [(j, i) for i, j in up]
-            side = [lax.ppermute(side[1], "col", up), lax.ppermute(side[0], "col", down)]
-        return far[::-1] + side
-
+    relay = with_relay(col, levels)
+
+    near, far = 2 + levels - 2, 2 + levels - 1
+    direct = list(range(2, near)) if relay else list(range(2, 2 + levels))
+    if relay:
+        sizes = [3, 2] + [1] * len(direct)
+        order = [(0, 0), (1, 1), (far, near), (near, far), (near, far)] + [(x, x) for x in direct]
+        count = 2 + len(direct)
+        moves = [(None, 1), (0, None)] + [(x, x) for x in direct] + [(count, count + 1), (count + 1, count)]
+        places = [(0, face, rows + x * face) for x in direct]
+        places += [(0, 2 * face, rows), (0, face, rows + count * face), (face, face, rows + (count + 1) * face)]
+    else:
+        sizes = [1] * (2 + levels)
+        order = [(x, x) for x in range(2 + levels)]
+        moves = order
+        places = [(0, face, rows + x * face) for x in direct[::-1] + [0, 1]]
+    piece_outs = [((size * face, width), f32) for size in sizes]
+    send_pad = -(-len(order) * face // 16) * 16
+
+    def with_partner(piece, level):
+        return lax.ppermute(piece, "dom", [(i, i ^ (1 << level)) for i in range(dom)])
+
+    def exchange_relay(outgoing, k):
+        side, pair, *rest = outgoing
+        swapped = [(0, 1), (1, 0)]
+        side = lax.ppermute(side, "col", swapped)
+        received = []
+        for x, piece in zip(direct, rest):
+            received.append(with_partner(piece, x - 2))
+        pair = lax.dynamic_update_slice(pair, side[2 * face :], (face, 0))
+        far_pairs = [
+            (i * 2 + c, (i ^ (1 << (near - 2 + c))) * 2 + c) for i in range(dom) for c in range(2)
+        ]
+        pair = lax.ppermute(pair, ("dom", "col"), far_pairs)
+        relayed = lax.ppermute(pair, "col", swapped)
+        return received + [side, pair, relayed]
+
+    def exchange_direct(outgoing, k):
+        up = [(i, i + 1) for i in range(col - 1)]
+        received = [with_partner(outgoing[x], x - 2) for x in direct[::-1]]
+        lower = lax.ppermute(outgoing[1], "col", up)
+        return received + [lower, lax.ppermute(outgoing[0], "col", [(j, i) for i, j in up])]
+
+    exchange = exchange_relay if relay else exchange_direct
+
+    place = jnp.full((1, LANE), lax.axis_index("col"), i32)
     send_hot, *outgoing = run(
-        first_body,
+        functools.partial(first_body, face, order),
         [((send_pad, rows), bf16)] + piece_outs,
-        (send_rows, start_vector),
-        "first",
+        (place, send_rows, start_vector),
         cost=(100_000_000_000, 1_000_000_000),
         scratch=[pltpu.VMEM((SUB, LANE), i32)],
     )
     vectors = [start_vector]
-    place = jnp.full((1, LANE), lax.axis_index("col"), i32)
-    received = exchange(outgoing)
-    own, neighbour_hot, wide, shift = run(
-        functools.partial(setup_body, face, swap),
-        [
-            ((rows, width), f32),
-            ((neighbours * rows, 2 * LANE), bf16),
-            ((neighbours, rows, width), f32),
-            ((powers, SUB, LANE), f32),
-        ],
-        (columns.T, couplings.transpose(1, 0, 2), shifts.reshape(1, powers), place, blocks, start_vector),
-        "setup",
-        cost=(20_000_000, 4_000_000),
-        scratch=[pltpu.VMEM((SUB, LANE), i32)],
-    )
     packet = ()
     for k in range(powers):
-        if k:
-            received = exchange(outgoing)
+        final = k + 1 == powers
+        received = exchange(outgoing, k)
+        if k == 0:
+            own, neighbour_hot, wide, shift = run(
+                functools.partial(setup_body, face, moves),
+                [
+                    ((rows, width), f32),
+                    ((neighbours * rows, 2 * LANE), bf16),
+                    ((neighbours, rows, width), f32),
+                    ((powers, SUB, LANE), f32),
+                ],
+                (columns.T, couplings.transpose(1, 0, 2), shifts.reshape(1, powers), place, blocks, start_vector),
+                cost=(20_000_000, 4_000_000),
+                scratch=[pltpu.VMEM((SUB, LANE), i32)],
+            )
+        else:
             *packet, own = run(
                 functools.partial(middle_body, k, False),
                 [((SUB, LANE), f32), ((rows, width), f32)],
                 (*vectors, sketch, *packet, blocks),
-                f"middle_{k}",
                 cost=(20_000_000, 4_000_000),
             )
-        final = k + 1 == powers
         vector, *outgoing = run(
-            functools.partial(next_body, k, starts, final),
+            functools.partial(next_body, k, places, final),
             [((rows, width), f32)] + ([] if final else piece_outs),
             (own, vectors[-1], neighbour_hot, wide, shift, *(() if final else (send_hot,)), *received),
-            f"next_{k}",
             cost=(1_000_000, 1_000_000),
             scratch=[pltpu.VMEM((LANE, LANE), f32)],
         )
         vectors.append(vector)
-    (packet,) = run(
-        functools.partial(middle_body, powers, True), [((SUB, LANE), f32)], (*vectors, sketch, *packet), "middle_last"
-    )
+    (packet,) = run(functools.partial(middle_body, powers, True), [((SUB, LANE), f32)], (*vectors, sketch, *packet))
 
     everyone = ("dom", "col")
     packets = lax.all_to_all(jnp.tile(packet, (dom * col, 1)), everyone, 0, 0, tiled=True)
@@ -446,7 +475,6 @@
         functools.partial(last_body, n, sketches, float(rows * width * dom * col)),
         [((n, rows, width), f32), ((n, n), f32), ((n, n), f32)],
         (packets, *vectors),
-        "last",
         cost=(5_000_000, 1_000_000),
     )
     return orthonormal, factor, sketch_factor

time: 65.1 us -> 78.9 us (1.21)
  waiting for transfers between devices: 4.91 us -> 23.4 us
  starting transfers between devices: 32.1 us -> 27.5 us
    ppermute x30, waiting for transfers between devices: 4.91 us -> 23.4 us  [the longest x6 11.5 us: exchange_relay(): pair = lax.ppermute(pair, ('dom', 'col'), far_pairs)]
    ppermute x30, starting transfers between devices: 32.1 us -> 27.5 us  [the longest x12 15.6 us: with_partner(): return lax.ppermute(piece, 'dom', [(i, i ^ 1 << level) for i in range(dom)])]
  transfers between devices with their start and end apart: 30 -> 30, of which waited for: 9 -> 21; matrix products, arithmetic and copies ran while one was open for 0% -> 0% of each run, Pallas kernels for 10% -> 9%
where the time goes in v3:
time: 78.9 us; the launch traced here: 78.7 us
  starting transfers between devices  27.5 us (35%)
  waiting for transfers between devices  23.4 us (30%)
  blocking collectives  14 us (18%)
  Pallas kernels  11.6 us (15%)
  local copies, waits for them, and re-layouts  1.53 us (2%)
    ppermute x12, starting transfers between devices, with_partner(): return lax.ppermute(piece, 'dom', [(i, i ^ 1 << level) for i in range(dom)])  15.6 us
    all_to_all x1, blocking collectives, shards(): lax.all_to_all(jnp.tile(packet, (dom * col, 1)), everyone, 0, 0, tiled=True)  14 us
    pallas_call x15, Pallas kernels, run(): pl.pallas_call(body, out_shape=[jax.ShapeDtypeStruct(shape, dtype) for sh...  11.6 us
    ppermute x6, waiting for transfers between devices, exchange_relay(): pair = lax.ppermute(pair, ('dom', 'col'), far_pairs)  11.5 us
    ppermute x6, starting transfers between devices, exchange_relay(): pair = lax.ppermute(pair, ('dom', 'col'), far_pairs)  11 us
    ppermute x6, waiting for transfers between devices, exchange_relay(): side = lax.ppermute(side, 'col', swapped)  6.74 us
    ppermute x12, waiting for transfers between devices, with_partner(): return lax.ppermute(piece, 'dom', [(i, i ^ 1 << level) for i in range(dom)])  5.12 us
  transfers between devices with their start and end apart: 30, of which 21 were waited for; matrix products, arithmetic and copies ran while one was open for 0% of the time, Pallas kernels for 9%

profile of v3, /device:TPU:0, one launch (start us, length us, event | category | flops | bytes accessed | tf_op | source)
XLA Modules:
  0.0 78.7 jit_solution(401461546157344640)
XLA Ops:
  3.8 2.9 %collective-permute-start.3 = (f32[8,128]{1,0:T(8,128)S(1)}, f32[8,128]{1,0:T(8,128)S(1)}, u32[]{:S(2)}, u32[]{:S(2)}) collective-permute-start(f32[8,128]{1,0:T(8,128)S(1)} %slice_dynamic-update-slice_fusion.5), channel_id=1, source_target_pairs={{0,8},{1,17},{2,10},{3,19},{4,12},{5,21},{6,14},{7,23},{8,0},{9,25... | collective-permute-start | bytes 12296 | tf_op jit(solution)/shard_map/ppermute | solution.py:417
  6.7 1.6 %collective-permute-done.3.refs_9_ = f32[8,128]{1,0:T(8,128)S(1)} collective-permute-done((f32[8,128]{1,0:T(8,128)S(1)}, f32[8,128]{1,0:T(8,128)S(1)}, u32[]{:S(2)}, u32[]{:S(2)}) %collective-permute-start.3) | collective-permute-done | bytes 4128 | tf_op jit(solution)/shard_map/ppermute | solution.py:417
  8.6 1.6 %collective-permute-start = (f32[4,128]{1,0:T(4,128)S(1)}, f32[4,128]{1,0:T(4,128)S(1)}, u32[]{:S(2)}, u32[]{:S(2)}) collective-permute-start(f32[4,128]{1,0:T(4,128)S(1)} %get-tuple-element.52), channel_id=1, source_target_pairs={{0,2},{2,0},{4,6},{6,4},{8,10},{10,8},{12,14},{14,12},{16,18},{18,... | collective-permute-start | bytes 6152 | tf_op jit(solution)/shard_map/ppermute | solution.py:404
  10.2 1.5 %collective-permute-start.1 = (f32[4,128]{1,0:T(4,128)S(1)}, f32[4,128]{1,0:T(4,128)S(1)}, u32[]{:S(2)}, u32[]{:S(2)}) collective-permute-start(f32[4,128]{1,0:T(4,128)S(1)} %get-tuple-element.53), channel_id=1, source_target_pairs={{0,4},{2,6},{4,0},{6,2},{8,12},{10,14},{12,8},{14,10},{16,20},{18,... | collective-permute-start | bytes 6152 | tf_op jit(solution)/shard_map/ppermute | solution.py:404
  14.2 1.2 %collective-permute-done.7.refs_8_ = f32[12,128]{1,0:T(8,128)S(1)} collective-permute-done((f32[12,128]{1,0:T(8,128)S(1)}, f32[12,128]{1,0:T(8,128)S(1)}, u32[]{:S(2)}, u32[]{:S(2)}) %collective-permute-start.7) | collective-permute-done | bytes 6176 | tf_op jit(solution)/shard_map/ppermute | solution.py:409
  15.4 1.6 %collective-permute-start.8 = (f32[8,128]{1,0:T(8,128)S(1)}, f32[8,128]{1,0:T(8,128)S(1)}, u32[]{:S(2)}, u32[]{:S(2)}) collective-permute-start(f32[8,128]{1,0:T(8,128)S(1)} %slice_dynamic-update-slice_fusion.4), channel_id=1, source_target_pairs={{0,8},{1,17},{2,10},{3,19},{4,12},{5,21},{6,14},{7,23},{8,0},{9,25... | collective-permute-start | bytes 12296 | tf_op jit(solution)/shard_map/ppermute | solution.py:417
  17.0 2.0 %collective-permute-done.8.refs_9_ = f32[8,128]{1,0:T(8,128)S(1)} collective-permute-done((f32[8,128]{1,0:T(8,128)S(1)}, f32[8,128]{1,0:T(8,128)S(1)}, u32[]{:S(2)}, u32[]{:S(2)}) %collective-permute-start.8) | collective-permute-done | bytes 4128 | tf_op jit(solution)/shard_map/ppermute | solution.py:417
  19.4 1.7 %collective-permute-start.6 = (f32[4,128]{1,0:T(4,128)S(1)}, f32[4,128]{1,0:T(4,128)S(1)}, u32[]{:S(2)}, u32[]{:S(2)}) collective-permute-start(f32[4,128]{1,0:T(4,128)S(1)} %get-tuple-element.59), channel_id=1, source_target_pairs={{0,4},{2,6},{4,0},{6,2},{8,12},{10,14},{12,8},{14,10},{16,20},{18,... | collective-permute-start | bytes 6152 | tf_op jit(solution)/shard_map/ppermute | solution.py:404
  21.1 1.3 %shard_map.97 = (f32[8,128]{1,0:T(8,128)S(1)}, f32[96,128]{1,0:T(8,128)S(1)}) custom-call(f32[96,128]{1,0:T(8,128)S(1)} %copy-done.3, f32[96,128]{1,0:T(8,128)S(1)} %get-tuple-element.56.refs_1_, bf16[32,96,128]{2,1,0:T(8,128)(2,1)S(1)} %copy-done.1, bf16[12288,128]{1,0:T(8,128)(2,1)S(1)} %bitcast.6), custom_call_target="tpu_custom_call" | custom-call | flops 20000000 | bytes 4000000 | tf_op jit(solution)/shard_map/pallas_call | solution.py:22
  23.4 1.2 %collective-permute-done.12.refs_8_ = f32[12,128]{1,0:T(8,128)S(1)} collective-permute-done((f32[12,128]{1,0:T(8,128)S(1)}, f32[12,128]{1,0:T(8,128)S(1)}, u32[]{:S(2)}, u32[]{:S(2)}) %collective-permute-start.12) | collective-permute-done | bytes 6176 | tf_op jit(solution)/shard_map/ppermute | solution.py:409
  24.6 1.7 %collective-permute-start.13 = (f32[8,128]{1,0:T(8,128)S(1)}, f32[8,128]{1,0:T(8,128)S(1)}, u32[]{:S(2)}, u32[]{:S(2)}) collective-permute-start(f32[8,128]{1,0:T(8,128)S(1)} %slice_dynamic-update-slice_fusion.3), channel_id=1, source_target_pairs={{0,8},{1,17},{2,10},{3,19},{4,12},{5,21},{6,14},{7,23},{8,0},{9,25... | collective-permute-start | bytes 12296 | tf_op jit(solution)/shard_map/ppermute | solution.py:417
  26.3 1.9 %collective-permute-done.13.refs_9_ = f32[8,128]{1,0:T(8,128)S(1)} collective-permute-done((f32[8,128]{1,0:T(8,128)S(1)}, f32[8,128]{1,0:T(8,128)S(1)}, u32[]{:S(2)}, u32[]{:S(2)}) %collective-permute-start.13) | collective-permute-done | bytes 4128 | tf_op jit(solution)/shard_map/ppermute | solution.py:417
  28.2 1.6 %collective-permute-start.10 = (f32[4,128]{1,0:T(4,128)S(1)}, f32[4,128]{1,0:T(4,128)S(1)}, u32[]{:S(2)}, u32[]{:S(2)}) collective-permute-start(f32[4,128]{1,0:T(4,128)S(1)} %get-tuple-element.65), channel_id=1, source_target_pairs={{0,2},{2,0},{4,6},{6,4},{8,10},{10,8},{12,14},{14,12},{16,18},{18,... | collective-permute-start | bytes 6152 | tf_op jit(solution)/shard_map/ppermute | solution.py:404
  29.9 1.5 %collective-permute-start.11 = (f32[4,128]{1,0:T(4,128)S(1)}, f32[4,128]{1,0:T(4,128)S(1)}, u32[]{:S(2)}, u32[]{:S(2)}) collective-permute-start(f32[4,128]{1,0:T(4,128)S(1)} %get-tuple-element.66), channel_id=1, source_target_pairs={{0,4},{2,6},{4,0},{6,2},{8,12},{10,14},{12,8},{14,10},{16,20},{18,... | collective-permute-start | bytes 6152 | tf_op jit(solution)/shard_map/ppermute | solution.py:404
  33.9 1.2 %collective-permute-done.17.refs_8_ = f32[12,128]{1,0:T(8,128)S(1)} collective-permute-done((f32[12,128]{1,0:T(8,128)S(1)}, f32[12,128]{1,0:T(8,128)S(1)}, u32[]{:S(2)}, u32[]{:S(2)}) %collective-permute-start.17) | collective-permute-done | bytes 6176 | tf_op jit(solution)/shard_map/ppermute | solution.py:409
  35.1 1.6 %collective-permute-start.18 = (f32[8,128]{1,0:T(8,128)S(1)}, f32[8,128]{1,0:T(8,128)S(1)}, u32[]{:S(2)}, u32[]{:S(2)}) collective-permute-start(f32[8,128]{1,0:T(8,128)S(1)} %slice_dynamic-update-slice_fusion.2), channel_id=1, source_target_pairs={{0,8},{1,17},{2,10},{3,19},{4,12},{5,21},{6,14},{7,23},{8,0},{9,25... | collective-permute-start | bytes 12296 | tf_op jit(solution)/shard_map/ppermute | solution.py:417
  36.6 2.0 %collective-permute-done.18.refs_9_ = f32[8,128]{1,0:T(8,128)S(1)} collective-permute-done((f32[8,128]{1,0:T(8,128)S(1)}, f32[8,128]{1,0:T(8,128)S(1)}, u32[]{:S(2)}, u32[]{:S(2)}) %collective-permute-start.18) | collective-permute-done | bytes 4128 | tf_op jit(solution)/shard_map/ppermute | solution.py:417
  39.1 1.6 %collective-permute-start.16 = (f32[4,128]{1,0:T(4,128)S(1)}, f32[4,128]{1,0:T(4,128)S(1)}, u32[]{:S(2)}, u32[]{:S(2)}) collective-permute-start(f32[4,128]{1,0:T(4,128)S(1)} %get-tuple-element.73), channel_id=1, source_target_pairs={{0,4},{2,6},{4,0},{6,2},{8,12},{10,14},{12,8},{14,10},{16,20},{18,... | collective-permute-start | bytes 6152 | tf_op jit(solution)/shard_map/ppermute | solution.py:404
  40.7 1.1 %shard_map.101 = (f32[8,128]{1,0:T(8,128)S(1)}, f32[96,128]{1,0:T(8,128)S(1)}) custom-call(f32[96,128]{1,0:T(8,128)S(1)} %copy-done.3, f32[96,128]{1,0:T(8,128)S(1)} %get-tuple-element.56.refs_1_, f32[96,128]{1,0:T(8,128)S(1)} %get-tuple-element.62.refs_2_.refs_1_, f32[96,128]{1,0:T(8,128)S(1)} %get-tuple-element.69.refs_3_.refs_1_, ...), custom_call_target="tpu_custom_call" | custom-call | flops 20000000 | bytes 4000000 | tf_op jit(solution)/shard_map/pallas_call | solution.py:22
  43.1 1.2 %collective-permute-done.22.refs_8_ = f32[12,128]{1,0:T(8,128)S(1)} collective-permute-done((f32[12,128]{1,0:T(8,128)S(1)}, f32[12,128]{1,0:T(8,128)S(1)}, u32[]{:S(2)}, u32[]{:S(2)}) %collective-permute-start.22) | collective-permute-done | bytes 6176 | tf_op jit(solution)/shard_map/ppermute | solution.py:409
  44.2 1.7 %collective-permute-start.23 = (f32[8,128]{1,0:T(8,128)S(1)}, f32[8,128]{1,0:T(8,128)S(1)}, u32[]{:S(2)}, u32[]{:S(2)}) collective-permute-start(f32[8,128]{1,0:T(8,128)S(1)} %slice_dynamic-update-slice_fusion.1), channel_id=1, source_target_pairs={{0,8},{1,17},{2,10},{3,19},{4,12},{5,21},{6,14},{7,23},{8,0},{9,25... | collective-permute-start | bytes 12296 | tf_op jit(solution)/shard_map/ppermute | solution.py:417
  45.9 1.9 %collective-permute-done.23.refs_9_ = f32[8,128]{1,0:T(8,128)S(1)} collective-permute-done((f32[8,128]{1,0:T(8,128)S(1)}, f32[8,128]{1,0:T(8,128)S(1)}, u32[]{:S(2)}, u32[]{:S(2)}) %collective-permute-start.23) | collective-permute-done | bytes 4128 | tf_op jit(solution)/shard_map/ppermute | solution.py:417
  47.9 1.6 %collective-permute-start.20 = (f32[4,128]{1,0:T(4,128)S(1)}, f32[4,128]{1,0:T(4,128)S(1)}, u32[]{:S(2)}, u32[]{:S(2)}) collective-permute-start(f32[4,128]{1,0:T(4,128)S(1)} %get-tuple-element.79), channel_id=1, source_target_pairs={{0,2},{2,0},{4,6},{6,4},{8,10},{10,8},{12,14},{14,12},{16,18},{18,... | collective-permute-start | bytes 6152 | tf_op jit(solution)/shard_map/ppermute | solution.py:404
  49.5 1.5 %collective-permute-start.21 = (f32[4,128]{1,0:T(4,128)S(1)}, f32[4,128]{1,0:T(4,128)S(1)}, u32[]{:S(2)}, u32[]{:S(2)}) collective-permute-start(f32[4,128]{1,0:T(4,128)S(1)} %get-tuple-element.80), channel_id=1, source_target_pairs={{0,4},{2,6},{4,0},{6,2},{8,12},{10,14},{12,8},{14,10},{16,20},{18,... | collective-permute-start | bytes 6152 | tf_op jit(solution)/shard_map/ppermute | solution.py:404
  51.0 1.2 %shard_map.103 = (f32[8,128]{1,0:T(8,128)S(1)}, f32[96,128]{1,0:T(8,128)S(1)}) custom-call(f32[96,128]{1,0:T(8,128)S(1)} %copy-done.3, f32[96,128]{1,0:T(8,128)S(1)} %get-tuple-element.56.refs_1_, f32[96,128]{1,0:T(8,128)S(1)} %get-tuple-element.62.refs_2_.refs_1_, f32[96,128]{1,0:T(8,128)S(1)} %get-tuple-element.69.refs_3_.refs_1_, ...), custom_call_target="tpu_custom_call" | custom-call | flops 20000000 | bytes 4000000 | tf_op jit(solution)/shard_map/pallas_call | solution.py:22
  53.5 1.2 %collective-permute-done.27.refs_7_ = f32[12,128]{1,0:T(8,128)S(1)} collective-permute-done((f32[12,128]{1,0:T(8,128)S(1)}, f32[12,128]{1,0:T(8,128)S(1)}, u32[]{:S(2)}, u32[]{:S(2)}) %collective-permute-start.27) | collective-permute-done | bytes 6176 | tf_op jit(solution)/shard_map/ppermute | solution.py:409
  54.7 1.6 %collective-permute-start.28 = (f32[8,128]{1,0:T(8,128)S(1)}, f32[8,128]{1,0:T(8,128)S(1)}, u32[]{:S(2)}, u32[]{:S(2)}) collective-permute-start(f32[8,128]{1,0:T(8,128)S(1)} %slice_dynamic-update-slice_fusion), channel_id=1, source_target_pairs={{0,8},{1,17},{2,10},{3,19},{4,12},{5,21},{6,14},{7,23},{8,0},{9,25... | collective-permute-start | bytes 12296 | tf_op jit(solution)/shard_map/ppermute | solution.py:417
  56.2 2.0 %collective-permute-done.28.refs_8_ = f32[8,128]{1,0:T(8,128)S(1)} collective-permute-done((f32[8,128]{1,0:T(8,128)S(1)}, f32[8,128]{1,0:T(8,128)S(1)}, u32[]{:S(2)}, u32[]{:S(2)}) %collective-permute-start.28) | collective-permute-done | bytes 4128 | tf_op jit(solution)/shard_map/ppermute | solution.py:417
  58.7 1.7 %collective-permute-start.26 = (f32[4,128]{1,0:T(4,128)S(1)}, f32[4,128]{1,0:T(4,128)S(1)}, u32[]{:S(2)}, u32[]{:S(2)}) collective-permute-start(f32[4,128]{1,0:T(4,128)S(1)} %get-tuple-element.87), channel_id=1, source_target_pairs={{0,4},{2,6},{4,0},{6,2},{8,12},{10,14},{12,8},{14,10},{16,20},{18,... | collective-permute-start | bytes 6152 | tf_op jit(solution)/shard_map/ppermute | solution.py:404
  60.3 1.2 %shard_map.105 = (f32[8,128]{1,0:T(8,128)S(1)}, f32[96,128]{1,0:T(8,128)S(1)}) custom-call(f32[96,128]{1,0:T(8,128)S(1)} %copy-done.3, f32[96,128]{1,0:T(8,128)S(1)} %get-tuple-element.56.refs_1_, f32[96,128]{1,0:T(8,128)S(1)} %get-tuple-element.62.refs_2_.refs_1_, f32[96,128]{1,0:T(8,128)S(1)} %get-tuple-element.69.refs_3_.refs_1_, ...), custom_call_target="tpu_custom_call" | custom-call | flops 20000000 | bytes 4000000 | tf_op jit(solution)/shard_map/pallas_call | solution.py:22
  63.3 14.0 %all_to_all.8 = f32[32,8,128]{2,1,0:T(8,128)S(1)} all-to-all(f32[32,8,128]{2,1,0:T(8,128)S(1)} %tile.2), channel_id=1, replica_groups=mesh['dom'=16,'col'=2] {'dom','col'}, dimensions={0} | all-to-all | bytes 262144 | tf_op jit(solution)/shard_map/all_to_all | solution.py:473
  77.3 1.4 %shard_map.108 = (f32[7,96,128]{2,1,0:T(8,128)}, f32[7,7]{1,0:T(8,128)}, f32[7,7]{1,0:T(8,128)}) custom-call(f32[256,128]{1,0:T(8,128)S(1)} %bitcast.11, f32[96,128]{1,0:T(8,128)S(1)} %copy-done.3, f32[96,128]{1,0:T(8,128)S(1)} %get-tuple-element.56.refs_1_, f32[96,128]{1,0:T(8,128)S(1)} %get-tuple-element.62.refs_2_.refs_1_, ...), custom_call_target="tpu_custom_call" | custom-call | flops 5000000 | bytes 1000000 | tf_op jit(solution)/shard_map/pallas_call | solution.py:22
  (68 shorter events, 14.9 us)
Async XLA Ops:
  2.1 9.7 %copy-start.6 = (f32[6]{0:T(128)S(1)}, f32[6]{0:T(128)}, u32[]{:S(2)}) copy-start(f32[6]{0:T(128)} %param.11) | copy-start | bytes 76
  2.5 18.6 %copy-start.1 = (bf16[32,96,128]{2,1,0:T(8,128)(2,1)S(1)}, bf16[32,96,128]{2,1,0:T(8,128)(2,1)}, u32[]{:S(2)}) copy-start(bf16[32,96,128]{2,1,0:T(8,128)(2,1)} %refs_7_.1) | copy-start | bytes 2359300
  2.5 1.3 %collective-permute-start.2 = (f32[12,128]{1,0:T(8,128)S(1)}, f32[12,128]{1,0:T(8,128)S(1)}, u32[]{:S(2)}, u32[]{:S(2)}) collective-permute-start(f32[12,128]{1,0:T(8,128)S(1)} %get-tuple-element.54), channel_id=1, source_target_pairs={{0,1},{1,0},{2,3},{3,2},{4,5},{5,4},{6,7},{7,6},{8,9},{9,8},{10,11... | collective-permute-start | bytes 18440 | tf_op jit(solution)/shard_map/ppermute | solution.py:409
  3.8 4.5 %collective-permute-start.3 = (f32[8,128]{1,0:T(8,128)S(1)}, f32[8,128]{1,0:T(8,128)S(1)}, u32[]{:S(2)}, u32[]{:S(2)}) collective-permute-start(f32[8,128]{1,0:T(8,128)S(1)} %slice_dynamic-update-slice_fusion.5), channel_id=1, source_target_pairs={{0,8},{1,17},{2,10},{3,19},{4,12},{5,21},{6,14},{7,23},{8,0},{9,25... | collective-permute-start | bytes 12296 | tf_op jit(solution)/shard_map/ppermute | solution.py:417
  8.3 5.5 %collective-permute-start.4 = (f32[8,128]{1,0:T(8,128)S(1)}, f32[8,128]{1,0:T(8,128)S(1)}, u32[]{:S(2)}, u32[]{:S(2)}) collective-permute-start(f32[8,128]{1,0:T(8,128)S(1)} %collective-permute-done.3.refs_9_), channel_id=1, source_target_pairs={{0,1},{1,0},{2,3},{3,2},{4,5},{5,4},{6,7},{7,6},{8,9},{9,8},{10,11... | collective-permute-start | bytes 12296 | tf_op jit(solution)/shard_map/ppermute | solution.py:418
  8.6 4.1 %collective-permute-start = (f32[4,128]{1,0:T(4,128)S(1)}, f32[4,128]{1,0:T(4,128)S(1)}, u32[]{:S(2)}, u32[]{:S(2)}) collective-permute-start(f32[4,128]{1,0:T(4,128)S(1)} %get-tuple-element.52), channel_id=1, source_target_pairs={{0,2},{2,0},{4,6},{6,4},{8,10},{10,8},{12,14},{14,12},{16,18},{18,... | collective-permute-start | bytes 6152 | tf_op jit(solution)/shard_map/ppermute | solution.py:404
  10.2 3.6 %collective-permute-start.1 = (f32[4,128]{1,0:T(4,128)S(1)}, f32[4,128]{1,0:T(4,128)S(1)}, u32[]{:S(2)}, u32[]{:S(2)}) collective-permute-start(f32[4,128]{1,0:T(4,128)S(1)} %get-tuple-element.53), channel_id=1, source_target_pairs={{0,4},{2,6},{4,0},{6,2},{8,12},{10,14},{12,8},{14,10},{16,20},{18,... | collective-permute-start | bytes 6152 | tf_op jit(solution)/shard_map/ppermute | solution.py:404
  14.2 1.2 %collective-permute-start.7 = (f32[12,128]{1,0:T(8,128)S(1)}, f32[12,128]{1,0:T(8,128)S(1)}, u32[]{:S(2)}, u32[]{:S(2)}) collective-permute-start(f32[12,128]{1,0:T(8,128)S(1)} %get-tuple-element.60), channel_id=1, source_target_pairs={{0,1},{1,0},{2,3},{3,2},{4,5},{5,4},{6,7},{7,6},{8,9},{9,8},{10,11... | collective-permute-start | bytes 18440 | tf_op jit(solution)/shard_map/ppermute | solution.py:409
  15.4 3.6 %collective-permute-start.8 = (f32[8,128]{1,0:T(8,128)S(1)}, f32[8,128]{1,0:T(8,128)S(1)}, u32[]{:S(2)}, u32[]{:S(2)}) collective-permute-start(f32[8,128]{1,0:T(8,128)S(1)} %slice_dynamic-update-slice_fusion.4), channel_id=1, source_target_pairs={{0,8},{1,17},{2,10},{3,19},{4,12},{5,21},{6,14},{7,23},{8,0},{9,25... | collective-permute-start | bytes 12296 | tf_op jit(solution)/shard_map/ppermute | solution.py:417
  19.0 4.0 %collective-permute-start.9 = (f32[8,128]{1,0:T(8,128)S(1)}, f32[8,128]{1,0:T(8,128)S(1)}, u32[]{:S(2)}, u32[]{:S(2)}) collective-permute-start(f32[8,128]{1,0:T(8,128)S(1)} %collective-permute-done.8.refs_9_), channel_id=1, source_target_pairs={{0,1},{1,0},{2,3},{3,2},{4,5},{5,4},{6,7},{7,6},{8,9},{9,8},{10,11... | collective-permute-start | bytes 12296 | tf_op jit(solution)/shard_map/ppermute | solution.py:418
  19.0 3.6 %collective-permute-start.5 = (f32[4,128]{1,0:T(4,128)S(1)}, f32[4,128]{1,0:T(4,128)S(1)}, u32[]{:S(2)}, u32[]{:S(2)}) collective-permute-start(f32[4,128]{1,0:T(4,128)S(1)} %get-tuple-element.58), channel_id=1, source_target_pairs={{0,2},{2,0},{4,6},{6,4},{8,10},{10,8},{12,14},{14,12},{16,18},{18,... | collective-permute-start | bytes 6152 | tf_op jit(solution)/shard_map/ppermute | solution.py:404
  19.4 3.6 %collective-permute-start.6 = (f32[4,128]{1,0:T(4,128)S(1)}, f32[4,128]{1,0:T(4,128)S(1)}, u32[]{:S(2)}, u32[]{:S(2)}) collective-permute-start(f32[4,128]{1,0:T(4,128)S(1)} %get-tuple-element.59), channel_id=1, source_target_pairs={{0,4},{2,6},{4,0},{6,2},{8,12},{10,14},{12,8},{14,10},{16,20},{18,... | collective-permute-start | bytes 6152 | tf_op jit(solution)/shard_map/ppermute | solution.py:404
  23.4 1.2 %collective-permute-start.12 = (f32[12,128]{1,0:T(8,128)S(1)}, f32[12,128]{1,0:T(8,128)S(1)}, u32[]{:S(2)}, u32[]{:S(2)}) collective-permute-start(f32[12,128]{1,0:T(8,128)S(1)} %get-tuple-element.67), channel_id=1, source_target_pairs={{0,1},{1,0},{2,3},{3,2},{4,5},{5,4},{6,7},{7,6},{8,9},{9,8},{10,11... | collective-permute-start | bytes 18440 | tf_op jit(solution)/shard_map/ppermute | solution.py:409
  24.6 3.6 %collective-permute-start.13 = (f32[8,128]{1,0:T(8,128)S(1)}, f32[8,128]{1,0:T(8,128)S(1)}, u32[]{:S(2)}, u32[]{:S(2)}) collective-permute-start(f32[8,128]{1,0:T(8,128)S(1)} %slice_dynamic-update-slice_fusion.3), channel_id=1, source_target_pairs={{0,8},{1,17},{2,10},{3,19},{4,12},{5,21},{6,14},{7,23},{8,0},{9,25... | collective-permute-start | bytes 12296 | tf_op jit(solution)/shard_map/ppermute | solution.py:417
  28.2 5.2 %collective-permute-start.14 = (f32[8,128]{1,0:T(8,128)S(1)}, f32[8,128]{1,0:T(8,128)S(1)}, u32[]{:S(2)}, u32[]{:S(2)}) collective-permute-start(f32[8,128]{1,0:T(8,128)S(1)} %collective-permute-done.13.refs_9_), channel_id=1, source_target_pairs={{0,1},{1,0},{2,3},{3,2},{4,5},{5,4},{6,7},{7,6},{8,9},{9,8},{10,11... | collective-permute-start | bytes 12296 | tf_op jit(solution)/shard_map/ppermute | solution.py:418
  28.2 4.2 %collective-permute-start.10 = (f32[4,128]{1,0:T(4,128)S(1)}, f32[4,128]{1,0:T(4,128)S(1)}, u32[]{:S(2)}, u32[]{:S(2)}) collective-permute-start(f32[4,128]{1,0:T(4,128)S(1)} %get-tuple-element.65), channel_id=1, source_target_pairs={{0,2},{2,0},{4,6},{6,4},{8,10},{10,8},{12,14},{14,12},{16,18},{18,... | collective-permute-start | bytes 6152 | tf_op jit(solution)/shard_map/ppermute | solution.py:404
  29.9 3.6 %collective-permute-start.11 = (f32[4,128]{1,0:T(4,128)S(1)}, f32[4,128]{1,0:T(4,128)S(1)}, u32[]{:S(2)}, u32[]{:S(2)}) collective-permute-start(f32[4,128]{1,0:T(4,128)S(1)} %get-tuple-element.66), channel_id=1, source_target_pairs={{0,4},{2,6},{4,0},{6,2},{8,12},{10,14},{12,8},{14,10},{16,20},{18,... | collective-permute-start | bytes 6152 | tf_op jit(solution)/shard_map/ppermute | solution.py:404
  33.9 1.2 %collective-permute-start.17 = (f32[12,128]{1,0:T(8,128)S(1)}, f32[12,128]{1,0:T(8,128)S(1)}, u32[]{:S(2)}, u32[]{:S(2)}) collective-permute-start(f32[12,128]{1,0:T(8,128)S(1)} %get-tuple-element.74), channel_id=1, source_target_pairs={{0,1},{1,0},{2,3},{3,2},{4,5},{5,4},{6,7},{7,6},{8,9},{9,8},{10,11... | collective-permute-start | bytes 18440 | tf_op jit(solution)/shard_map/ppermute | solution.py:409
  35.1 3.6 %collective-permute-start.18 = (f32[8,128]{1,0:T(8,128)S(1)}, f32[8,128]{1,0:T(8,128)S(1)}, u32[]{:S(2)}, u32[]{:S(2)}) collective-permute-start(f32[8,128]{1,0:T(8,128)S(1)} %slice_dynamic-update-slice_fusion.2), channel_id=1, source_target_pairs={{0,8},{1,17},{2,10},{3,19},{4,12},{5,21},{6,14},{7,23},{8,0},{9,25... | collective-permute-start | bytes 12296 | tf_op jit(solution)/shard_map/ppermute | solution.py:417
  38.7 4.0 %collective-permute-start.19 = (f32[8,128]{1,0:T(8,128)S(1)}, f32[8,128]{1,0:T(8,128)S(1)}, u32[]{:S(2)}, u32[]{:S(2)}) collective-permute-start(f32[8,128]{1,0:T(8,128)S(1)} %collective-permute-done.18.refs_9_), channel_id=1, source_target_pairs={{0,1},{1,0},{2,3},{3,2},{4,5},{5,4},{6,7},{7,6},{8,9},{9,8},{10,11... | collective-permute-start | bytes 12296 | tf_op jit(solution)/shard_map/ppermute | solution.py:418
  38.7 3.6 %collective-permute-start.15 = (f32[4,128]{1,0:T(4,128)S(1)}, f32[4,128]{1,0:T(4,128)S(1)}, u32[]{:S(2)}, u32[]{:S(2)}) collective-permute-start(f32[4,128]{1,0:T(4,128)S(1)} %get-tuple-element.72), channel_id=1, source_target_pairs={{0,2},{2,0},{4,6},{6,4},{8,10},{10,8},{12,14},{14,12},{16,18},{18,... | collective-permute-start | bytes 6152 | tf_op jit(solution)/shard_map/ppermute | solution.py:404
  39.1 3.6 %collective-permute-start.16 = (f32[4,128]{1,0:T(4,128)S(1)}, f32[4,128]{1,0:T(4,128)S(1)}, u32[]{:S(2)}, u32[]{:S(2)}) collective-permute-start(f32[4,128]{1,0:T(4,128)S(1)} %get-tuple-element.73), channel_id=1, source_target_pairs={{0,4},{2,6},{4,0},{6,2},{8,12},{10,14},{12,8},{14,10},{16,20},{18,... | collective-permute-start | bytes 6152 | tf_op jit(solution)/shard_map/ppermute | solution.py:404
  43.1 1.2 %collective-permute-start.22 = (f32[12,128]{1,0:T(8,128)S(1)}, f32[12,128]{1,0:T(8,128)S(1)}, u32[]{:S(2)}, u32[]{:S(2)}) collective-permute-start(f32[12,128]{1,0:T(8,128)S(1)} %get-tuple-element.81), channel_id=1, source_target_pairs={{0,1},{1,0},{2,3},{3,2},{4,5},{5,4},{6,7},{7,6},{8,9},{9,8},{10,11... | collective-permute-start | bytes 18440 | tf_op jit(solution)/shard_map/ppermute | solution.py:409
  44.2 3.6 %collective-permute-start.23 = (f32[8,128]{1,0:T(8,128)S(1)}, f32[8,128]{1,0:T(8,128)S(1)}, u32[]{:S(2)}, u32[]{:S(2)}) collective-permute-start(f32[8,128]{1,0:T(8,128)S(1)} %slice_dynamic-update-slice_fusion.1), channel_id=1, source_target_pairs={{0,8},{1,17},{2,10},{3,19},{4,12},{5,21},{6,14},{7,23},{8,0},{9,25... | collective-permute-start | bytes 12296 | tf_op jit(solution)/shard_map/ppermute | solution.py:417
  47.9 5.2 %collective-permute-start.24 = (f32[8,128]{1,0:T(8,128)S(1)}, f32[8,128]{1,0:T(8,128)S(1)}, u32[]{:S(2)}, u32[]{:S(2)}) collective-permute-start(f32[8,128]{1,0:T(8,128)S(1)} %collective-permute-done.23.refs_9_), channel_id=1, source_target_pairs={{0,1},{1,0},{2,3},{3,2},{4,5},{5,4},{6,7},{7,6},{8,9},{9,8},{10,11... | collective-permute-start | bytes 12296 | tf_op jit(solution)/shard_map/ppermute | solution.py:418
  47.9 4.3 %collective-permute-start.20 = (f32[4,128]{1,0:T(4,128)S(1)}, f32[4,128]{1,0:T(4,128)S(1)}, u32[]{:S(2)}, u32[]{:S(2)}) collective-permute-start(f32[4,128]{1,0:T(4,128)S(1)} %get-tuple-element.79), channel_id=1, source_target_pairs={{0,2},{2,0},{4,6},{6,4},{8,10},{10,8},{12,14},{14,12},{16,18},{18,... | collective-permute-start | bytes 6152 | tf_op jit(solution)/shard_map/ppermute | solution.py:404
  49.5 3.6 %collective-permute-start.21 = (f32[4,128]{1,0:T(4,128)S(1)}, f32[4,128]{1,0:T(4,128)S(1)}, u32[]{:S(2)}, u32[]{:S(2)}) collective-permute-start(f32[4,128]{1,0:T(4,128)S(1)} %get-tuple-element.80), channel_id=1, source_target_pairs={{0,4},{2,6},{4,0},{6,2},{8,12},{10,14},{12,8},{14,10},{16,20},{18,... | collective-permute-start | bytes 6152 | tf_op jit(solution)/shard_map/ppermute | solution.py:404
  53.5 1.2 %collective-permute-start.27 = (f32[12,128]{1,0:T(8,128)S(1)}, f32[12,128]{1,0:T(8,128)S(1)}, u32[]{:S(2)}, u32[]{:S(2)}) collective-permute-start(f32[12,128]{1,0:T(8,128)S(1)} %get-tuple-element.88), channel_id=1, source_target_pairs={{0,1},{1,0},{2,3},{3,2},{4,5},{5,4},{6,7},{7,6},{8,9},{9,8},{10,11... | collective-permute-start | bytes 18440 | tf_op jit(solution)/shard_map/ppermute | solution.py:409
  54.7 3.6 %collective-permute-start.28 = (f32[8,128]{1,0:T(8,128)S(1)}, f32[8,128]{1,0:T(8,128)S(1)}, u32[]{:S(2)}, u32[]{:S(2)}) collective-permute-start(f32[8,128]{1,0:T(8,128)S(1)} %slice_dynamic-update-slice_fusion), channel_id=1, source_target_pairs={{0,8},{1,17},{2,10},{3,19},{4,12},{5,21},{6,14},{7,23},{8,0},{9,25... | collective-permute-start | bytes 12296 | tf_op jit(solution)/shard_map/ppermute | solution.py:417
  58.3 4.0 %collective-permute-start.29 = (f32[8,128]{1,0:T(8,128)S(1)}, f32[8,128]{1,0:T(8,128)S(1)}, u32[]{:S(2)}, u32[]{:S(2)}) collective-permute-start(f32[8,128]{1,0:T(8,128)S(1)} %collective-permute-done.28.refs_8_), channel_id=1, source_target_pairs={{0,1},{1,0},{2,3},{3,2},{4,5},{5,4},{6,7},{7,6},{8,9},{9,8},{10,11... | collective-permute-start | bytes 12296 | tf_op jit(solution)/shard_map/ppermute | solution.py:418
  58.3 3.6 %collective-permute-start.25 = (f32[4,128]{1,0:T(4,128)S(1)}, f32[4,128]{1,0:T(4,128)S(1)}, u32[]{:S(2)}, u32[]{:S(2)}) collective-permute-start(f32[4,128]{1,0:T(4,128)S(1)} %get-tuple-element.86), channel_id=1, source_target_pairs={{0,2},{2,0},{4,6},{6,4},{8,10},{10,8},{12,14},{14,12},{16,18},{18,... | collective-permute-start | bytes 6152 | tf_op jit(solution)/shard_map/ppermute | solution.py:404
  58.7 3.6 %collective-permute-start.26 = (f32[4,128]{1,0:T(4,128)S(1)}, f32[4,128]{1,0:T(4,128)S(1)}, u32[]{:S(2)}, u32[]{:S(2)}) collective-permute-start(f32[4,128]{1,0:T(4,128)S(1)} %get-tuple-element.87), channel_id=1, source_target_pairs={{0,4},{2,6},{4,0},{6,2},{8,12},{10,14},{12,8},{14,10},{16,20},{18,... | collective-permute-start | bytes 6152 | tf_op jit(solution)/shard_map/ppermute | solution.py:404
  (6 other events, 40.1 us)

commit v4 on v3

--- a/solution.py
+++ b/solution.py
@@ -11,7 +11,8 @@
 f32, bf16, i32 = jnp.float32, jnp.bfloat16, jnp.int32
 VMEM = pl.BlockSpec(memory_space=pltpu.VMEM)
 SUB, LANE = 8, 128
-HI_LANE, LO_LANE = 32, 64
+HI_LANE, LO_LANE = 64, 80
+HALF, FOLD = 4, 32
 
 
 def params():
@@ -70,10 +71,9 @@
     return high, a - high
 
 
-def two_product(a, a_split, b, b_split):
-    product = a * b
+def two_product(a, a_split, b_split):
     (ah, al), (bh, bl) = a_split, b_split
-    return product, ((ah * bh - product) + ah * bl + al * bh) + al * bl
+    return ah * bh, a * bl + al * bh
 
 
 def pair_add(a, b):
@@ -98,7 +98,11 @@
     return jnp.where(wanted == subs((LANE, LANE)), 1.0, 0.0).astype(f32).T[:rows]
 
 
-def first_body(face, order, place_ref, sends_ref, vector_ref, hot_ref, *rest):
+def begin_body(place_ref, out_ref):
+    out_ref[...] = place_ref[...]
+
+
+def first_body(face, order, place_ref, sends_ref, vector_ref, hot_ref, sent_ref, *rest):
     out_refs, row_ref = rest[:-1], rest[-1]
     row_ref[...] = jnp.full((SUB, LANE), -1, i32)
     even = place_ref[0:1, 0:face] == 0
@@ -109,7 +113,9 @@
         row_ref[0:1, to * face : (to + 1) * face] = taken
     hot = one_hot(row_ref[0:1, :], hot_ref.shape[0])[:, : hot_ref.shape[1]].astype(bf16)
     hot_ref[...] = hot
-    write_pieces(take_rows(hot, vector_ref[...]), out_refs)
+    sent = take_rows(hot, vector_ref[...])
+    sent_ref[...] = sent
+    write_pieces(sent, out_refs)
 
 
 def prepare(face, moves, columns_ref, couplings_ref, shifts_ref, place_ref, row_ref, hot_ref, wide_ref, shift_ref):
@@ -178,12 +184,13 @@
 
     wide = (jnp.zeros((SUB, LANE), f32), jnp.zeros((SUB, LANE), f32))
     for l in range(k + 1):
-        total = None
+        terms = []
         for g in range(groups):
-            other = vectors[l][g * SUB : (g + 1) * SUB, :] if l < k else newest[g]
-            other_split = split(other) if l < k else new_split[g]
-            product = two_product(newest[g], new_split[g], other, other_split)
-            total = product if total is None else pair_add(total, product)
+            other_split = split(vectors[l][g * SUB : (g + 1) * SUB, :]) if l < k else new_split[g]
+            terms.append(two_product(newest[g], new_split[g], other_split))
+        while len(terms) > 1:
+            terms = [pair_add(a, b) for a, b in zip(terms[::2], terms[1::2])] + terms[len(terms) // 2 * 2 :]
+        total = terms[0]
         for step in (4, 2, 1):
             total = pair_add(total, tuple(pltpu.roll(x, step, 0) for x in total))
         wide = tuple(jnp.where(sub == l, t, w) for t, w in zip(total, wide))
@@ -194,8 +201,7 @@
     row_k = sub == k
     packet = jnp.where(row_k & (lane < sketches), sketch_row, packet)
     for part, first in zip(wide, (HI_LANE, LO_LANE)):
-        column = lane == first + k
-        packet = jnp.where(column & (sub <= k), part, packet)
+        packet = jnp.where((lane == first + k) & (sub <= k), part, packet)
         turned = jnp.where(lane == first + sub, part, 0.0)
         for step in (4, 2, 1):
             turned = turned + pltpu.roll(turned, step, 0)
@@ -204,34 +210,34 @@
 
 
 def setup_body(face, moves, *refs):
-    columns_ref, couplings_ref, shifts_ref, place_ref, blocks_ref, vector_ref = refs[:6]
-    own_ref, hot_ref, wide_ref, shift_ref, row_ref = refs[6:]
+    columns_ref, couplings_ref, shifts_ref, place_ref, blocks_ref, vector_ref, send_ref, sent_ref = refs[:8]
+    own_ref, base_ref, hot_ref, wide_ref, send_hot_ref, send_wide_ref, shift_ref, row_ref = refs[8:]
     prepare(face, moves, columns_ref, couplings_ref, shifts_ref, place_ref, row_ref, hot_ref, wide_ref, shift_ref)
+    neighbours, rows = columns_ref.shape
+    count = send_ref.shape[0]
+    for k in range(neighbours):
+        picked = dot(send_ref[...], hot_ref[k * rows : (k + 1) * rows, :])
+        send_hot_ref[k * count : (k + 1) * count, :] = picked.astype(bf16)
+        send_wide_ref[k] = dot(send_ref[...], couplings_ref[k])
     matvec(blocks_ref, vector_ref, own_ref)
-
-
-def middle_body(k, last, *refs):
-    vectors, refs = refs[: k + 1], list(refs[k + 1 :])
-    sketch_ref = refs.pop(0)
-    packet = jnp.zeros((SUB, LANE), f32) if k == 1 else refs.pop(0)[...]
-    if last:
-        (packet_ref,) = refs
-    else:
-        blocks_ref, packet_ref, own_ref = refs
-        matvec(blocks_ref, vectors[k], own_ref)
-    for newest in range(0 if k == 1 else k, k + 1):
-        packet = statistics(newest, vectors, sketch_ref, packet)
-    packet_ref[...] = packet
-
-
-def next_body(k, places, last, *refs):
-    own_ref, vector_ref, hot_ref, wide_ref, shift_ref = refs[:5]
-    refs = refs[5:]
-    if not last:
-        send_ref, refs = refs[0], refs[1:]
-    halo_refs, refs = refs[: len(places)], refs[len(places) :]
-    next_ref, refs = refs[0], refs[1:]
-    out_refs, extended_ref = refs[:-1], refs[-1]
+    base_ref[...] = take_rows(send_ref[...], own_ref[...]) - shift_ref[0, 0:1, :] * sent_ref[...]
+
+
+def matvec_body(k, blocks_ref, vector_ref, *refs):
+    if len(refs) == 1:
+        return matvec(blocks_ref, vector_ref, refs[0])
+    send_ref, sent_ref, shift_ref, own_ref, base_ref = refs
+    matvec(blocks_ref, vector_ref, own_ref)
+    base_ref[...] = take_rows(send_ref[...], own_ref[...]) - shift_ref[k, 0:1, :] * sent_ref[...]
+
+
+def sums_body(k, *refs):
+    vectors, sketch_ref, refs = refs[: k + 1], refs[k + 1], refs[k + 2 :]
+    packet = refs[0][...] if k else jnp.zeros((SUB, LANE), f32)
+    refs[-1][...] = statistics(k, vectors, sketch_ref, packet)
+
+
+def extend(places, vector_ref, halo_refs, extended_ref):
     rows = vector_ref.shape[0]
     extended_ref[0:rows, :] = vector_ref[...]
     for (first, count, to), ref in zip(places, halo_refs):
@@ -239,17 +245,45 @@
     end = rows + sum(count for _, count, _ in places)
     if end < LANE:
         extended_ref[end:LANE, :] = jnp.zeros((LANE - end, LANE), f32)
-    parts = jnp.concatenate(two_parts(extended_ref[...]), axis=0)
-    gathered = dot(hot_ref[...], parts)
-    shift = shift_ref[k]
-    for g in range(rows // SUB):
-        at = slice(g * SUB, (g + 1) * SUB)
-        total = own_ref[at, :] - shift * vector_ref[at, :]
-        for n in range(wide_ref.shape[0]):
-            total = total + wide_ref[n, at, :] * gathered[n * rows + g * SUB : n * rows + (g + 1) * SUB]
-        next_ref[at, :] = total
-    if not last:
-        write_pieces(take_rows(send_ref[...], next_ref[...]), out_refs)
+    return jnp.concatenate(two_parts(extended_ref[...]), axis=0)
+
+
+def coupled(base, hot, wide_ref, parts):
+    gathered = dot(hot, parts)
+    count = base.shape[0]
+    for n in range(wide_ref.shape[0]):
+        base = base + wide_ref[n] * gathered[n * count : (n + 1) * count]
+    return base
+
+
+def sends_body(places, keep, *refs):
+    base_ref, vector_ref, send_hot_ref, send_wide_ref = refs[:4]
+    halo_refs, refs = refs[4 : 4 + len(places)], refs[4 + len(places) :]
+    parts_ref, extended_ref, out_refs = refs[0], refs[-1], refs[1:-1]
+    parts = extend(places, vector_ref, halo_refs, extended_ref)
+    parts_ref[...] = parts
+    sent = coupled(base_ref[...], send_hot_ref[...], send_wide_ref, parts)
+    if keep:
+        out_refs[0][...] = sent
+        out_refs = out_refs[1:]
+    write_pieces(sent, out_refs)
+
+
+def rest_body(k, own_ref, vector_ref, hot_ref, wide_ref, shift_ref, parts_ref, next_ref):
+    base = own_ref[...] - shift_ref[k, 0:1, :] * vector_ref[...]
+    next_ref[...] = coupled(base, hot_ref[...], wide_ref, parts_ref[...])
+
+
+def final_body(k, places, *refs):
+    own_ref, hot_ref, wide_ref, shift_ref, sketch_ref, packet_ref = refs[:6]
+    vectors, refs = refs[6 : 7 + k], refs[7 + k :]
+    halo_refs, (next_ref, folded_ref, extended_ref) = refs[: len(places)], refs[len(places) :]
+    vector_ref = vectors[-1]
+    parts = extend(places, vector_ref, halo_refs, extended_ref)
+    base = own_ref[...] - shift_ref[k, 0:1, :] * vector_ref[...]
+    next_ref[...] = coupled(base, hot_ref[...], wide_ref, parts)
+    packet = statistics(k + 1, [*vectors, next_ref], sketch_ref, packet_ref[...])
+    folded_ref[...] = (packet + pltpu.roll(pltpu.roll(packet, HALF, 0), FOLD, 1))[:HALF]
 
 
 def splat(value, row, column):
@@ -307,18 +341,18 @@
 
 
 def times_pair(pair, factor, factor_split):
-    product, error = two_product(pair[0], split(pair[0]), factor, factor_split)
+    product, error = two_product(pair[0], split(pair[0]), factor_split)
     return product, error + pair[1] * factor
 
 
 def last_body(n, sketches, total_rows, packets_ref, *refs):
     vector_refs, (orthonormal_ref, factor_ref, sketch_factor_ref) = refs[:n], refs[n:]
     lane, sub = lanes(), subs()
-    devices = packets_ref.shape[0] // SUB
-    sums = [(packets_ref[i * SUB : (i + 1) * SUB, :], jnp.zeros((SUB, LANE), f32)) for i in range(devices)]
+    sums = [(packets_ref[i : i + SUB, :], jnp.zeros((SUB, LANE), f32)) for i in range(0, packets_ref.shape[0], SUB)]
     while len(sums) > 1:
         sums = [pair_add(a, b) for a, b in zip(sums[::2], sums[1::2])] + sums[len(sums) // 2 * 2 :]
-    total, error = sums[0]
+    folded = pair_add(sums[0], tuple(pltpu.roll(x, HALF, 0) for x in sums[0]))
+    total, error = (jnp.where(sub < HALF, x, pltpu.roll(x, LANE - FOLD, 1)) for x in folded)
     low_parts = pltpu.roll(total + error, LANE - (LO_LANE - HI_LANE), 1)
     gram = two_sum(total, error + low_parts)
 
@@ -337,7 +371,8 @@
         row = jnp.zeros((SUB, LANE), f32)
         for j in range(k, n):
             row = jnp.where(lane == j, mixing[k, j], row)
-        column = tuple(jnp.broadcast_to(x[:, HI_LANE + k : HI_LANE + k + 1], (SUB, LANE)) for x in gram)
+        at = HI_LANE + k
+        column = tuple(jnp.broadcast_to(x[:, at : at + 1], (SUB, LANE)) for x in gram)
         term = times_pair(column, row, split(row))
         half = term if half is None else pair_add(half, term)
     half = two_sum(*half)
@@ -426,49 +461,88 @@
 
     exchange = exchange_relay if relay else exchange_direct
 
+    sent_out = ((send_pad, width), f32)
+    vector_out = ((rows, width), f32)
+    extended = [pltpu.VMEM((LANE, LANE), f32)]
+
     place = jnp.full((1, LANE), lax.axis_index("col"), i32)
-    send_hot, *outgoing = run(
+    (place,) = run(begin_body, [((1, LANE), i32)], (place,), cost=(1_000_000_000, 40_000_000))
+    send_ones, sent, *outgoing = run(
         functools.partial(first_body, face, order),
-        [((send_pad, rows), bf16)] + piece_outs,
+        [((send_pad, rows), bf16), sent_out] + piece_outs,
         (place, send_rows, start_vector),
         cost=(100_000_000_000, 1_000_000_000),
         scratch=[pltpu.VMEM((SUB, LANE), i32)],
     )
     vectors = [start_vector]
-    packet = ()
+    packet = []
+
+    def sums(packet):
+        k = len(vectors) - 1
+        args = (*vectors, sketch, *packet)
+        return run(functools.partial(sums_body, k), [((SUB, LANE), f32)], args, (4_000_000, 2_000_000))
+
+    rest = None
     for k in range(powers):
         final = k + 1 == powers
         received = exchange(outgoing, k)
+        if k:
+            (vector,) = run(functools.partial(rest_body, k - 1), [vector_out], rest, (1_000_000, 1_000_000))
+            vectors.append(vector)
         if k == 0:
-            own, neighbour_hot, wide, shift = run(
+            own, *base, neighbour_hot, wide, send_hot, send_wide, shift = run(
                 functools.partial(setup_body, face, moves),
                 [
-                    ((rows, width), f32),
+                    vector_out,
+                    sent_out,
                     ((neighbours * rows, 2 * LANE), bf16),
                     ((neighbours, rows, width), f32),
+                    ((neighbours * send_pad, 2 * LANE), bf16),
+                    ((neighbours, send_pad, width), f32),
                     ((powers, SUB, LANE), f32),
                 ],
-                (columns.T, couplings.transpose(1, 0, 2), shifts.reshape(1, powers), place, blocks, start_vector),
+                (
+                    columns.T,
+                    couplings.transpose(1, 0, 2),
+                    shifts.reshape(1, powers),
+                    place,
+                    blocks,
+                    start_vector,
+                    send_ones,
+                    sent,
+                ),
                 cost=(20_000_000, 4_000_000),
                 scratch=[pltpu.VMEM((SUB, LANE), i32)],
             )
         else:
-            *packet, own = run(
-                functools.partial(middle_body, k, False),
-                [((SUB, LANE), f32), ((rows, width), f32)],
-                (*vectors, sketch, *packet, blocks),
-                cost=(20_000_000, 4_000_000),
+            own, *base = run(
+                functools.partial(matvec_body, k),
+                [vector_out] if final else [vector_out, sent_out],
+                (blocks, vectors[-1], *(() if final else (send_ones, sent, shift))),
+                (20_000_000, 4_000_000),
             )
-        vector, *outgoing = run(
-            functools.partial(next_body, k, places, final),
-            [((rows, width), f32)] + ([] if final else piece_outs),
-            (own, vectors[-1], neighbour_hot, wide, shift, *(() if final else (send_hot,)), *received),
-            cost=(1_000_000, 1_000_000),
-            scratch=[pltpu.VMEM((LANE, LANE), f32)],
-        )
-        vectors.append(vector)
-    (packet,) = run(functools.partial(middle_body, powers, True), [((SUB, LANE), f32)], (*vectors, sketch, *packet))
-
+        packet = sums(packet)
+        if final:
+            vector, packet = run(
+                functools.partial(final_body, k, places),
+                [vector_out, ((HALF, LANE), f32)],
+                (own, neighbour_hot, wide, shift, sketch, *packet, *vectors, *received),
+                cost=(4_000_000, 2_000_000),
+                scratch=extended,
+            )
+            vectors.append(vector)
+        else:
+            keep = k + 2 < powers
+            parts, *outgoing = run(
+                functools.partial(sends_body, places, keep),
+                [((2 * LANE, width), bf16)] + ([sent_out] if keep else []) + piece_outs,
+                (*base, vectors[-1], send_hot, send_wide, *received),
+                cost=(1_000_000, 1_000_000),
+                scratch=extended,
+            )
+            if keep:
+                sent, *outgoing = outgoing
+            rest = (own, vectors[-1], neighbour_hot, wide, shift, parts)
     everyone = ("dom", "col")
     packets = lax.all_to_all(jnp.tile(packet, (dom * col, 1)), everyone, 0, 0, tiled=True)
     orthonormal, factor, sketch_factor = run(

time: 78.9 us -> 79.3 us (level)
  Pallas kernels: 11.6 us -> 15.2 us
  waiting for transfers between devices: 23.4 us -> 21.1 us
  blocking collectives: 14 us -> 13.2 us
    pallas_call x15 -> x26, Pallas kernels: 11.6 us -> 15.2 us  [run(): pl.pallas_call(body, out_shape=[jax.ShapeDtypeStruct(shape, dtype) for sh...]
    ppermute x12, waiting for transfers between devices: 5.12 us -> 3.55 us  [with_partner(): return lax.ppermute(piece, 'dom', [(i, i ^ 1 << level) for i in range(dom)])]
    all_to_all x1, blocking collectives: 14 us -> 13.2 us  [shards(): lax.all_to_all(jnp.tile(packet, (dom * col, 1)), everyone, 0, 0, tiled=True)]
  transfers between devices with their start and end apart: 30 -> 30, of which waited for: 21 -> 20; matrix products, arithmetic and copies ran while one was open for 0% -> 0% of each run, Pallas kernels for 9% -> 14%
where the time goes in v4:
time: 79.3 us; the launch traced here: 79.1 us
  starting transfers between devices  27.9 us (35%)
  waiting for transfers between devices  21.1 us (27%)
  Pallas kernels  15.2 us (19%)
  blocking collectives  13.2 us (17%)
  between operations  0.9 us (1%)
  local copies, waits for them, and re-layouts  0.84 us (1%)
    ppermute x12, starting transfers between devices, with_partner(): return lax.ppermute(piece, 'dom', [(i, i ^ 1 << level) for i in range(dom)])  15.7 us
    pallas_call x26, Pallas kernels, run(): pl.pallas_call(body, out_shape=[jax.ShapeDtypeStruct(shape, dtype) for sh...  15.2 us
    all_to_all x1, blocking collectives, shards(): lax.all_to_all(jnp.tile(packet, (dom * col, 1)), everyone, 0, 0, tiled=True)  13.2 us
    ppermute x6, starting transfers between devices, exchange_relay(): pair = lax.ppermute(pair, ('dom', 'col'), far_pairs)  11.1 us
    ppermute x6, waiting for transfers between devices, exchange_relay(): pair = lax.ppermute(pair, ('dom', 'col'), far_pairs)  10.9 us
    ppermute x6, waiting for transfers between devices, exchange_relay(): side = lax.ppermute(side, 'col', swapped)  6.62 us
    ppermute x12, waiting for transfers between devices, with_partner(): return lax.ppermute(piece, 'dom', [(i, i ^ 1 << level) for i in range(dom)])  3.55 us
  transfers between devices with their start and end apart: 30, of which 20 were waited for; matrix products, arithmetic and copies ran while one was open for 0% of the time, Pallas kernels for 14%

profile of v4, /device:TPU:0, one launch (start us, length us, event | category | flops | bytes accessed | tf_op | source)
XLA Modules:
  0.0 79.1 jit_solution(8350387169581850817)
XLA Ops:
  3.1 2.9 %collective-permute-start.3 = (f32[8,128]{1,0:T(8,128)S(1)}, f32[8,128]{1,0:T(8,128)S(1)}, u32[]{:S(2)}, u32[]{:S(2)}) collective-permute-start(f32[8,128]{1,0:T(8,128)S(1)} %slice_dynamic-update-slice_fusion.5), channel_id=1, source_target_pairs={{0,8},{1,17},{2,10},{3,19},{4,12},{5,21},{6,14},{7,23},{8,0},{9,25... | collective-permute-start | bytes 12296 | tf_op jit(solution)/shard_map/ppermute | solution.py:452
  6.0 1.6 %collective-permute-done.3.refs_7_ = f32[8,128]{1,0:T(8,128)S(1)} collective-permute-done((f32[8,128]{1,0:T(8,128)S(1)}, f32[8,128]{1,0:T(8,128)S(1)}, u32[]{:S(2)}, u32[]{:S(2)}) %collective-permute-start.3) | collective-permute-done | bytes 4128 | tf_op jit(solution)/shard_map/ppermute | solution.py:452
  7.9 1.6 %collective-permute-start = (f32[4,128]{1,0:T(4,128)S(1)}, f32[4,128]{1,0:T(4,128)S(1)}, u32[]{:S(2)}, u32[]{:S(2)}) collective-permute-start(f32[4,128]{1,0:T(4,128)S(1)} %get-tuple-element.64), channel_id=1, source_target_pairs={{0,2},{2,0},{4,6},{6,4},{8,10},{10,8},{12,14},{14,12},{16,18},{18,... | collective-permute-start | bytes 6152 | tf_op jit(solution)/shard_map/ppermute | solution.py:439
  9.6 1.5 %collective-permute-start.1 = (f32[4,128]{1,0:T(4,128)S(1)}, f32[4,128]{1,0:T(4,128)S(1)}, u32[]{:S(2)}, u32[]{:S(2)}) collective-permute-start(f32[4,128]{1,0:T(4,128)S(1)} %get-tuple-element.65), channel_id=1, source_target_pairs={{0,4},{2,6},{4,0},{6,2},{8,12},{10,14},{12,8},{14,10},{16,20},{18,... | collective-permute-start | bytes 6152 | tf_op jit(solution)/shard_map/ppermute | solution.py:439
  11.1 1.3 %shard_map.96 = (f32[96,128]{1,0:T(8,128)S(1)}, f32[32,128]{1,0:T(8,128)S(1)}, bf16[576,256]{1,0:T(8,128)(2,1)S(1)}, f32[6,96,128]{2,1,0:T(8,128)S(1)}, bf16[192...) custom-call(s32[6,96]{1,0:T(8,128)S(1)} %bitcast.13, bf16[6,96,128]{2,1,0:T(8,128)(2,1)S(1)} %bitcast.12, ...), custom_call_target="tpu_custom_call" | custom-call | flops 20000000 | bytes 4000000 | tf_op jit(solution)/shard_map/pallas_call | solution.py:23
  13.4 1.2 %collective-permute-done.7.refs_6_ = f32[12,128]{1,0:T(8,128)S(1)} collective-permute-done((f32[12,128]{1,0:T(8,128)S(1)}, f32[12,128]{1,0:T(8,128)S(1)}, u32[]{:S(2)}, u32[]{:S(2)}) %collective-permute-start.7) | collective-permute-done | bytes 6176 | tf_op jit(solution)/shard_map/ppermute | solution.py:444
  14.6 1.6 %collective-permute-start.8 = (f32[8,128]{1,0:T(8,128)S(1)}, f32[8,128]{1,0:T(8,128)S(1)}, u32[]{:S(2)}, u32[]{:S(2)}) collective-permute-start(f32[8,128]{1,0:T(8,128)S(1)} %slice_dynamic-update-slice_fusion.4), channel_id=1, source_target_pairs={{0,8},{1,17},{2,10},{3,19},{4,12},{5,21},{6,14},{7,23},{8,0},{9,25... | collective-permute-start | bytes 12296 | tf_op jit(solution)/shard_map/ppermute | solution.py:452
  16.2 2.0 %collective-permute-done.8.refs_7_ = f32[8,128]{1,0:T(8,128)S(1)} collective-permute-done((f32[8,128]{1,0:T(8,128)S(1)}, f32[8,128]{1,0:T(8,128)S(1)}, u32[]{:S(2)}, u32[]{:S(2)}) %collective-permute-start.8) | collective-permute-done | bytes 4128 | tf_op jit(solution)/shard_map/ppermute | solution.py:452
  18.6 1.7 %collective-permute-start.6 = (f32[4,128]{1,0:T(4,128)S(1)}, f32[4,128]{1,0:T(4,128)S(1)}, u32[]{:S(2)}, u32[]{:S(2)}) collective-permute-start(f32[4,128]{1,0:T(4,128)S(1)} %get-tuple-element.73), channel_id=1, source_target_pairs={{0,4},{2,6},{4,0},{6,2},{8,12},{10,14},{12,8},{14,10},{16,20},{18,... | collective-permute-start | bytes 6152 | tf_op jit(solution)/shard_map/ppermute | solution.py:439
  22.4 1.2 %collective-permute-done.12.refs_6_ = f32[12,128]{1,0:T(8,128)S(1)} collective-permute-done((f32[12,128]{1,0:T(8,128)S(1)}, f32[12,128]{1,0:T(8,128)S(1)}, u32[]{:S(2)}, u32[]{:S(2)}) %collective-permute-start.12) | collective-permute-done | bytes 6176 | tf_op jit(solution)/shard_map/ppermute | solution.py:444
  23.6 1.7 %collective-permute-start.13 = (f32[8,128]{1,0:T(8,128)S(1)}, f32[8,128]{1,0:T(8,128)S(1)}, u32[]{:S(2)}, u32[]{:S(2)}) collective-permute-start(f32[8,128]{1,0:T(8,128)S(1)} %slice_dynamic-update-slice_fusion.3), channel_id=1, source_target_pairs={{0,8},{1,17},{2,10},{3,19},{4,12},{5,21},{6,14},{7,23},{8,0},{9,25... | collective-permute-start | bytes 12296 | tf_op jit(solution)/shard_map/ppermute | solution.py:452
  25.3 1.9 %collective-permute-done.13.refs_7_ = f32[8,128]{1,0:T(8,128)S(1)} collective-permute-done((f32[8,128]{1,0:T(8,128)S(1)}, f32[8,128]{1,0:T(8,128)S(1)}, u32[]{:S(2)}, u32[]{:S(2)}) %collective-permute-start.13) | collective-permute-done | bytes 4128 | tf_op jit(solution)/shard_map/ppermute | solution.py:452
  27.2 1.6 %collective-permute-start.10 = (f32[4,128]{1,0:T(4,128)S(1)}, f32[4,128]{1,0:T(4,128)S(1)}, u32[]{:S(2)}, u32[]{:S(2)}) collective-permute-start(f32[4,128]{1,0:T(4,128)S(1)} %get-tuple-element.80), channel_id=1, source_target_pairs={{0,2},{2,0},{4,6},{6,4},{8,10},{10,8},{12,14},{14,12},{16,18},{18,... | collective-permute-start | bytes 6152 | tf_op jit(solution)/shard_map/ppermute | solution.py:439
  28.9 1.5 %collective-permute-start.11 = (f32[4,128]{1,0:T(4,128)S(1)}, f32[4,128]{1,0:T(4,128)S(1)}, u32[]{:S(2)}, u32[]{:S(2)}) collective-permute-start(f32[4,128]{1,0:T(4,128)S(1)} %get-tuple-element.81), channel_id=1, source_target_pairs={{0,4},{2,6},{4,0},{6,2},{8,12},{10,14},{12,8},{14,10},{16,20},{18,... | collective-permute-start | bytes 6152 | tf_op jit(solution)/shard_map/ppermute | solution.py:439
  30.6 1.1 %shard_map.102 = (f32[96,128]{1,0:T(8,128)S(1)}, f32[32,128]{1,0:T(8,128)S(1)}) custom-call(bf16[12288,128]{1,0:T(8,128)(2,1)S(1)} %bitcast.7, f32[96,128]{1,0:T(8,128)S(1)} %shard_map.101.vector_ref.refs_1_.refs_2_.refs_8_, bf16[32,96]{1,0:T(8,128)(2,1)S(1)} %get-tuple-element.55.refs_6_.refs_0_, f32[32,128]{1,0:T(8,128)S(1)} %get-tuple-element.77.refs_1_, ...), custom_call_target="tpu_custom_call" | custom-call | flops 20000000 | bytes 4000000 | tf_op jit(solution)/shard_map/pallas_call | solution.py:23
  32.7 1.2 %collective-permute-done.17.refs_6_ = f32[12,128]{1,0:T(8,128)S(1)} collective-permute-done((f32[12,128]{1,0:T(8,128)S(1)}, f32[12,128]{1,0:T(8,128)S(1)}, u32[]{:S(2)}, u32[]{:S(2)}) %collective-permute-start.17) | collective-permute-done | bytes 6176 | tf_op jit(solution)/shard_map/ppermute | solution.py:444
  33.9 1.6 %collective-permute-start.18 = (f32[8,128]{1,0:T(8,128)S(1)}, f32[8,128]{1,0:T(8,128)S(1)}, u32[]{:S(2)}, u32[]{:S(2)}) collective-permute-start(f32[8,128]{1,0:T(8,128)S(1)} %slice_dynamic-update-slice_fusion.2), channel_id=1, source_target_pairs={{0,8},{1,17},{2,10},{3,19},{4,12},{5,21},{6,14},{7,23},{8,0},{9,25... | collective-permute-start | bytes 12296 | tf_op jit(solution)/shard_map/ppermute | solution.py:452
  35.4 2.0 %collective-permute-done.18.refs_7_ = f32[8,128]{1,0:T(8,128)S(1)} collective-permute-done((f32[8,128]{1,0:T(8,128)S(1)}, f32[8,128]{1,0:T(8,128)S(1)}, u32[]{:S(2)}, u32[]{:S(2)}) %collective-permute-start.18) | collective-permute-done | bytes 4128 | tf_op jit(solution)/shard_map/ppermute | solution.py:452
  37.9 1.7 %collective-permute-start.16 = (f32[4,128]{1,0:T(4,128)S(1)}, f32[4,128]{1,0:T(4,128)S(1)}, u32[]{:S(2)}, u32[]{:S(2)}) collective-permute-start(f32[4,128]{1,0:T(4,128)S(1)} %get-tuple-element.89), channel_id=1, source_target_pairs={{0,4},{2,6},{4,0},{6,2},{8,12},{10,14},{12,8},{14,10},{16,20},{18,... | collective-permute-start | bytes 6152 | tf_op jit(solution)/shard_map/ppermute | solution.py:439
  39.8 1.1 %shard_map.105 = (f32[96,128]{1,0:T(8,128)S(1)}, f32[32,128]{1,0:T(8,128)S(1)}) custom-call(bf16[12288,128]{1,0:T(8,128)(2,1)S(1)} %bitcast.8, f32[96,128]{1,0:T(8,128)S(1)} %shard_map.104.vector_ref.refs_1_.refs_3_.refs_9_, bf16[32,96]{1,0:T(8,128)(2,1)S(1)} %get-tuple-element.55.refs_6_.refs_0_, f32[32,128]{1,0:T(8,128)S(1)} %get-tuple-element.85.refs_1_, ...), custom_call_target="tpu_custom_call" | custom-call | flops 20000000 | bytes 4000000 | tf_op jit(solution)/shard_map/pallas_call | solution.py:23
  41.7 1.2 %collective-permute-done.22.refs_6_ = f32[12,128]{1,0:T(8,128)S(1)} collective-permute-done((f32[12,128]{1,0:T(8,128)S(1)}, f32[12,128]{1,0:T(8,128)S(1)}, u32[]{:S(2)}, u32[]{:S(2)}) %collective-permute-start.22) | collective-permute-done | bytes 6176 | tf_op jit(solution)/shard_map/ppermute | solution.py:444
  42.9 1.7 %collective-permute-start.23 = (f32[8,128]{1,0:T(8,128)S(1)}, f32[8,128]{1,0:T(8,128)S(1)}, u32[]{:S(2)}, u32[]{:S(2)}) collective-permute-start(f32[8,128]{1,0:T(8,128)S(1)} %slice_dynamic-update-slice_fusion.1), channel_id=1, source_target_pairs={{0,8},{1,17},{2,10},{3,19},{4,12},{5,21},{6,14},{7,23},{8,0},{9,25... | collective-permute-start | bytes 12296 | tf_op jit(solution)/shard_map/ppermute | solution.py:452
  44.6 1.9 %collective-permute-done.23.refs_7_ = f32[8,128]{1,0:T(8,128)S(1)} collective-permute-done((f32[8,128]{1,0:T(8,128)S(1)}, f32[8,128]{1,0:T(8,128)S(1)}, u32[]{:S(2)}, u32[]{:S(2)}) %collective-permute-start.23) | collective-permute-done | bytes 4128 | tf_op jit(solution)/shard_map/ppermute | solution.py:452
  46.5 1.6 %collective-permute-start.20 = (f32[4,128]{1,0:T(4,128)S(1)}, f32[4,128]{1,0:T(4,128)S(1)}, u32[]{:S(2)}, u32[]{:S(2)}) collective-permute-start(f32[4,128]{1,0:T(4,128)S(1)} %get-tuple-element.96), channel_id=1, source_target_pairs={{0,2},{2,0},{4,6},{6,4},{8,10},{10,8},{12,14},{14,12},{16,18},{18,... | collective-permute-start | bytes 6152 | tf_op jit(solution)/shard_map/ppermute | solution.py:439
  48.1 1.5 %collective-permute-start.21 = (f32[4,128]{1,0:T(4,128)S(1)}, f32[4,128]{1,0:T(4,128)S(1)}, u32[]{:S(2)}, u32[]{:S(2)}) collective-permute-start(f32[4,128]{1,0:T(4,128)S(1)} %get-tuple-element.97), channel_id=1, source_target_pairs={{0,4},{2,6},{4,0},{6,2},{8,12},{10,14},{12,8},{14,10},{16,20},{18,... | collective-permute-start | bytes 6152 | tf_op jit(solution)/shard_map/ppermute | solution.py:439
  52.0 1.2 %collective-permute-done.27.refs_14_ = f32[12,128]{1,0:T(8,128)S(1)} collective-permute-done((f32[12,128]{1,0:T(8,128)S(1)}, f32[12,128]{1,0:T(8,128)S(1)}, u32[]{:S(2)}, u32[]{:S(2)}) %collective-permute-start.27) | collective-permute-done | bytes 6176 | tf_op jit(solution)/shard_map/ppermute | solution.py:444
  53.1 1.6 %collective-permute-start.28 = (f32[8,128]{1,0:T(8,128)S(1)}, f32[8,128]{1,0:T(8,128)S(1)}, u32[]{:S(2)}, u32[]{:S(2)}) collective-permute-start(f32[8,128]{1,0:T(8,128)S(1)} %slice_dynamic-update-slice_fusion), channel_id=1, source_target_pairs={{0,8},{1,17},{2,10},{3,19},{4,12},{5,21},{6,14},{7,23},{8,0},{9,25... | collective-permute-start | bytes 12296 | tf_op jit(solution)/shard_map/ppermute | solution.py:452
  55.3 1.5 %collective-permute-done.28.refs_15_ = f32[8,128]{1,0:T(8,128)S(1)} collective-permute-done((f32[8,128]{1,0:T(8,128)S(1)}, f32[8,128]{1,0:T(8,128)S(1)}, u32[]{:S(2)}, u32[]{:S(2)}) %collective-permute-start.28) | collective-permute-done | bytes 4128 | tf_op jit(solution)/shard_map/ppermute | solution.py:452
  59.7 1.7 %collective-permute-start.26 = (f32[4,128]{1,0:T(4,128)S(1)}, f32[4,128]{1,0:T(4,128)S(1)}, u32[]{:S(2)}, u32[]{:S(2)}) collective-permute-start(f32[4,128]{1,0:T(4,128)S(1)} %get-tuple-element.102), channel_id=1, source_target_pairs={{0,4},{2,6},{4,0},{6,2},{8,12},{10,14},{12,8},{14,10},{16,20},{18,... | collective-permute-start | bytes 6152 | tf_op jit(solution)/shard_map/ppermute | solution.py:439
  63.3 1.2 %shard_map.118 = (f32[96,128]{1,0:T(8,128)S(1)}, f32[4,128]{1,0:T(4,128)S(1)}) custom-call(f32[96,128]{1,0:T(8,128)S(1)} %shard_map.111.refs_0_, bf16[576,256]{1,0:T(8,128)(2,1)S(1)} %get-tuple-element.58.hot_ref.refs_1_, f32[6,96,128]{2,1,0:T(8,128)S(1)} %get-tuple-element.59.wide_ref.refs_2_, f32[6,8,128]{2,1,0:T(8,128)S(1)} %get-tuple-element.60.shift_ref.refs_2_.refs_3_, ...), custom_call_target="tpu_custom_call" | custom-call | flops 4000000 | bytes 2000000 | tf_op jit(solution)/shard_map/pallas_call | solution.py:23
  64.5 13.2 %all_to_all.8 = f32[32,4,128]{2,1,0:T(4,128)S(1)} all-to-all(f32[32,4,128]{2,1,0:T(4,128)S(1)} %tile.2), channel_id=1, replica_groups=mesh['dom'=16,'col'=2] {'dom','col'}, dimensions={0} | all-to-all | bytes 131072 | tf_op jit(solution)/shard_map/all_to_all | solution.py:547
  77.7 1.4 %shard_map.119 = (f32[7,96,128]{2,1,0:T(8,128)}, f32[7,7]{1,0:T(8,128)}, f32[7,7]{1,0:T(8,128)}) custom-call(f32[128,128]{1,0:T(8,128)S(1)} %bitcast.11, f32[96,128]{1,0:T(8,128)S(1)} %copy-done.2, f32[96,128]{1,0:T(8,128)S(1)} %shard_map.98.vector_ref.refs_1_.refs_7_, f32[96,128]{1,0:T(8,128)S(1)} %shard_map.101.vector_ref.refs_1_.refs_2_.refs_8_, ...), custom_call_target="tpu_custom_call" | custom-call | flops 5000000 | bytes 1000000 | tf_op jit(solution)/shard_map/pallas_call | solution.py:23
  (77 shorter events, 16.8 us)
Async XLA Ops:
  1.4 9.7 %copy-start.4 = (s32[96,6]{0,1:T(8,128)S(1)}, s32[96,6]{0,1:T(8,128)}, u32[]{:S(2)}) copy-start(s32[96,6]{0,1:T(8,128)} %param.9) | copy-start | bytes 6916
  1.8 1.3 %collective-permute-start.2 = (f32[12,128]{1,0:T(8,128)S(1)}, f32[12,128]{1,0:T(8,128)S(1)}, u32[]{:S(2)}, u32[]{:S(2)}) collective-permute-start(f32[12,128]{1,0:T(8,128)S(1)} %get-tuple-element.66), channel_id=1, source_target_pairs={{0,1},{1,0},{2,3},{3,2},{4,5},{5,4},{6,7},{7,6},{8,9},{9,8},{10,11... | collective-permute-start | bytes 18440 | tf_op jit(solution)/shard_map/ppermute | solution.py:444
  3.1 4.5 %collective-permute-start.3 = (f32[8,128]{1,0:T(8,128)S(1)}, f32[8,128]{1,0:T(8,128)S(1)}, u32[]{:S(2)}, u32[]{:S(2)}) collective-permute-start(f32[8,128]{1,0:T(8,128)S(1)} %slice_dynamic-update-slice_fusion.5), channel_id=1, source_target_pairs={{0,8},{1,17},{2,10},{3,19},{4,12},{5,21},{6,14},{7,23},{8,0},{9,25... | collective-permute-start | bytes 12296 | tf_op jit(solution)/shard_map/ppermute | solution.py:452
  7.6 5.5 %collective-permute-start.4 = (f32[8,128]{1,0:T(8,128)S(1)}, f32[8,128]{1,0:T(8,128)S(1)}, u32[]{:S(2)}, u32[]{:S(2)}) collective-permute-start(f32[8,128]{1,0:T(8,128)S(1)} %collective-permute-done.3.refs_7_), channel_id=1, source_target_pairs={{0,1},{1,0},{2,3},{3,2},{4,5},{5,4},{6,7},{7,6},{8,9},{9,8},{10,11... | collective-permute-start | bytes 12296 | tf_op jit(solution)/shard_map/ppermute | solution.py:453
  7.9 4.5 %collective-permute-start = (f32[4,128]{1,0:T(4,128)S(1)}, f32[4,128]{1,0:T(4,128)S(1)}, u32[]{:S(2)}, u32[]{:S(2)}) collective-permute-start(f32[4,128]{1,0:T(4,128)S(1)} %get-tuple-element.64), channel_id=1, source_target_pairs={{0,2},{2,0},{4,6},{6,4},{8,10},{10,8},{12,14},{14,12},{16,18},{18,... | collective-permute-start | bytes 6152 | tf_op jit(solution)/shard_map/ppermute | solution.py:439
  9.6 3.6 %collective-permute-start.1 = (f32[4,128]{1,0:T(4,128)S(1)}, f32[4,128]{1,0:T(4,128)S(1)}, u32[]{:S(2)}, u32[]{:S(2)}) collective-permute-start(f32[4,128]{1,0:T(4,128)S(1)} %get-tuple-element.65), channel_id=1, source_target_pairs={{0,4},{2,6},{4,0},{6,2},{8,12},{10,14},{12,8},{14,10},{16,20},{18,... | collective-permute-start | bytes 6152 | tf_op jit(solution)/shard_map/ppermute | solution.py:439
  13.3 1.2 %collective-permute-start.7 = (f32[12,128]{1,0:T(8,128)S(1)}, f32[12,128]{1,0:T(8,128)S(1)}, u32[]{:S(2)}, u32[]{:S(2)}) collective-permute-start(f32[12,128]{1,0:T(8,128)S(1)} %get-tuple-element.74), channel_id=1, source_target_pairs={{0,1},{1,0},{2,3},{3,2},{4,5},{5,4},{6,7},{7,6},{8,9},{9,8},{10,11... | collective-permute-start | bytes 18440 | tf_op jit(solution)/shard_map/ppermute | solution.py:444
  14.6 3.6 %collective-permute-start.8 = (f32[8,128]{1,0:T(8,128)S(1)}, f32[8,128]{1,0:T(8,128)S(1)}, u32[]{:S(2)}, u32[]{:S(2)}) collective-permute-start(f32[8,128]{1,0:T(8,128)S(1)} %slice_dynamic-update-slice_fusion.4), channel_id=1, source_target_pairs={{0,8},{1,17},{2,10},{3,19},{4,12},{5,21},{6,14},{7,23},{8,0},{9,25... | collective-permute-start | bytes 12296 | tf_op jit(solution)/shard_map/ppermute | solution.py:452
  18.2 4.0 %collective-permute-start.9 = (f32[8,128]{1,0:T(8,128)S(1)}, f32[8,128]{1,0:T(8,128)S(1)}, u32[]{:S(2)}, u32[]{:S(2)}) collective-permute-start(f32[8,128]{1,0:T(8,128)S(1)} %collective-permute-done.8.refs_7_), channel_id=1, source_target_pairs={{0,1},{1,0},{2,3},{3,2},{4,5},{5,4},{6,7},{7,6},{8,9},{9,8},{10,11... | collective-permute-start | bytes 12296 | tf_op jit(solution)/shard_map/ppermute | solution.py:453
  18.2 3.6 %collective-permute-start.5 = (f32[4,128]{1,0:T(4,128)S(1)}, f32[4,128]{1,0:T(4,128)S(1)}, u32[]{:S(2)}, u32[]{:S(2)}) collective-permute-start(f32[4,128]{1,0:T(4,128)S(1)} %get-tuple-element.72), channel_id=1, source_target_pairs={{0,2},{2,0},{4,6},{6,4},{8,10},{10,8},{12,14},{14,12},{16,18},{18,... | collective-permute-start | bytes 6152 | tf_op jit(solution)/shard_map/ppermute | solution.py:439
  18.6 3.6 %collective-permute-start.6 = (f32[4,128]{1,0:T(4,128)S(1)}, f32[4,128]{1,0:T(4,128)S(1)}, u32[]{:S(2)}, u32[]{:S(2)}) collective-permute-start(f32[4,128]{1,0:T(4,128)S(1)} %get-tuple-element.73), channel_id=1, source_target_pairs={{0,4},{2,6},{4,0},{6,2},{8,12},{10,14},{12,8},{14,10},{16,20},{18,... | collective-permute-start | bytes 6152 | tf_op jit(solution)/shard_map/ppermute | solution.py:439
  22.4 1.2 %collective-permute-start.12 = (f32[12,128]{1,0:T(8,128)S(1)}, f32[12,128]{1,0:T(8,128)S(1)}, u32[]{:S(2)}, u32[]{:S(2)}) collective-permute-start(f32[12,128]{1,0:T(8,128)S(1)} %get-tuple-element.82), channel_id=1, source_target_pairs={{0,1},{1,0},{2,3},{3,2},{4,5},{5,4},{6,7},{7,6},{8,9},{9,8},{10,11... | collective-permute-start | bytes 18440 | tf_op jit(solution)/shard_map/ppermute | solution.py:444
  23.6 3.6 %collective-permute-start.13 = (f32[8,128]{1,0:T(8,128)S(1)}, f32[8,128]{1,0:T(8,128)S(1)}, u32[]{:S(2)}, u32[]{:S(2)}) collective-permute-start(f32[8,128]{1,0:T(8,128)S(1)} %slice_dynamic-update-slice_fusion.3), channel_id=1, source_target_pairs={{0,8},{1,17},{2,10},{3,19},{4,12},{5,21},{6,14},{7,23},{8,0},{9,25... | collective-permute-start | bytes 12296 | tf_op jit(solution)/shard_map/ppermute | solution.py:452
  27.2 5.2 %collective-permute-start.14 = (f32[8,128]{1,0:T(8,128)S(1)}, f32[8,128]{1,0:T(8,128)S(1)}, u32[]{:S(2)}, u32[]{:S(2)}) collective-permute-start(f32[8,128]{1,0:T(8,128)S(1)} %collective-permute-done.13.refs_7_), channel_id=1, source_target_pairs={{0,1},{1,0},{2,3},{3,2},{4,5},{5,4},{6,7},{7,6},{8,9},{9,8},{10,11... | collective-permute-start | bytes 12296 | tf_op jit(solution)/shard_map/ppermute | solution.py:453
  27.2 4.5 %collective-permute-start.10 = (f32[4,128]{1,0:T(4,128)S(1)}, f32[4,128]{1,0:T(4,128)S(1)}, u32[]{:S(2)}, u32[]{:S(2)}) collective-permute-start(f32[4,128]{1,0:T(4,128)S(1)} %get-tuple-element.80), channel_id=1, source_target_pairs={{0,2},{2,0},{4,6},{6,4},{8,10},{10,8},{12,14},{14,12},{16,18},{18,... | collective-permute-start | bytes 6152 | tf_op jit(solution)/shard_map/ppermute | solution.py:439
  28.9 3.6 %collective-permute-start.11 = (f32[4,128]{1,0:T(4,128)S(1)}, f32[4,128]{1,0:T(4,128)S(1)}, u32[]{:S(2)}, u32[]{:S(2)}) collective-permute-start(f32[4,128]{1,0:T(4,128)S(1)} %get-tuple-element.81), channel_id=1, source_target_pairs={{0,4},{2,6},{4,0},{6,2},{8,12},{10,14},{12,8},{14,10},{16,20},{18,... | collective-permute-start | bytes 6152 | tf_op jit(solution)/shard_map/ppermute | solution.py:439
  32.6 1.2 %collective-permute-start.17 = (f32[12,128]{1,0:T(8,128)S(1)}, f32[12,128]{1,0:T(8,128)S(1)}, u32[]{:S(2)}, u32[]{:S(2)}) collective-permute-start(f32[12,128]{1,0:T(8,128)S(1)} %get-tuple-element.90), channel_id=1, source_target_pairs={{0,1},{1,0},{2,3},{3,2},{4,5},{5,4},{6,7},{7,6},{8,9},{9,8},{10,11... | collective-permute-start | bytes 18440 | tf_op jit(solution)/shard_map/ppermute | solution.py:444
  33.9 3.6 %collective-permute-start.18 = (f32[8,128]{1,0:T(8,128)S(1)}, f32[8,128]{1,0:T(8,128)S(1)}, u32[]{:S(2)}, u32[]{:S(2)}) collective-permute-start(f32[8,128]{1,0:T(8,128)S(1)} %slice_dynamic-update-slice_fusion.2), channel_id=1, source_target_pairs={{0,8},{1,17},{2,10},{3,19},{4,12},{5,21},{6,14},{7,23},{8,0},{9,25... | collective-permute-start | bytes 12296 | tf_op jit(solution)/shard_map/ppermute | solution.py:452
  37.5 4.0 %collective-permute-start.19 = (f32[8,128]{1,0:T(8,128)S(1)}, f32[8,128]{1,0:T(8,128)S(1)}, u32[]{:S(2)}, u32[]{:S(2)}) collective-permute-start(f32[8,128]{1,0:T(8,128)S(1)} %collective-permute-done.18.refs_7_), channel_id=1, source_target_pairs={{0,1},{1,0},{2,3},{3,2},{4,5},{5,4},{6,7},{7,6},{8,9},{9,8},{10,11... | collective-permute-start | bytes 12296 | tf_op jit(solution)/shard_map/ppermute | solution.py:453
  37.5 3.6 %collective-permute-start.15 = (f32[4,128]{1,0:T(4,128)S(1)}, f32[4,128]{1,0:T(4,128)S(1)}, u32[]{:S(2)}, u32[]{:S(2)}) collective-permute-start(f32[4,128]{1,0:T(4,128)S(1)} %get-tuple-element.88), channel_id=1, source_target_pairs={{0,2},{2,0},{4,6},{6,4},{8,10},{10,8},{12,14},{14,12},{16,18},{18,... | collective-permute-start | bytes 6152 | tf_op jit(solution)/shard_map/ppermute | solution.py:439
  37.9 3.6 %collective-permute-start.16 = (f32[4,128]{1,0:T(4,128)S(1)}, f32[4,128]{1,0:T(4,128)S(1)}, u32[]{:S(2)}, u32[]{:S(2)}) collective-permute-start(f32[4,128]{1,0:T(4,128)S(1)} %get-tuple-element.89), channel_id=1, source_target_pairs={{0,4},{2,6},{4,0},{6,2},{8,12},{10,14},{12,8},{14,10},{16,20},{18,... | collective-permute-start | bytes 6152 | tf_op jit(solution)/shard_map/ppermute | solution.py:439
  39.8 14.9 %copy-start.1 = (bf16[32,96,128]{2,1,0:T(8,128)(2,1)S(1)}, bf16[32,96,128]{2,1,0:T(8,128)(2,1)}, u32[]{:S(2)}) copy-start(bf16[32,96,128]{2,1,0:T(8,128)(2,1)} %refs_4_.3) | copy-start | bytes 2359300
  41.6 1.2 %collective-permute-start.22 = (f32[12,128]{1,0:T(8,128)S(1)}, f32[12,128]{1,0:T(8,128)S(1)}, u32[]{:S(2)}, u32[]{:S(2)}) collective-permute-start(f32[12,128]{1,0:T(8,128)S(1)} %get-tuple-element.98), channel_id=1, source_target_pairs={{0,1},{1,0},{2,3},{3,2},{4,5},{5,4},{6,7},{7,6},{8,9},{9,8},{10,11... | collective-permute-start | bytes 18440 | tf_op jit(solution)/shard_map/ppermute | solution.py:444
  42.9 3.6 %collective-permute-start.23 = (f32[8,128]{1,0:T(8,128)S(1)}, f32[8,128]{1,0:T(8,128)S(1)}, u32[]{:S(2)}, u32[]{:S(2)}) collective-permute-start(f32[8,128]{1,0:T(8,128)S(1)} %slice_dynamic-update-slice_fusion.1), channel_id=1, source_target_pairs={{0,8},{1,17},{2,10},{3,19},{4,12},{5,21},{6,14},{7,23},{8,0},{9,25... | collective-permute-start | bytes 12296 | tf_op jit(solution)/shard_map/ppermute | solution.py:452
  46.5 5.2 %collective-permute-start.24 = (f32[8,128]{1,0:T(8,128)S(1)}, f32[8,128]{1,0:T(8,128)S(1)}, u32[]{:S(2)}, u32[]{:S(2)}) collective-permute-start(f32[8,128]{1,0:T(8,128)S(1)} %collective-permute-done.23.refs_7_), channel_id=1, source_target_pairs={{0,1},{1,0},{2,3},{3,2},{4,5},{5,4},{6,7},{7,6},{8,9},{9,8},{10,11... | collective-permute-start | bytes 12296 | tf_op jit(solution)/shard_map/ppermute | solution.py:453
  46.5 4.5 %collective-permute-start.20 = (f32[4,128]{1,0:T(4,128)S(1)}, f32[4,128]{1,0:T(4,128)S(1)}, u32[]{:S(2)}, u32[]{:S(2)}) collective-permute-start(f32[4,128]{1,0:T(4,128)S(1)} %get-tuple-element.96), channel_id=1, source_target_pairs={{0,2},{2,0},{4,6},{6,4},{8,10},{10,8},{12,14},{14,12},{16,18},{18,... | collective-permute-start | bytes 6152 | tf_op jit(solution)/shard_map/ppermute | solution.py:439
  48.1 3.6 %collective-permute-start.21 = (f32[4,128]{1,0:T(4,128)S(1)}, f32[4,128]{1,0:T(4,128)S(1)}, u32[]{:S(2)}, u32[]{:S(2)}) collective-permute-start(f32[4,128]{1,0:T(4,128)S(1)} %get-tuple-element.97), channel_id=1, source_target_pairs={{0,4},{2,6},{4,0},{6,2},{8,12},{10,14},{12,8},{14,10},{16,20},{18,... | collective-permute-start | bytes 6152 | tf_op jit(solution)/shard_map/ppermute | solution.py:439
  51.9 1.2 %collective-permute-start.27 = (f32[12,128]{1,0:T(8,128)S(1)}, f32[12,128]{1,0:T(8,128)S(1)}, u32[]{:S(2)}, u32[]{:S(2)}) collective-permute-start(f32[12,128]{1,0:T(8,128)S(1)} %get-tuple-element.103), channel_id=1, source_target_pairs={{0,1},{1,0},{2,3},{3,2},{4,5},{5,4},{6,7},{7,6},{8,9},{9,8},{10,11... | collective-permute-start | bytes 18440 | tf_op jit(solution)/shard_map/ppermute | solution.py:444
  53.1 3.6 %collective-permute-start.28 = (f32[8,128]{1,0:T(8,128)S(1)}, f32[8,128]{1,0:T(8,128)S(1)}, u32[]{:S(2)}, u32[]{:S(2)}) collective-permute-start(f32[8,128]{1,0:T(8,128)S(1)} %slice_dynamic-update-slice_fusion), channel_id=1, source_target_pairs={{0,8},{1,17},{2,10},{3,19},{4,12},{5,21},{6,14},{7,23},{8,0},{9,25... | collective-permute-start | bytes 12296 | tf_op jit(solution)/shard_map/ppermute | solution.py:452
  56.8 6.6 %collective-permute-start.29 = (f32[8,128]{1,0:T(8,128)S(1)}, f32[8,128]{1,0:T(8,128)S(1)}, u32[]{:S(2)}, u32[]{:S(2)}) collective-permute-start(f32[8,128]{1,0:T(8,128)S(1)} %collective-permute-done.28.refs_15_), channel_id=1, source_target_pairs={{0,1},{1,0},{2,3},{3,2},{4,5},{5,4},{6,7},{7,6},{8,9},{9,8},{10,11... | collective-permute-start | bytes 12296 | tf_op jit(solution)/shard_map/ppermute | solution.py:453
  59.3 4.0 %collective-permute-start.25 = (f32[4,128]{1,0:T(4,128)S(1)}, f32[4,128]{1,0:T(4,128)S(1)}, u32[]{:S(2)}, u32[]{:S(2)}) collective-permute-start(f32[4,128]{1,0:T(4,128)S(1)} %get-tuple-element.101), channel_id=1, source_target_pairs={{0,2},{2,0},{4,6},{6,4},{8,10},{10,8},{12,14},{14,12},{16,18},{18,... | collective-permute-start | bytes 6152 | tf_op jit(solution)/shard_map/ppermute | solution.py:439
  59.7 3.6 %collective-permute-start.26 = (f32[4,128]{1,0:T(4,128)S(1)}, f32[4,128]{1,0:T(4,128)S(1)}, u32[]{:S(2)}, u32[]{:S(2)}) collective-permute-start(f32[4,128]{1,0:T(4,128)S(1)} %get-tuple-element.102), channel_id=1, source_target_pairs={{0,4},{2,6},{4,0},{6,2},{8,12},{10,14},{12,8},{14,10},{16,20},{18,... | collective-permute-start | bytes 6152 | tf_op jit(solution)/shard_map/ppermute | solution.py:439
  (5 other events, 30.6 us)

commit v5 on v4

--- a/solution.py
+++ b/solution.py
@@ -118,7 +118,7 @@
     write_pieces(sent, out_refs)
 
 
-def prepare(face, moves, columns_ref, couplings_ref, shifts_ref, place_ref, row_ref, hot_ref, wide_ref, shift_ref):
+def prepare(face, moves, columns_ref, couplings_ref, place_ref, row_ref, hot_ref, wide_ref):
     neighbours, own_rows = columns_ref.shape
     row_ref[...] = jnp.full((SUB, LANE), -1, i32)
     row_ref[0:neighbours, 0:own_rows] = columns_ref[...]
@@ -138,20 +138,18 @@
         hot_ref[k * own_rows : (k + 1) * own_rows, 0:LANE] = hot
         hot_ref[k * own_rows : (k + 1) * own_rows, LANE : 2 * LANE] = hot
         wide_ref[k] = couplings_ref[k].astype(f32)
-    for k in range(shift_ref.shape[0]):
-        shift_ref[k] = jnp.broadcast_to(shifts_ref[0:1, k : k + 1], (SUB, LANE))
 
 
 def matvec(blocks_ref, vector_ref, own_ref):
     sub = subs()
     for g in range(vector_ref.shape[0] // SUB):
-        high, low = two_parts(vector_ref[g * SUB : (g + 1) * SUB, :])
-        left = jnp.concatenate([high.astype(f32), low.astype(f32)], axis=0).astype(bf16)
+        parts = three_parts(vector_ref[g * SUB : (g + 1) * SUB, :])
+        left = jnp.concatenate([part.astype(f32) for part in parts], axis=0).astype(bf16)
         total = None
         for b in range(0, SUB, 2):
             start = (g * SUB + b) * LANE
             out = dot_nt(left, blocks_ref[start : start + 2 * LANE, :])
-            both = out[:SUB] + out[SUB:]
+            both = out[:SUB] + (out[SUB : 2 * SUB] + out[2 * SUB :])
             total = both[:, :LANE] if total is None else jnp.where(sub == b, both[:, :LANE], total)
             total = jnp.where(sub == b + 1, both[:, LANE:], total)
         own_ref[g * SUB : (g + 1) * SUB, :] = total
@@ -210,31 +208,40 @@
 
 
 def setup_body(face, moves, *refs):
-    columns_ref, couplings_ref, shifts_ref, place_ref, blocks_ref, vector_ref, send_ref, sent_ref = refs[:8]
-    own_ref, base_ref, hot_ref, wide_ref, send_hot_ref, send_wide_ref, shift_ref, row_ref = refs[8:]
-    prepare(face, moves, columns_ref, couplings_ref, shifts_ref, place_ref, row_ref, hot_ref, wide_ref, shift_ref)
+    columns_ref, couplings_ref, place_ref, own_ref, send_ref, sent_ref, shifts_ref = refs[:7]
+    base_ref, hot_ref, wide_ref, send_hot_ref, send_wide_ref, row_ref = refs[7:]
+    base_ref[...] = base_of(0, own_ref, send_ref, sent_ref, shifts_ref)
+    prepare(face, moves, columns_ref, couplings_ref, place_ref, row_ref, hot_ref, wide_ref)
     neighbours, rows = columns_ref.shape
     count = send_ref.shape[0]
     for k in range(neighbours):
         picked = dot(send_ref[...], hot_ref[k * rows : (k + 1) * rows, :])
         send_hot_ref[k * count : (k + 1) * count, :] = picked.astype(bf16)
         send_wide_ref[k] = dot(send_ref[...], couplings_ref[k])
+
+
+def shift_of(shifts_ref, k):
+    return shifts_ref[0:1, k : k + 1]
+
+
+def matvec_body(blocks_ref, vector_ref, own_ref):
     matvec(blocks_ref, vector_ref, own_ref)
-    base_ref[...] = take_rows(send_ref[...], own_ref[...]) - shift_ref[0, 0:1, :] * sent_ref[...]
-
-
-def matvec_body(k, blocks_ref, vector_ref, *refs):
-    if len(refs) == 1:
-        return matvec(blocks_ref, vector_ref, refs[0])
-    send_ref, sent_ref, shift_ref, own_ref, base_ref = refs
-    matvec(blocks_ref, vector_ref, own_ref)
-    base_ref[...] = take_rows(send_ref[...], own_ref[...]) - shift_ref[k, 0:1, :] * sent_ref[...]
-
-
-def sums_body(k, *refs):
-    vectors, sketch_ref, refs = refs[: k + 1], refs[k + 1], refs[k + 2 :]
-    packet = refs[0][...] if k else jnp.zeros((SUB, LANE), f32)
-    refs[-1][...] = statistics(k, vectors, sketch_ref, packet)
+
+
+def base_of(k, own_ref, send_ref, sent_ref, shifts_ref):
+    return take_rows(send_ref[...], own_ref[...]) - shift_of(shifts_ref, k) * sent_ref[...]
+
+
+def sums_body(k, final, *refs):
+    vectors, refs = refs[: k + 1], list(refs[k + 1 :])
+    if not final:
+        base_refs = [refs.pop(0) for _ in range(4)]
+        refs.pop()[...] = base_of(k, *base_refs)
+    sketch_ref, refs = refs[0], refs[1:]
+    packet = refs[0][...] if k > 1 else jnp.zeros((SUB, LANE), f32)
+    for newest in range(k if k > 1 else 0, k + 1):
+        packet = statistics(newest, vectors, sketch_ref, packet)
+    refs[-1][...] = packet
 
 
 def extend(places, vector_ref, halo_refs, extended_ref):
@@ -269,20 +276,21 @@
     write_pieces(sent, out_refs)
 
 
-def rest_body(k, own_ref, vector_ref, hot_ref, wide_ref, shift_ref, parts_ref, next_ref):
-    base = own_ref[...] - shift_ref[k, 0:1, :] * vector_ref[...]
+def rest_body(k, own_ref, vector_ref, hot_ref, wide_ref, shifts_ref, parts_ref, next_ref):
+    base = own_ref[...] - shift_of(shifts_ref, k) * vector_ref[...]
     next_ref[...] = coupled(base, hot_ref[...], wide_ref, parts_ref[...])
 
 
 def final_body(k, places, *refs):
-    own_ref, hot_ref, wide_ref, shift_ref, sketch_ref, packet_ref = refs[:6]
+    own_ref, hot_ref, wide_ref, shifts_ref, sketch_ref, packet_ref = refs[:6]
     vectors, refs = refs[6 : 7 + k], refs[7 + k :]
     halo_refs, (next_ref, folded_ref, extended_ref) = refs[: len(places)], refs[len(places) :]
     vector_ref = vectors[-1]
     parts = extend(places, vector_ref, halo_refs, extended_ref)
-    base = own_ref[...] - shift_ref[k, 0:1, :] * vector_ref[...]
-    next_ref[...] = coupled(base, hot_ref[...], wide_ref, parts)
-    packet = statistics(k + 1, [*vectors, next_ref], sketch_ref, packet_ref[...])
+    base = own_ref[...] - shift_of(shifts_ref, k) * vector_ref[...]
+    newest = coupled(base, hot_ref[...], wide_ref, parts)
+    next_ref[...] = newest
+    packet = statistics(k + 1, [*vectors, newest], sketch_ref, packet_ref[...])
     folded_ref[...] = (packet + pltpu.roll(pltpu.roll(packet, HALF, 0), FOLD, 1))[:HALF]
 
 
@@ -413,6 +421,7 @@
     sends = send_rows.shape[1]
     face = sends // (2 + levels)
     powers = shifts.shape[0]
+    shifts = shifts.reshape(1, powers)
     n = powers + 1
     sketches = sketch.shape[0]
     blocks = diag_blocks.reshape(rows * width, width)
@@ -477,10 +486,11 @@
     vectors = [start_vector]
     packet = []
 
-    def sums(packet):
+    def sums(packet, final):
         k = len(vectors) - 1
-        args = (*vectors, sketch, *packet)
-        return run(functools.partial(sums_body, k), [((SUB, LANE), f32)], args, (4_000_000, 2_000_000))
+        args = (*vectors, *(() if final else (own, send_ones, sent, shifts)), sketch, *packet)
+        outs = [((SUB, LANE), f32)] + ([] if final else [sent_out])
+        return run(functools.partial(sums_body, k, final), outs, args, (4_000_000, 2_000_000))
 
     rest = None
     for k in range(powers):
@@ -489,44 +499,29 @@
         if k:
             (vector,) = run(functools.partial(rest_body, k - 1), [vector_out], rest, (1_000_000, 1_000_000))
             vectors.append(vector)
+        (own,) = run(matvec_body, [vector_out], (blocks, vectors[-1]), (20_000_000, 4_000_000))
         if k == 0:
-            own, *base, neighbour_hot, wide, send_hot, send_wide, shift = run(
+            base, neighbour_hot, wide, send_hot, send_wide = run(
                 functools.partial(setup_body, face, moves),
                 [
-                    vector_out,
                     sent_out,
                     ((neighbours * rows, 2 * LANE), bf16),
                     ((neighbours, rows, width), f32),
                     ((neighbours * send_pad, 2 * LANE), bf16),
                     ((neighbours, send_pad, width), f32),
-                    ((powers, SUB, LANE), f32),
                 ],
-                (
-                    columns.T,
-                    couplings.transpose(1, 0, 2),
-                    shifts.reshape(1, powers),
-                    place,
-                    blocks,
-                    start_vector,
-                    send_ones,
-                    sent,
-                ),
-                cost=(20_000_000, 4_000_000),
+                (columns.T, couplings.transpose(1, 0, 2), place, own, send_ones, sent, shifts),
+                cost=(4_000_000, 2_000_000),
                 scratch=[pltpu.VMEM((SUB, LANE), i32)],
             )
         else:
-            own, *base = run(
-                functools.partial(matvec_body, k),
-                [vector_out] if final else [vector_out, sent_out],
-                (blocks, vectors[-1], *(() if final else (send_ones, sent, shift))),
-                (20_000_000, 4_000_000),
-            )
-        packet = sums(packet)
+            packet, base = sums(packet, final) if not final else (*sums(packet, final), None)
+            packet = [packet]
         if final:
             vector, packet = run(
                 functools.partial(final_body, k, places),
                 [vector_out, ((HALF, LANE), f32)],
-                (own, neighbour_hot, wide, shift, sketch, *packet, *vectors, *received),
+                (own, neighbour_hot, wide, shifts, sketch, *packet, *vectors, *received),
                 cost=(4_000_000, 2_000_000),
                 scratch=extended,
             )
@@ -536,13 +531,13 @@
             parts, *outgoing = run(
                 functools.partial(sends_body, places, keep),
                 [((2 * LANE, width), bf16)] + ([sent_out] if keep else []) + piece_outs,
-                (*base, vectors[-1], send_hot, send_wide, *received),
+                (base, vectors[-1], send_hot, send_wide, *received),
                 cost=(1_000_000, 1_000_000),
                 scratch=extended,
             )
             if keep:
                 sent, *outgoing = outgoing
-            rest = (own, vectors[-1], neighbour_hot, wide, shift, parts)
+            rest = (own, vectors[-1], neighbour_hot, wide, shifts, parts)
     everyone = ("dom", "col")
     packets = lax.all_to_all(jnp.tile(packet, (dom * col, 1)), everyone, 0, 0, tiled=True)
     orthonormal, factor, sketch_factor = run(

time: 79.3 us -> 76.8 us (0.968)
  waiting for transfers between devices: 21.1 us -> 19.4 us
  starting transfers between devices: 27.9 us -> 26.7 us
    ppermute x12, waiting for transfers between devices: 3.55 us -> 1.03 us  [with_partner(): return lax.ppermute(piece, 'dom', [(i, i ^ 1 << level) for i in range(dom)])]
    ppermute x12, starting transfers between devices: 15.7 us -> 14.7 us  [with_partner(): return lax.ppermute(piece, 'dom', [(i, i ^ 1 << level) for i in range(dom)])]
    ppermute x6, waiting for transfers between devices: 10.9 us -> 11.7 us  [exchange_relay(): pair = lax.ppermute(pair, ('dom', 'col'), far_pairs)]
  transfers between devices with their start and end apart: 30 -> 30, of which waited for: 20 -> 17; matrix products, arithmetic and copies ran while one was open for 0% -> 0% of each run, Pallas kernels for 14% -> 16%
where the time goes in v5:
time: 76.8 us; the launch traced here: 76.6 us
  starting transfers between devices  26.7 us (35%)
  waiting for transfers between devices  19.4 us (25%)
  Pallas kernels  15.8 us (21%)
  blocking collectives  12.9 us (17%)
  between operations  0.96 us (1%)
  local copies, waits for them, and re-layouts  0.89 us (1%)
    pallas_call x26, Pallas kernels, run(): pl.pallas_call(body, out_shape=[jax.ShapeDtypeStruct(shape, dtype) for sh...  15.8 us
    ppermute x12, starting transfers between devices, with_partner(): return lax.ppermute(piece, 'dom', [(i, i ^ 1 << level) for i in range(dom)])  14.7 us
    all_to_all x1, blocking collectives, shards(): lax.all_to_all(jnp.tile(packet, (dom * col, 1)), everyone, 0, 0, tiled=True)  12.9 us
    ppermute x6, waiting for transfers between devices, exchange_relay(): pair = lax.ppermute(pair, ('dom', 'col'), far_pairs)  11.7 us
    ppermute x6, starting transfers between devices, exchange_relay(): pair = lax.ppermute(pair, ('dom', 'col'), far_pairs)  10.8 us
    ppermute x6, waiting for transfers between devices, exchange_relay(): side = lax.ppermute(side, 'col', swapped)  6.62 us
  transfers between devices with their start and end apart: 30, of which 17 were waited for; matrix products, arithmetic and copies ran while one was open for 0% of the time, Pallas kernels for 16%

profile of v5, /device:TPU:0, one launch (start us, length us, event | category | flops | bytes accessed | tf_op | source)
XLA Modules:
  0.0 76.6 jit_solution(3714120406485112786)
XLA Ops:
  3.2 2.9 %collective-permute-start.3 = (f32[8,128]{1,0:T(8,128)S(1)}, f32[8,128]{1,0:T(8,128)S(1)}, u32[]{:S(2)}, u32[]{:S(2)}) collective-permute-start(f32[8,128]{1,0:T(8,128)S(1)} %slice_dynamic-update-slice_fusion.5), channel_id=1, source_target_pairs={{0,8},{1,17},{2,10},{3,19},{4,12},{5,21},{6,14},{7,23},{8,0},{9,25... | collective-permute-start | bytes 12296 | tf_op jit(solution)/shard_map/ppermute | solution.py:461
  6.1 1.6 %collective-permute-done.3.refs_7_ = f32[8,128]{1,0:T(8,128)S(1)} collective-permute-done((f32[8,128]{1,0:T(8,128)S(1)}, f32[8,128]{1,0:T(8,128)S(1)}, u32[]{:S(2)}, u32[]{:S(2)}) %collective-permute-start.3) | collective-permute-done | bytes 4128 | tf_op jit(solution)/shard_map/ppermute | solution.py:461
  8.0 1.6 %collective-permute-start = (f32[4,128]{1,0:T(4,128)S(1)}, f32[4,128]{1,0:T(4,128)S(1)}, u32[]{:S(2)}, u32[]{:S(2)}) collective-permute-start(f32[4,128]{1,0:T(4,128)S(1)} %get-tuple-element.60), channel_id=1, source_target_pairs={{0,2},{2,0},{4,6},{6,4},{8,10},{10,8},{12,14},{14,12},{16,18},{18,... | collective-permute-start | bytes 6152 | tf_op jit(solution)/shard_map/ppermute | solution.py:448
  9.6 1.5 %collective-permute-start.1 = (f32[4,128]{1,0:T(4,128)S(1)}, f32[4,128]{1,0:T(4,128)S(1)}, u32[]{:S(2)}, u32[]{:S(2)}) collective-permute-start(f32[4,128]{1,0:T(4,128)S(1)} %get-tuple-element.61), channel_id=1, source_target_pairs={{0,4},{2,6},{4,0},{6,2},{8,12},{10,14},{12,8},{14,10},{16,20},{18,... | collective-permute-start | bytes 6152 | tf_op jit(solution)/shard_map/ppermute | solution.py:448
  13.5 1.2 %collective-permute-done.7.refs_6_ = f32[12,128]{1,0:T(8,128)S(1)} collective-permute-done((f32[12,128]{1,0:T(8,128)S(1)}, f32[12,128]{1,0:T(8,128)S(1)}, u32[]{:S(2)}, u32[]{:S(2)}) %collective-permute-start.7) | collective-permute-done | bytes 6176 | tf_op jit(solution)/shard_map/ppermute | solution.py:453
  14.6 1.6 %collective-permute-start.8 = (f32[8,128]{1,0:T(8,128)S(1)}, f32[8,128]{1,0:T(8,128)S(1)}, u32[]{:S(2)}, u32[]{:S(2)}) collective-permute-start(f32[8,128]{1,0:T(8,128)S(1)} %slice_dynamic-update-slice_fusion.4), channel_id=1, source_target_pairs={{0,8},{1,17},{2,10},{3,19},{4,12},{5,21},{6,14},{7,23},{8,0},{9,25... | collective-permute-start | bytes 12296 | tf_op jit(solution)/shard_map/ppermute | solution.py:461
  16.2 2.0 %collective-permute-done.8.refs_7_ = f32[8,128]{1,0:T(8,128)S(1)} collective-permute-done((f32[8,128]{1,0:T(8,128)S(1)}, f32[8,128]{1,0:T(8,128)S(1)}, u32[]{:S(2)}, u32[]{:S(2)}) %collective-permute-start.8) | collective-permute-done | bytes 4128 | tf_op jit(solution)/shard_map/ppermute | solution.py:461
  18.6 1.7 %collective-permute-start.6 = (f32[4,128]{1,0:T(4,128)S(1)}, f32[4,128]{1,0:T(4,128)S(1)}, u32[]{:S(2)}, u32[]{:S(2)}) collective-permute-start(f32[4,128]{1,0:T(4,128)S(1)} %get-tuple-element.68), channel_id=1, source_target_pairs={{0,4},{2,6},{4,0},{6,2},{8,12},{10,14},{12,8},{14,10},{16,20},{18,... | collective-permute-start | bytes 6152 | tf_op jit(solution)/shard_map/ppermute | solution.py:448
  20.5 1.1 %shard_map.100.refs_2_.own_ref = f32[96,128]{1,0:T(8,128)S(1)} custom-call(bf16[12288,128]{1,0:T(8,128)(2,1)S(1)} %bitcast.6, f32[96,128]{1,0:T(8,128)S(1)} %shard_map.99.vector_ref.refs_1_.refs_7_), custom_call_target="tpu_custom_call" | custom-call | flops 20000000 | bytes 4000000 | tf_op jit(solution)/shard_map/pallas_call | solution.py:23
  22.8 1.2 %collective-permute-done.12.refs_6_ = f32[12,128]{1,0:T(8,128)S(1)} collective-permute-done((f32[12,128]{1,0:T(8,128)S(1)}, f32[12,128]{1,0:T(8,128)S(1)}, u32[]{:S(2)}, u32[]{:S(2)}) %collective-permute-start.12) | collective-permute-done | bytes 6176 | tf_op jit(solution)/shard_map/ppermute | solution.py:453
  24.0 1.6 %collective-permute-start.13 = (f32[8,128]{1,0:T(8,128)S(1)}, f32[8,128]{1,0:T(8,128)S(1)}, u32[]{:S(2)}, u32[]{:S(2)}) collective-permute-start(f32[8,128]{1,0:T(8,128)S(1)} %slice_dynamic-update-slice_fusion.3), channel_id=1, source_target_pairs={{0,8},{1,17},{2,10},{3,19},{4,12},{5,21},{6,14},{7,23},{8,0},{9,25... | collective-permute-start | bytes 12296 | tf_op jit(solution)/shard_map/ppermute | solution.py:461
  25.5 2.0 %collective-permute-done.13.refs_7_ = f32[8,128]{1,0:T(8,128)S(1)} collective-permute-done((f32[8,128]{1,0:T(8,128)S(1)}, f32[8,128]{1,0:T(8,128)S(1)}, u32[]{:S(2)}, u32[]{:S(2)}) %collective-permute-start.13) | collective-permute-done | bytes 4128 | tf_op jit(solution)/shard_map/ppermute | solution.py:461
  27.6 1.5 %collective-permute-start.10 = (f32[4,128]{1,0:T(4,128)S(1)}, f32[4,128]{1,0:T(4,128)S(1)}, u32[]{:S(2)}, u32[]{:S(2)}) collective-permute-start(f32[4,128]{1,0:T(4,128)S(1)} %get-tuple-element.75), channel_id=1, source_target_pairs={{0,2},{2,0},{4,6},{6,4},{8,10},{10,8},{12,14},{14,12},{16,18},{18,... | collective-permute-start | bytes 6152 | tf_op jit(solution)/shard_map/ppermute | solution.py:448
  29.1 1.3 %collective-permute-start.11 = (f32[4,128]{1,0:T(4,128)S(1)}, f32[4,128]{1,0:T(4,128)S(1)}, u32[]{:S(2)}, u32[]{:S(2)}) collective-permute-start(f32[4,128]{1,0:T(4,128)S(1)} %get-tuple-element.76), channel_id=1, source_target_pairs={{0,4},{2,6},{4,0},{6,2},{8,12},{10,14},{12,8},{14,10},{16,20},{18,... | collective-permute-start | bytes 6152 | tf_op jit(solution)/shard_map/ppermute | solution.py:448
  30.7 1.1 %shard_map.104.refs_3_.own_ref = f32[96,128]{1,0:T(8,128)S(1)} custom-call(bf16[12288,128]{1,0:T(8,128)(2,1)S(1)} %bitcast.7, f32[96,128]{1,0:T(8,128)S(1)} %shard_map.103.vector_ref.refs_2_.refs_1_.refs_8_), custom_call_target="tpu_custom_call" | custom-call | flops 20000000 | bytes 4000000 | tf_op jit(solution)/shard_map/pallas_call | solution.py:23
  32.9 1.2 %collective-permute-done.17.refs_6_ = f32[12,128]{1,0:T(8,128)S(1)} collective-permute-done((f32[12,128]{1,0:T(8,128)S(1)}, f32[12,128]{1,0:T(8,128)S(1)}, u32[]{:S(2)}, u32[]{:S(2)}) %collective-permute-start.17) | collective-permute-done | bytes 6176 | tf_op jit(solution)/shard_map/ppermute | solution.py:453
  34.1 1.6 %collective-permute-start.18 = (f32[8,128]{1,0:T(8,128)S(1)}, f32[8,128]{1,0:T(8,128)S(1)}, u32[]{:S(2)}, u32[]{:S(2)}) collective-permute-start(f32[8,128]{1,0:T(8,128)S(1)} %slice_dynamic-update-slice_fusion.2), channel_id=1, source_target_pairs={{0,8},{1,17},{2,10},{3,19},{4,12},{5,21},{6,14},{7,23},{8,0},{9,25... | collective-permute-start | bytes 12296 | tf_op jit(solution)/shard_map/ppermute | solution.py:461
  35.7 2.0 %collective-permute-done.18.refs_7_ = f32[8,128]{1,0:T(8,128)S(1)} collective-permute-done((f32[8,128]{1,0:T(8,128)S(1)}, f32[8,128]{1,0:T(8,128)S(1)}, u32[]{:S(2)}, u32[]{:S(2)}) %collective-permute-start.18) | collective-permute-done | bytes 4128 | tf_op jit(solution)/shard_map/ppermute | solution.py:461
  38.2 1.4 %collective-permute-start.16 = (f32[4,128]{1,0:T(4,128)S(1)}, f32[4,128]{1,0:T(4,128)S(1)}, u32[]{:S(2)}, u32[]{:S(2)}) collective-permute-start(f32[4,128]{1,0:T(4,128)S(1)} %get-tuple-element.84), channel_id=1, source_target_pairs={{0,4},{2,6},{4,0},{6,2},{8,12},{10,14},{12,8},{14,10},{16,20},{18,... | collective-permute-start | bytes 6152 | tf_op jit(solution)/shard_map/ppermute | solution.py:448
  42.1 1.2 %collective-permute-done.22.refs_6_ = f32[12,128]{1,0:T(8,128)S(1)} collective-permute-done((f32[12,128]{1,0:T(8,128)S(1)}, f32[12,128]{1,0:T(8,128)S(1)}, u32[]{:S(2)}, u32[]{:S(2)}) %collective-permute-start.22) | collective-permute-done | bytes 6176 | tf_op jit(solution)/shard_map/ppermute | solution.py:453
  43.2 1.6 %collective-permute-start.23 = (f32[8,128]{1,0:T(8,128)S(1)}, f32[8,128]{1,0:T(8,128)S(1)}, u32[]{:S(2)}, u32[]{:S(2)}) collective-permute-start(f32[8,128]{1,0:T(8,128)S(1)} %slice_dynamic-update-slice_fusion.1), channel_id=1, source_target_pairs={{0,8},{1,17},{2,10},{3,19},{4,12},{5,21},{6,14},{7,23},{8,0},{9,25... | collective-permute-start | bytes 12296 | tf_op jit(solution)/shard_map/ppermute | solution.py:461
  44.8 2.0 %collective-permute-done.23.refs_7_ = f32[8,128]{1,0:T(8,128)S(1)} collective-permute-done((f32[8,128]{1,0:T(8,128)S(1)}, f32[8,128]{1,0:T(8,128)S(1)}, u32[]{:S(2)}, u32[]{:S(2)}) %collective-permute-start.23) | collective-permute-done | bytes 4128 | tf_op jit(solution)/shard_map/ppermute | solution.py:461
  46.9 1.5 %collective-permute-start.20 = (f32[4,128]{1,0:T(4,128)S(1)}, f32[4,128]{1,0:T(4,128)S(1)}, u32[]{:S(2)}, u32[]{:S(2)}) collective-permute-start(f32[4,128]{1,0:T(4,128)S(1)} %get-tuple-element.91), channel_id=1, source_target_pairs={{0,2},{2,0},{4,6},{6,4},{8,10},{10,8},{12,14},{14,12},{16,18},{18,... | collective-permute-start | bytes 6152 | tf_op jit(solution)/shard_map/ppermute | solution.py:448
  48.4 1.4 %collective-permute-start.21 = (f32[4,128]{1,0:T(4,128)S(1)}, f32[4,128]{1,0:T(4,128)S(1)}, u32[]{:S(2)}, u32[]{:S(2)}) collective-permute-start(f32[4,128]{1,0:T(4,128)S(1)} %get-tuple-element.92), channel_id=1, source_target_pairs={{0,4},{2,6},{4,0},{6,2},{8,12},{10,14},{12,8},{14,10},{16,20},{18,... | collective-permute-start | bytes 6152 | tf_op jit(solution)/shard_map/ppermute | solution.py:448
  52.2 1.2 %collective-permute-done.27.refs_14_ = f32[12,128]{1,0:T(8,128)S(1)} collective-permute-done((f32[12,128]{1,0:T(8,128)S(1)}, f32[12,128]{1,0:T(8,128)S(1)}, u32[]{:S(2)}, u32[]{:S(2)}) %collective-permute-start.27) | collective-permute-done | bytes 6176 | tf_op jit(solution)/shard_map/ppermute | solution.py:453
  53.4 1.6 %collective-permute-start.28 = (f32[8,128]{1,0:T(8,128)S(1)}, f32[8,128]{1,0:T(8,128)S(1)}, u32[]{:S(2)}, u32[]{:S(2)}) collective-permute-start(f32[8,128]{1,0:T(8,128)S(1)} %slice_dynamic-update-slice_fusion), channel_id=1, source_target_pairs={{0,8},{1,17},{2,10},{3,19},{4,12},{5,21},{6,14},{7,23},{8,0},{9,25... | collective-permute-start | bytes 12296 | tf_op jit(solution)/shard_map/ppermute | solution.py:461
  55.0 2.0 %collective-permute-done.28.refs_15_ = f32[8,128]{1,0:T(8,128)S(1)} collective-permute-done((f32[8,128]{1,0:T(8,128)S(1)}, f32[8,128]{1,0:T(8,128)S(1)}, u32[]{:S(2)}, u32[]{:S(2)}) %collective-permute-start.28) | collective-permute-done | bytes 4128 | tf_op jit(solution)/shard_map/ppermute | solution.py:461
  57.5 1.4 %collective-permute-start.26 = (f32[4,128]{1,0:T(4,128)S(1)}, f32[4,128]{1,0:T(4,128)S(1)}, u32[]{:S(2)}, u32[]{:S(2)}) collective-permute-start(f32[4,128]{1,0:T(4,128)S(1)} %get-tuple-element.98), channel_id=1, source_target_pairs={{0,4},{2,6},{4,0},{6,2},{8,12},{10,14},{12,8},{14,10},{16,20},{18,... | collective-permute-start | bytes 6152 | tf_op jit(solution)/shard_map/ppermute | solution.py:448
  59.8 1.1 %shard_map.116.refs_0_ = f32[96,128]{1,0:T(8,128)S(1)} custom-call(bf16[12288,128]{1,0:T(8,128)(2,1)S(1)} %bitcast.10, f32[96,128]{1,0:T(8,128)S(1)} %shard_map.115.vector_ref.refs_5_.refs_11_), custom_call_target="tpu_custom_call" | custom-call | flops 20000000 | bytes 4000000 | tf_op jit(solution)/shard_map/pallas_call | solution.py:23
  61.1 1.2 %shard_map.118 = (f32[96,128]{1,0:T(8,128)S(1)}, f32[4,128]{1,0:T(4,128)S(1)}) custom-call(f32[96,128]{1,0:T(8,128)S(1)} %shard_map.116.refs_0_, bf16[576,256]{1,0:T(8,128)(2,1)S(1)} %get-tuple-element.55.hot_ref.refs_1_, f32[6,96,128]{2,1,0:T(8,128)S(1)} %get-tuple-element.56.wide_ref.refs_2_, f32[1,6]{1,0:T(1,128)S(1)} %bitcast.23, ...), custom_call_target="tpu_custom_call" | custom-call | flops 4000000 | bytes 2000000 | tf_op jit(solution)/shard_map/pallas_call | solution.py:23
  62.3 12.9 %all_to_all.8 = f32[32,4,128]{2,1,0:T(4,128)S(1)} all-to-all(f32[32,4,128]{2,1,0:T(4,128)S(1)} %tile.2), channel_id=1, replica_groups=mesh['dom'=16,'col'=2] {'dom','col'}, dimensions={0} | all-to-all | bytes 131072 | tf_op jit(solution)/shard_map/all_to_all | solution.py:542
  75.2 1.4 %shard_map.119 = (f32[7,96,128]{2,1,0:T(8,128)}, f32[7,7]{1,0:T(8,128)}, f32[7,7]{1,0:T(8,128)}) custom-call(f32[128,128]{1,0:T(8,128)S(1)} %bitcast.11, f32[96,128]{1,0:T(8,128)S(1)} %copy-done.2, f32[96,128]{1,0:T(8,128)S(1)} %shard_map.99.vector_ref.refs_1_.refs_7_, f32[96,128]{1,0:T(8,128)S(1)} %shard_map.103.vector_ref.refs_2_.refs_1_.refs_8_, ...), custom_call_target="tpu_custom_call" | custom-call | flops 5000000 | bytes 1000000 | tf_op jit(solution)/shard_map/pallas_call | solution.py:23
  (77 shorter events, 15.2 us)
Async XLA Ops:
  1.8 10.6 %copy-start.4 = (f32[6]{0:T(128)S(1)}, f32[6]{0:T(128)}, u32[]{:S(2)}) copy-start(f32[6]{0:T(128)} %param.11) | copy-start | bytes 76
  1.8 1.4 %collective-permute-start.2 = (f32[12,128]{1,0:T(8,128)S(1)}, f32[12,128]{1,0:T(8,128)S(1)}, u32[]{:S(2)}, u32[]{:S(2)}) collective-permute-start(f32[12,128]{1,0:T(8,128)S(1)} %get-tuple-element.62), channel_id=1, source_target_pairs={{0,1},{1,0},{2,3},{3,2},{4,5},{5,4},{6,7},{7,6},{8,9},{9,8},{10,11... | collective-permute-start | bytes 18440 | tf_op jit(solution)/shard_map/ppermute | solution.py:453
  3.2 4.5 %collective-permute-start.3 = (f32[8,128]{1,0:T(8,128)S(1)}, f32[8,128]{1,0:T(8,128)S(1)}, u32[]{:S(2)}, u32[]{:S(2)}) collective-permute-start(f32[8,128]{1,0:T(8,128)S(1)} %slice_dynamic-update-slice_fusion.5), channel_id=1, source_target_pairs={{0,8},{1,17},{2,10},{3,19},{4,12},{5,21},{6,14},{7,23},{8,0},{9,25... | collective-permute-start | bytes 12296 | tf_op jit(solution)/shard_map/ppermute | solution.py:461
  7.7 5.5 %collective-permute-start.4 = (f32[8,128]{1,0:T(8,128)S(1)}, f32[8,128]{1,0:T(8,128)S(1)}, u32[]{:S(2)}, u32[]{:S(2)}) collective-permute-start(f32[8,128]{1,0:T(8,128)S(1)} %collective-permute-done.3.refs_7_), channel_id=1, source_target_pairs={{0,1},{1,0},{2,3},{3,2},{4,5},{5,4},{6,7},{7,6},{8,9},{9,8},{10,11... | collective-permute-start | bytes 12296 | tf_op jit(solution)/shard_map/ppermute | solution.py:462
  8.0 4.7 %collective-permute-start = (f32[4,128]{1,0:T(4,128)S(1)}, f32[4,128]{1,0:T(4,128)S(1)}, u32[]{:S(2)}, u32[]{:S(2)}) collective-permute-start(f32[4,128]{1,0:T(4,128)S(1)} %get-tuple-element.60), channel_id=1, source_target_pairs={{0,2},{2,0},{4,6},{6,4},{8,10},{10,8},{12,14},{14,12},{16,18},{18,... | collective-permute-start | bytes 6152 | tf_op jit(solution)/shard_map/ppermute | solution.py:448
  9.6 3.6 %collective-permute-start.1 = (f32[4,128]{1,0:T(4,128)S(1)}, f32[4,128]{1,0:T(4,128)S(1)}, u32[]{:S(2)}, u32[]{:S(2)}) collective-permute-start(f32[4,128]{1,0:T(4,128)S(1)} %get-tuple-element.61), channel_id=1, source_target_pairs={{0,4},{2,6},{4,0},{6,2},{8,12},{10,14},{12,8},{14,10},{16,20},{18,... | collective-permute-start | bytes 6152 | tf_op jit(solution)/shard_map/ppermute | solution.py:448
  11.1 10.6 %copy-start.1 = (bf16[32,96,128]{2,1,0:T(8,128)(2,1)S(1)}, bf16[32,96,128]{2,1,0:T(8,128)(2,1)}, u32[]{:S(2)}) copy-start(bf16[32,96,128]{2,1,0:T(8,128)(2,1)} %refs_4_.1) | copy-start | bytes 2359300
  13.4 1.2 %collective-permute-start.7 = (f32[12,128]{1,0:T(8,128)S(1)}, f32[12,128]{1,0:T(8,128)S(1)}, u32[]{:S(2)}, u32[]{:S(2)}) collective-permute-start(f32[12,128]{1,0:T(8,128)S(1)} %get-tuple-element.69), channel_id=1, source_target_pairs={{0,1},{1,0},{2,3},{3,2},{4,5},{5,4},{6,7},{7,6},{8,9},{9,8},{10,11... | collective-permute-start | bytes 18440 | tf_op jit(solution)/shard_map/ppermute | solution.py:453
  14.6 3.6 %collective-permute-start.8 = (f32[8,128]{1,0:T(8,128)S(1)}, f32[8,128]{1,0:T(8,128)S(1)}, u32[]{:S(2)}, u32[]{:S(2)}) collective-permute-start(f32[8,128]{1,0:T(8,128)S(1)} %slice_dynamic-update-slice_fusion.4), channel_id=1, source_target_pairs={{0,8},{1,17},{2,10},{3,19},{4,12},{5,21},{6,14},{7,23},{8,0},{9,25... | collective-permute-start | bytes 12296 | tf_op jit(solution)/shard_map/ppermute | solution.py:461
  18.2 4.3 %collective-permute-start.9 = (f32[8,128]{1,0:T(8,128)S(1)}, f32[8,128]{1,0:T(8,128)S(1)}, u32[]{:S(2)}, u32[]{:S(2)}) collective-permute-start(f32[8,128]{1,0:T(8,128)S(1)} %collective-permute-done.8.refs_7_), channel_id=1, source_target_pairs={{0,1},{1,0},{2,3},{3,2},{4,5},{5,4},{6,7},{7,6},{8,9},{9,8},{10,11... | collective-permute-start | bytes 12296 | tf_op jit(solution)/shard_map/ppermute | solution.py:462
  18.3 4.3 %collective-permute-start.5 = (f32[4,128]{1,0:T(4,128)S(1)}, f32[4,128]{1,0:T(4,128)S(1)}, u32[]{:S(2)}, u32[]{:S(2)}) collective-permute-start(f32[4,128]{1,0:T(4,128)S(1)} %get-tuple-element.67), channel_id=1, source_target_pairs={{0,2},{2,0},{4,6},{6,4},{8,10},{10,8},{12,14},{14,12},{16,18},{18,... | collective-permute-start | bytes 6152 | tf_op jit(solution)/shard_map/ppermute | solution.py:448
  18.6 3.9 %collective-permute-start.6 = (f32[4,128]{1,0:T(4,128)S(1)}, f32[4,128]{1,0:T(4,128)S(1)}, u32[]{:S(2)}, u32[]{:S(2)}) collective-permute-start(f32[4,128]{1,0:T(4,128)S(1)} %get-tuple-element.68), channel_id=1, source_target_pairs={{0,4},{2,6},{4,0},{6,2},{8,12},{10,14},{12,8},{14,10},{16,20},{18,... | collective-permute-start | bytes 6152 | tf_op jit(solution)/shard_map/ppermute | solution.py:448
  22.7 1.2 %collective-permute-start.12 = (f32[12,128]{1,0:T(8,128)S(1)}, f32[12,128]{1,0:T(8,128)S(1)}, u32[]{:S(2)}, u32[]{:S(2)}) collective-permute-start(f32[12,128]{1,0:T(8,128)S(1)} %get-tuple-element.77), channel_id=1, source_target_pairs={{0,1},{1,0},{2,3},{3,2},{4,5},{5,4},{6,7},{7,6},{8,9},{9,8},{10,11... | collective-permute-start | bytes 18440 | tf_op jit(solution)/shard_map/ppermute | solution.py:453
  24.0 3.6 %collective-permute-start.13 = (f32[8,128]{1,0:T(8,128)S(1)}, f32[8,128]{1,0:T(8,128)S(1)}, u32[]{:S(2)}, u32[]{:S(2)}) collective-permute-start(f32[8,128]{1,0:T(8,128)S(1)} %slice_dynamic-update-slice_fusion.3), channel_id=1, source_target_pairs={{0,8},{1,17},{2,10},{3,19},{4,12},{5,21},{6,14},{7,23},{8,0},{9,25... | collective-permute-start | bytes 12296 | tf_op jit(solution)/shard_map/ppermute | solution.py:461
  27.6 5.1 %collective-permute-start.14 = (f32[8,128]{1,0:T(8,128)S(1)}, f32[8,128]{1,0:T(8,128)S(1)}, u32[]{:S(2)}, u32[]{:S(2)}) collective-permute-start(f32[8,128]{1,0:T(8,128)S(1)} %collective-permute-done.13.refs_7_), channel_id=1, source_target_pairs={{0,1},{1,0},{2,3},{3,2},{4,5},{5,4},{6,7},{7,6},{8,9},{9,8},{10,11... | collective-permute-start | bytes 12296 | tf_op jit(solution)/shard_map/ppermute | solution.py:462
  27.6 4.9 %collective-permute-start.10 = (f32[4,128]{1,0:T(4,128)S(1)}, f32[4,128]{1,0:T(4,128)S(1)}, u32[]{:S(2)}, u32[]{:S(2)}) collective-permute-start(f32[4,128]{1,0:T(4,128)S(1)} %get-tuple-element.75), channel_id=1, source_target_pairs={{0,2},{2,0},{4,6},{6,4},{8,10},{10,8},{12,14},{14,12},{16,18},{18,... | collective-permute-start | bytes 6152 | tf_op jit(solution)/shard_map/ppermute | solution.py:448
  29.1 3.6 %collective-permute-start.11 = (f32[4,128]{1,0:T(4,128)S(1)}, f32[4,128]{1,0:T(4,128)S(1)}, u32[]{:S(2)}, u32[]{:S(2)}) collective-permute-start(f32[4,128]{1,0:T(4,128)S(1)} %get-tuple-element.76), channel_id=1, source_target_pairs={{0,4},{2,6},{4,0},{6,2},{8,12},{10,14},{12,8},{14,10},{16,20},{18,... | collective-permute-start | bytes 6152 | tf_op jit(solution)/shard_map/ppermute | solution.py:448
  32.8 1.2 %collective-permute-start.17 = (f32[12,128]{1,0:T(8,128)S(1)}, f32[12,128]{1,0:T(8,128)S(1)}, u32[]{:S(2)}, u32[]{:S(2)}) collective-permute-start(f32[12,128]{1,0:T(8,128)S(1)} %get-tuple-element.85), channel_id=1, source_target_pairs={{0,1},{1,0},{2,3},{3,2},{4,5},{5,4},{6,7},{7,6},{8,9},{9,8},{10,11... | collective-permute-start | bytes 18440 | tf_op jit(solution)/shard_map/ppermute | solution.py:453
  34.1 3.6 %collective-permute-start.18 = (f32[8,128]{1,0:T(8,128)S(1)}, f32[8,128]{1,0:T(8,128)S(1)}, u32[]{:S(2)}, u32[]{:S(2)}) collective-permute-start(f32[8,128]{1,0:T(8,128)S(1)} %slice_dynamic-update-slice_fusion.2), channel_id=1, source_target_pairs={{0,8},{1,17},{2,10},{3,19},{4,12},{5,21},{6,14},{7,23},{8,0},{9,25... | collective-permute-start | bytes 12296 | tf_op jit(solution)/shard_map/ppermute | solution.py:461
  37.7 4.1 %collective-permute-start.19 = (f32[8,128]{1,0:T(8,128)S(1)}, f32[8,128]{1,0:T(8,128)S(1)}, u32[]{:S(2)}, u32[]{:S(2)}) collective-permute-start(f32[8,128]{1,0:T(8,128)S(1)} %collective-permute-done.18.refs_7_), channel_id=1, source_target_pairs={{0,1},{1,0},{2,3},{3,2},{4,5},{5,4},{6,7},{7,6},{8,9},{9,8},{10,11... | collective-permute-start | bytes 12296 | tf_op jit(solution)/shard_map/ppermute | solution.py:462
  37.7 4.0 %collective-permute-start.15 = (f32[4,128]{1,0:T(4,128)S(1)}, f32[4,128]{1,0:T(4,128)S(1)}, u32[]{:S(2)}, u32[]{:S(2)}) collective-permute-start(f32[4,128]{1,0:T(4,128)S(1)} %get-tuple-element.83), channel_id=1, source_target_pairs={{0,2},{2,0},{4,6},{6,4},{8,10},{10,8},{12,14},{14,12},{16,18},{18,... | collective-permute-start | bytes 6152 | tf_op jit(solution)/shard_map/ppermute | solution.py:448
  38.2 3.6 %collective-permute-start.16 = (f32[4,128]{1,0:T(4,128)S(1)}, f32[4,128]{1,0:T(4,128)S(1)}, u32[]{:S(2)}, u32[]{:S(2)}) collective-permute-start(f32[4,128]{1,0:T(4,128)S(1)} %get-tuple-element.84), channel_id=1, source_target_pairs={{0,4},{2,6},{4,0},{6,2},{8,12},{10,14},{12,8},{14,10},{16,20},{18,... | collective-permute-start | bytes 6152 | tf_op jit(solution)/shard_map/ppermute | solution.py:448
  42.0 1.2 %collective-permute-start.22 = (f32[12,128]{1,0:T(8,128)S(1)}, f32[12,128]{1,0:T(8,128)S(1)}, u32[]{:S(2)}, u32[]{:S(2)}) collective-permute-start(f32[12,128]{1,0:T(8,128)S(1)} %get-tuple-element.93), channel_id=1, source_target_pairs={{0,1},{1,0},{2,3},{3,2},{4,5},{5,4},{6,7},{7,6},{8,9},{9,8},{10,11... | collective-permute-start | bytes 18440 | tf_op jit(solution)/shard_map/ppermute | solution.py:453
  43.2 3.6 %collective-permute-start.23 = (f32[8,128]{1,0:T(8,128)S(1)}, f32[8,128]{1,0:T(8,128)S(1)}, u32[]{:S(2)}, u32[]{:S(2)}) collective-permute-start(f32[8,128]{1,0:T(8,128)S(1)} %slice_dynamic-update-slice_fusion.1), channel_id=1, source_target_pairs={{0,8},{1,17},{2,10},{3,19},{4,12},{5,21},{6,14},{7,23},{8,0},{9,25... | collective-permute-start | bytes 12296 | tf_op jit(solution)/shard_map/ppermute | solution.py:461
  46.9 5.1 %collective-permute-start.24 = (f32[8,128]{1,0:T(8,128)S(1)}, f32[8,128]{1,0:T(8,128)S(1)}, u32[]{:S(2)}, u32[]{:S(2)}) collective-permute-start(f32[8,128]{1,0:T(8,128)S(1)} %collective-permute-done.23.refs_7_), channel_id=1, source_target_pairs={{0,1},{1,0},{2,3},{3,2},{4,5},{5,4},{6,7},{7,6},{8,9},{9,8},{10,11... | collective-permute-start | bytes 12296 | tf_op jit(solution)/shard_map/ppermute | solution.py:462
  46.9 5.0 %collective-permute-start.20 = (f32[4,128]{1,0:T(4,128)S(1)}, f32[4,128]{1,0:T(4,128)S(1)}, u32[]{:S(2)}, u32[]{:S(2)}) collective-permute-start(f32[4,128]{1,0:T(4,128)S(1)} %get-tuple-element.91), channel_id=1, source_target_pairs={{0,2},{2,0},{4,6},{6,4},{8,10},{10,8},{12,14},{14,12},{16,18},{18,... | collective-permute-start | bytes 6152 | tf_op jit(solution)/shard_map/ppermute | solution.py:448
  48.4 3.6 %collective-permute-start.21 = (f32[4,128]{1,0:T(4,128)S(1)}, f32[4,128]{1,0:T(4,128)S(1)}, u32[]{:S(2)}, u32[]{:S(2)}) collective-permute-start(f32[4,128]{1,0:T(4,128)S(1)} %get-tuple-element.92), channel_id=1, source_target_pairs={{0,4},{2,6},{4,0},{6,2},{8,12},{10,14},{12,8},{14,10},{16,20},{18,... | collective-permute-start | bytes 6152 | tf_op jit(solution)/shard_map/ppermute | solution.py:448
  52.1 1.2 %collective-permute-start.27 = (f32[12,128]{1,0:T(8,128)S(1)}, f32[12,128]{1,0:T(8,128)S(1)}, u32[]{:S(2)}, u32[]{:S(2)}) collective-permute-start(f32[12,128]{1,0:T(8,128)S(1)} %get-tuple-element.99), channel_id=1, source_target_pairs={{0,1},{1,0},{2,3},{3,2},{4,5},{5,4},{6,7},{7,6},{8,9},{9,8},{10,11... | collective-permute-start | bytes 18440 | tf_op jit(solution)/shard_map/ppermute | solution.py:453
  53.4 3.6 %collective-permute-start.28 = (f32[8,128]{1,0:T(8,128)S(1)}, f32[8,128]{1,0:T(8,128)S(1)}, u32[]{:S(2)}, u32[]{:S(2)}) collective-permute-start(f32[8,128]{1,0:T(8,128)S(1)} %slice_dynamic-update-slice_fusion), channel_id=1, source_target_pairs={{0,8},{1,17},{2,10},{3,19},{4,12},{5,21},{6,14},{7,23},{8,0},{9,25... | collective-permute-start | bytes 12296 | tf_op jit(solution)/shard_map/ppermute | solution.py:461
  57.0 4.1 %collective-permute-start.29 = (f32[8,128]{1,0:T(8,128)S(1)}, f32[8,128]{1,0:T(8,128)S(1)}, u32[]{:S(2)}, u32[]{:S(2)}) collective-permute-start(f32[8,128]{1,0:T(8,128)S(1)} %collective-permute-done.28.refs_15_), channel_id=1, source_target_pairs={{0,1},{1,0},{2,3},{3,2},{4,5},{5,4},{6,7},{7,6},{8,9},{9,8},{10,11... | collective-permute-start | bytes 12296 | tf_op jit(solution)/shard_map/ppermute | solution.py:462
  57.0 4.0 %collective-permute-start.25 = (f32[4,128]{1,0:T(4,128)S(1)}, f32[4,128]{1,0:T(4,128)S(1)}, u32[]{:S(2)}, u32[]{:S(2)}) collective-permute-start(f32[4,128]{1,0:T(4,128)S(1)} %get-tuple-element.97), channel_id=1, source_target_pairs={{0,2},{2,0},{4,6},{6,4},{8,10},{10,8},{12,14},{14,12},{16,18},{18,... | collective-permute-start | bytes 6152 | tf_op jit(solution)/shard_map/ppermute | solution.py:448
  57.5 3.6 %collective-permute-start.26 = (f32[4,128]{1,0:T(4,128)S(1)}, f32[4,128]{1,0:T(4,128)S(1)}, u32[]{:S(2)}, u32[]{:S(2)}) collective-permute-start(f32[4,128]{1,0:T(4,128)S(1)} %get-tuple-element.98), channel_id=1, source_target_pairs={{0,4},{2,6},{4,0},{6,2},{8,12},{10,14},{12,8},{14,10},{16,20},{18,... | collective-permute-start | bytes 6152 | tf_op jit(solution)/shard_map/ppermute | solution.py:448
  (5 other events, 32.4 us)

commit v6 on v5

--- a/solution.py
+++ b/solution.py
@@ -37,11 +37,6 @@
 
 def subs(shape=(SUB, LANE)):
     return lax.broadcasted_iota(i32, shape, len(shape) - 2)
-
-
-def two_parts(value):
-    high = value.astype(bf16)
-    return high, (value - high.astype(f32)).astype(bf16)
 
 
 def three_parts(value):
@@ -137,6 +132,7 @@
         hot = one_hot(columns[k : k + 1, :], own_rows).astype(bf16)
         hot_ref[k * own_rows : (k + 1) * own_rows, 0:LANE] = hot
         hot_ref[k * own_rows : (k + 1) * own_rows, LANE : 2 * LANE] = hot
+        hot_ref[k * own_rows : (k + 1) * own_rows, 2 * LANE : 3 * LANE] = hot
         wide_ref[k] = couplings_ref[k].astype(f32)
 
 
@@ -252,7 +248,7 @@
     end = rows + sum(count for _, count, _ in places)
     if end < LANE:
         extended_ref[end:LANE, :] = jnp.zeros((LANE - end, LANE), f32)
-    return jnp.concatenate(two_parts(extended_ref[...]), axis=0)
+    return jnp.concatenate(three_parts(extended_ref[...]), axis=0)
 
 
 def coupled(base, hot, wide_ref, parts):
@@ -505,9 +501,9 @@
                 functools.partial(setup_body, face, moves),
                 [
                     sent_out,
-                    ((neighbours * rows, 2 * LANE), bf16),
+                    ((neighbours * rows, 3 * LANE), bf16),
                     ((neighbours, rows, width), f32),
-                    ((neighbours * send_pad, 2 * LANE), bf16),
+                    ((neighbours * send_pad, 3 * LANE), bf16),
                     ((neighbours, send_pad, width), f32),
                 ],
                 (columns.T, couplings.transpose(1, 0, 2), place, own, send_ones, sent, shifts),
@@ -530,7 +526,7 @@
             keep = k + 2 < powers
             parts, *outgoing = run(
                 functools.partial(sends_body, places, keep),
-                [((2 * LANE, width), bf16)] + ([sent_out] if keep else []) + piece_outs,
+                [((3 * LANE, width), bf16)] + ([sent_out] if keep else []) + piece_outs,
                 (base, vectors[-1], send_hot, send_wide, *received),
                 cost=(1_000_000, 1_000_000),
                 scratch=extended,

time: 76.8 us -> 77 us (level)
  no operation moved by 1% of the time
where the time goes in v6:
time: 77 us; the launch traced here: 76.8 us
  starting transfers between devices  26.5 us (34%)
  waiting for transfers between devices  19.4 us (25%)
  Pallas kernels  16.2 us (21%)
  blocking collectives  12.9 us (17%)
  between operations  0.96 us (1%)
  local copies, waits for them, and re-layouts  0.89 us (1%)
    pallas_call x26, Pallas kernels, run(): pl.pallas_call(body, out_shape=[jax.ShapeDtypeStruct(shape, dtype) for sh...  16.2 us
    ppermute x12, starting transfers between devices, with_partner(): return lax.ppermute(piece, 'dom', [(i, i ^ 1 << level) for i in range(dom)])  14.5 us
    all_to_all x1, blocking collectives, shards(): lax.all_to_all(jnp.tile(packet, (dom * col, 1)), everyone, 0, 0, tiled=True)  12.9 us
    ppermute x6, waiting for transfers between devices, exchange_relay(): pair = lax.ppermute(pair, ('dom', 'col'), far_pairs)  11.7 us
    ppermute x6, starting transfers between devices, exchange_relay(): pair = lax.ppermute(pair, ('dom', 'col'), far_pairs)  10.8 us
    ppermute x6, waiting for transfers between devices, exchange_relay(): side = lax.ppermute(side, 'col', swapped)  6.62 us
  transfers between devices with their start and end apart: 30, of which 17 were waited for; matrix products, arithmetic and copies ran while one was open for 0% of the time, Pallas kernels for 16%

profile of v6, /device:TPU:0, one launch (start us, length us, event | category | flops | bytes accessed | tf_op | source)
XLA Modules:
  0.0 76.8 jit_solution(17853388638346009103)
XLA Ops:
  3.2 2.9 %collective-permute-start.3 = (f32[8,128]{1,0:T(8,128)S(1)}, f32[8,128]{1,0:T(8,128)S(1)}, u32[]{:S(2)}, u32[]{:S(2)}) collective-permute-start(f32[8,128]{1,0:T(8,128)S(1)} %slice_dynamic-update-slice_fusion.5), channel_id=1, source_target_pairs={{0,8},{1,17},{2,10},{3,19},{4,12},{5,21},{6,14},{7,23},{8,0},{9,25... | collective-permute-start | bytes 12296 | tf_op jit(solution)/shard_map/ppermute | solution.py:457
  6.1 1.6 %collective-permute-done.3.refs_7_ = f32[8,128]{1,0:T(8,128)S(1)} collective-permute-done((f32[8,128]{1,0:T(8,128)S(1)}, f32[8,128]{1,0:T(8,128)S(1)}, u32[]{:S(2)}, u32[]{:S(2)}) %collective-permute-start.3) | collective-permute-done | bytes 4128 | tf_op jit(solution)/shard_map/ppermute | solution.py:457
  8.0 1.6 %collective-permute-start = (f32[4,128]{1,0:T(4,128)S(1)}, f32[4,128]{1,0:T(4,128)S(1)}, u32[]{:S(2)}, u32[]{:S(2)}) collective-permute-start(f32[4,128]{1,0:T(4,128)S(1)} %get-tuple-element.60), channel_id=1, source_target_pairs={{0,2},{2,0},{4,6},{6,4},{8,10},{10,8},{12,14},{14,12},{16,18},{18,... | collective-permute-start | bytes 6152 | tf_op jit(solution)/shard_map/ppermute | solution.py:444
  9.6 1.5 %collective-permute-start.1 = (f32[4,128]{1,0:T(4,128)S(1)}, f32[4,128]{1,0:T(4,128)S(1)}, u32[]{:S(2)}, u32[]{:S(2)}) collective-permute-start(f32[4,128]{1,0:T(4,128)S(1)} %get-tuple-element.61), channel_id=1, source_target_pairs={{0,4},{2,6},{4,0},{6,2},{8,12},{10,14},{12,8},{14,10},{16,20},{18,... | collective-permute-start | bytes 6152 | tf_op jit(solution)/shard_map/ppermute | solution.py:444
  13.5 1.2 %collective-permute-done.7.refs_6_ = f32[12,128]{1,0:T(8,128)S(1)} collective-permute-done((f32[12,128]{1,0:T(8,128)S(1)}, f32[12,128]{1,0:T(8,128)S(1)}, u32[]{:S(2)}, u32[]{:S(2)}) %collective-permute-start.7) | collective-permute-done | bytes 6176 | tf_op jit(solution)/shard_map/ppermute | solution.py:449
  14.7 1.6 %collective-permute-start.8 = (f32[8,128]{1,0:T(8,128)S(1)}, f32[8,128]{1,0:T(8,128)S(1)}, u32[]{:S(2)}, u32[]{:S(2)}) collective-permute-start(f32[8,128]{1,0:T(8,128)S(1)} %slice_dynamic-update-slice_fusion.4), channel_id=1, source_target_pairs={{0,8},{1,17},{2,10},{3,19},{4,12},{5,21},{6,14},{7,23},{8,0},{9,25... | collective-permute-start | bytes 12296 | tf_op jit(solution)/shard_map/ppermute | solution.py:457
  16.2 2.0 %collective-permute-done.8.refs_7_ = f32[8,128]{1,0:T(8,128)S(1)} collective-permute-done((f32[8,128]{1,0:T(8,128)S(1)}, f32[8,128]{1,0:T(8,128)S(1)}, u32[]{:S(2)}, u32[]{:S(2)}) %collective-permute-start.8) | collective-permute-done | bytes 4128 | tf_op jit(solution)/shard_map/ppermute | solution.py:457
  18.7 1.7 %collective-permute-start.6 = (f32[4,128]{1,0:T(4,128)S(1)}, f32[4,128]{1,0:T(4,128)S(1)}, u32[]{:S(2)}, u32[]{:S(2)}) collective-permute-start(f32[4,128]{1,0:T(4,128)S(1)} %get-tuple-element.68), channel_id=1, source_target_pairs={{0,4},{2,6},{4,0},{6,2},{8,12},{10,14},{12,8},{14,10},{16,20},{18,... | collective-permute-start | bytes 6152 | tf_op jit(solution)/shard_map/ppermute | solution.py:444
  22.9 1.2 %collective-permute-done.12.refs_6_ = f32[12,128]{1,0:T(8,128)S(1)} collective-permute-done((f32[12,128]{1,0:T(8,128)S(1)}, f32[12,128]{1,0:T(8,128)S(1)}, u32[]{:S(2)}, u32[]{:S(2)}) %collective-permute-start.12) | collective-permute-done | bytes 6176 | tf_op jit(solution)/shard_map/ppermute | solution.py:449
  24.1 1.6 %collective-permute-start.13 = (f32[8,128]{1,0:T(8,128)S(1)}, f32[8,128]{1,0:T(8,128)S(1)}, u32[]{:S(2)}, u32[]{:S(2)}) collective-permute-start(f32[8,128]{1,0:T(8,128)S(1)} %slice_dynamic-update-slice_fusion.3), channel_id=1, source_target_pairs={{0,8},{1,17},{2,10},{3,19},{4,12},{5,21},{6,14},{7,23},{8,0},{9,25... | collective-permute-start | bytes 12296 | tf_op jit(solution)/shard_map/ppermute | solution.py:457
  25.6 2.0 %collective-permute-done.13.refs_7_ = f32[8,128]{1,0:T(8,128)S(1)} collective-permute-done((f32[8,128]{1,0:T(8,128)S(1)}, f32[8,128]{1,0:T(8,128)S(1)}, u32[]{:S(2)}, u32[]{:S(2)}) %collective-permute-start.13) | collective-permute-done | bytes 4128 | tf_op jit(solution)/shard_map/ppermute | solution.py:457
  27.7 1.5 %collective-permute-start.10 = (f32[4,128]{1,0:T(4,128)S(1)}, f32[4,128]{1,0:T(4,128)S(1)}, u32[]{:S(2)}, u32[]{:S(2)}) collective-permute-start(f32[4,128]{1,0:T(4,128)S(1)} %get-tuple-element.75), channel_id=1, source_target_pairs={{0,2},{2,0},{4,6},{6,4},{8,10},{10,8},{12,14},{14,12},{16,18},{18,... | collective-permute-start | bytes 6152 | tf_op jit(solution)/shard_map/ppermute | solution.py:444
  29.2 1.3 %collective-permute-start.11 = (f32[4,128]{1,0:T(4,128)S(1)}, f32[4,128]{1,0:T(4,128)S(1)}, u32[]{:S(2)}, u32[]{:S(2)}) collective-permute-start(f32[4,128]{1,0:T(4,128)S(1)} %get-tuple-element.76), channel_id=1, source_target_pairs={{0,4},{2,6},{4,0},{6,2},{8,12},{10,14},{12,8},{14,10},{16,20},{18,... | collective-permute-start | bytes 6152 | tf_op jit(solution)/shard_map/ppermute | solution.py:444
  30.8 1.1 %shard_map.104.refs_3_.own_ref = f32[96,128]{1,0:T(8,128)S(1)} custom-call(bf16[12288,128]{1,0:T(8,128)(2,1)S(1)} %bitcast.7, f32[96,128]{1,0:T(8,128)S(1)} %shard_map.103.vector_ref.refs_2_.refs_1_.refs_8_), custom_call_target="tpu_custom_call" | custom-call | flops 20000000 | bytes 4000000 | tf_op jit(solution)/shard_map/pallas_call | solution.py:23
  33.0 1.2 %collective-permute-done.17.refs_6_ = f32[12,128]{1,0:T(8,128)S(1)} collective-permute-done((f32[12,128]{1,0:T(8,128)S(1)}, f32[12,128]{1,0:T(8,128)S(1)}, u32[]{:S(2)}, u32[]{:S(2)}) %collective-permute-start.17) | collective-permute-done | bytes 6176 | tf_op jit(solution)/shard_map/ppermute | solution.py:449
  34.2 1.6 %collective-permute-start.18 = (f32[8,128]{1,0:T(8,128)S(1)}, f32[8,128]{1,0:T(8,128)S(1)}, u32[]{:S(2)}, u32[]{:S(2)}) collective-permute-start(f32[8,128]{1,0:T(8,128)S(1)} %slice_dynamic-update-slice_fusion.2), channel_id=1, source_target_pairs={{0,8},{1,17},{2,10},{3,19},{4,12},{5,21},{6,14},{7,23},{8,0},{9,25... | collective-permute-start | bytes 12296 | tf_op jit(solution)/shard_map/ppermute | solution.py:457
  35.8 2.0 %collective-permute-done.18.refs_7_ = f32[8,128]{1,0:T(8,128)S(1)} collective-permute-done((f32[8,128]{1,0:T(8,128)S(1)}, f32[8,128]{1,0:T(8,128)S(1)}, u32[]{:S(2)}, u32[]{:S(2)}) %collective-permute-start.18) | collective-permute-done | bytes 4128 | tf_op jit(solution)/shard_map/ppermute | solution.py:457
  38.3 1.3 %collective-permute-start.16 = (f32[4,128]{1,0:T(4,128)S(1)}, f32[4,128]{1,0:T(4,128)S(1)}, u32[]{:S(2)}, u32[]{:S(2)}) collective-permute-start(f32[4,128]{1,0:T(4,128)S(1)} %get-tuple-element.84), channel_id=1, source_target_pairs={{0,4},{2,6},{4,0},{6,2},{8,12},{10,14},{12,8},{14,10},{16,20},{18,... | collective-permute-start | bytes 6152 | tf_op jit(solution)/shard_map/ppermute | solution.py:444
  39.9 1.1 %shard_map.108.refs_4_.own_ref = f32[96,128]{1,0:T(8,128)S(1)} custom-call(bf16[12288,128]{1,0:T(8,128)(2,1)S(1)} %bitcast.8, f32[96,128]{1,0:T(8,128)S(1)} %shard_map.107.vector_ref.refs_3_.refs_1_.refs_9_), custom_call_target="tpu_custom_call" | custom-call | flops 20000000 | bytes 4000000 | tf_op jit(solution)/shard_map/pallas_call | solution.py:23
  42.2 1.2 %collective-permute-done.22.refs_6_ = f32[12,128]{1,0:T(8,128)S(1)} collective-permute-done((f32[12,128]{1,0:T(8,128)S(1)}, f32[12,128]{1,0:T(8,128)S(1)}, u32[]{:S(2)}, u32[]{:S(2)}) %collective-permute-start.22) | collective-permute-done | bytes 6176 | tf_op jit(solution)/shard_map/ppermute | solution.py:449
  43.4 1.6 %collective-permute-start.23 = (f32[8,128]{1,0:T(8,128)S(1)}, f32[8,128]{1,0:T(8,128)S(1)}, u32[]{:S(2)}, u32[]{:S(2)}) collective-permute-start(f32[8,128]{1,0:T(8,128)S(1)} %slice_dynamic-update-slice_fusion.1), channel_id=1, source_target_pairs={{0,8},{1,17},{2,10},{3,19},{4,12},{5,21},{6,14},{7,23},{8,0},{9,25... | collective-permute-start | bytes 12296 | tf_op jit(solution)/shard_map/ppermute | solution.py:457
  45.0 2.0 %collective-permute-done.23.refs_7_ = f32[8,128]{1,0:T(8,128)S(1)} collective-permute-done((f32[8,128]{1,0:T(8,128)S(1)}, f32[8,128]{1,0:T(8,128)S(1)}, u32[]{:S(2)}, u32[]{:S(2)}) %collective-permute-start.23) | collective-permute-done | bytes 4128 | tf_op jit(solution)/shard_map/ppermute | solution.py:457
  47.0 1.5 %collective-permute-start.20 = (f32[4,128]{1,0:T(4,128)S(1)}, f32[4,128]{1,0:T(4,128)S(1)}, u32[]{:S(2)}, u32[]{:S(2)}) collective-permute-start(f32[4,128]{1,0:T(4,128)S(1)} %get-tuple-element.91), channel_id=1, source_target_pairs={{0,2},{2,0},{4,6},{6,4},{8,10},{10,8},{12,14},{14,12},{16,18},{18,... | collective-permute-start | bytes 6152 | tf_op jit(solution)/shard_map/ppermute | solution.py:444
  48.5 1.3 %collective-permute-start.21 = (f32[4,128]{1,0:T(4,128)S(1)}, f32[4,128]{1,0:T(4,128)S(1)}, u32[]{:S(2)}, u32[]{:S(2)}) collective-permute-start(f32[4,128]{1,0:T(4,128)S(1)} %get-tuple-element.92), channel_id=1, source_target_pairs={{0,4},{2,6},{4,0},{6,2},{8,12},{10,14},{12,8},{14,10},{16,20},{18,... | collective-permute-start | bytes 6152 | tf_op jit(solution)/shard_map/ppermute | solution.py:444
  52.4 1.2 %collective-permute-done.27.refs_14_ = f32[12,128]{1,0:T(8,128)S(1)} collective-permute-done((f32[12,128]{1,0:T(8,128)S(1)}, f32[12,128]{1,0:T(8,128)S(1)}, u32[]{:S(2)}, u32[]{:S(2)}) %collective-permute-start.27) | collective-permute-done | bytes 6176 | tf_op jit(solution)/shard_map/ppermute | solution.py:449
  53.5 1.6 %collective-permute-start.28 = (f32[8,128]{1,0:T(8,128)S(1)}, f32[8,128]{1,0:T(8,128)S(1)}, u32[]{:S(2)}, u32[]{:S(2)}) collective-permute-start(f32[8,128]{1,0:T(8,128)S(1)} %slice_dynamic-update-slice_fusion), channel_id=1, source_target_pairs={{0,8},{1,17},{2,10},{3,19},{4,12},{5,21},{6,14},{7,23},{8,0},{9,25... | collective-permute-start | bytes 12296 | tf_op jit(solution)/shard_map/ppermute | solution.py:457
  55.1 2.0 %collective-permute-done.28.refs_15_ = f32[8,128]{1,0:T(8,128)S(1)} collective-permute-done((f32[8,128]{1,0:T(8,128)S(1)}, f32[8,128]{1,0:T(8,128)S(1)}, u32[]{:S(2)}, u32[]{:S(2)}) %collective-permute-start.28) | collective-permute-done | bytes 4128 | tf_op jit(solution)/shard_map/ppermute | solution.py:457
  57.7 1.3 %collective-permute-start.26 = (f32[4,128]{1,0:T(4,128)S(1)}, f32[4,128]{1,0:T(4,128)S(1)}, u32[]{:S(2)}, u32[]{:S(2)}) collective-permute-start(f32[4,128]{1,0:T(4,128)S(1)} %get-tuple-element.98), channel_id=1, source_target_pairs={{0,4},{2,6},{4,0},{6,2},{8,12},{10,14},{12,8},{14,10},{16,20},{18,... | collective-permute-start | bytes 6152 | tf_op jit(solution)/shard_map/ppermute | solution.py:444
  60.0 1.1 %shard_map.116.refs_0_ = f32[96,128]{1,0:T(8,128)S(1)} custom-call(bf16[12288,128]{1,0:T(8,128)(2,1)S(1)} %bitcast.10, f32[96,128]{1,0:T(8,128)S(1)} %shard_map.115.vector_ref.refs_5_.refs_11_), custom_call_target="tpu_custom_call" | custom-call | flops 20000000 | bytes 4000000 | tf_op jit(solution)/shard_map/pallas_call | solution.py:23
  61.3 1.2 %shard_map.118 = (f32[96,128]{1,0:T(8,128)S(1)}, f32[4,128]{1,0:T(4,128)S(1)}) custom-call(f32[96,128]{1,0:T(8,128)S(1)} %shard_map.116.refs_0_, bf16[576,384]{1,0:T(8,128)(2,1)S(1)} %get-tuple-element.55.hot_ref.refs_1_, f32[6,96,128]{2,1,0:T(8,128)S(1)} %get-tuple-element.56.wide_ref.refs_2_, f32[1,6]{1,0:T(1,128)S(1)} %bitcast.23, ...), custom_call_target="tpu_custom_call" | custom-call | flops 4000000 | bytes 2000000 | tf_op jit(solution)/shard_map/pallas_call | solution.py:23
  62.5 12.9 %all_to_all.8 = f32[32,4,128]{2,1,0:T(4,128)S(1)} all-to-all(f32[32,4,128]{2,1,0:T(4,128)S(1)} %tile.2), channel_id=1, replica_groups=mesh['dom'=16,'col'=2] {'dom','col'}, dimensions={0} | all-to-all | bytes 131072 | tf_op jit(solution)/shard_map/all_to_all | solution.py:538
  75.4 1.4 %shard_map.119 = (f32[7,96,128]{2,1,0:T(8,128)}, f32[7,7]{1,0:T(8,128)}, f32[7,7]{1,0:T(8,128)}) custom-call(f32[128,128]{1,0:T(8,128)S(1)} %bitcast.11, f32[96,128]{1,0:T(8,128)S(1)} %copy-done.2, f32[96,128]{1,0:T(8,128)S(1)} %shard_map.99.vector_ref.refs_1_.refs_7_, f32[96,128]{1,0:T(8,128)S(1)} %shard_map.103.vector_ref.refs_2_.refs_1_.refs_8_, ...), custom_call_target="tpu_custom_call" | custom-call | flops 5000000 | bytes 1000000 | tf_op jit(solution)/shard_map/pallas_call | solution.py:23
  (77 shorter events, 15.5 us)
Async XLA Ops:
  1.8 10.6 %copy-start.3 = (bf16[96,6,128]{2,0,1:T(8,128)(2,1)S(1)}, bf16[96,6,128]{2,0,1:T(8,128)(2,1)}, u32[]{:S(2)}) copy-start(bf16[96,6,128]{2,0,1:T(8,128)(2,1)} %param.8) | copy-start | bytes 442372
  1.8 10.6 %copy-start.4 = (f32[6]{0:T(128)S(1)}, f32[6]{0:T(128)}, u32[]{:S(2)}) copy-start(f32[6]{0:T(128)} %param.11) | copy-start | bytes 76
  1.8 1.4 %collective-permute-start.2 = (f32[12,128]{1,0:T(8,128)S(1)}, f32[12,128]{1,0:T(8,128)S(1)}, u32[]{:S(2)}, u32[]{:S(2)}) collective-permute-start(f32[12,128]{1,0:T(8,128)S(1)} %get-tuple-element.62), channel_id=1, source_target_pairs={{0,1},{1,0},{2,3},{3,2},{4,5},{5,4},{6,7},{7,6},{8,9},{9,8},{10,11... | collective-permute-start | bytes 18440 | tf_op jit(solution)/shard_map/ppermute | solution.py:449
  3.2 4.5 %collective-permute-start.3 = (f32[8,128]{1,0:T(8,128)S(1)}, f32[8,128]{1,0:T(8,128)S(1)}, u32[]{:S(2)}, u32[]{:S(2)}) collective-permute-start(f32[8,128]{1,0:T(8,128)S(1)} %slice_dynamic-update-slice_fusion.5), channel_id=1, source_target_pairs={{0,8},{1,17},{2,10},{3,19},{4,12},{5,21},{6,14},{7,23},{8,0},{9,25... | collective-permute-start | bytes 12296 | tf_op jit(solution)/shard_map/ppermute | solution.py:457
  7.7 5.5 %collective-permute-start.4 = (f32[8,128]{1,0:T(8,128)S(1)}, f32[8,128]{1,0:T(8,128)S(1)}, u32[]{:S(2)}, u32[]{:S(2)}) collective-permute-start(f32[8,128]{1,0:T(8,128)S(1)} %collective-permute-done.3.refs_7_), channel_id=1, source_target_pairs={{0,1},{1,0},{2,3},{3,2},{4,5},{5,4},{6,7},{7,6},{8,9},{9,8},{10,11... | collective-permute-start | bytes 12296 | tf_op jit(solution)/shard_map/ppermute | solution.py:458
  8.0 4.7 %collective-permute-start = (f32[4,128]{1,0:T(4,128)S(1)}, f32[4,128]{1,0:T(4,128)S(1)}, u32[]{:S(2)}, u32[]{:S(2)}) collective-permute-start(f32[4,128]{1,0:T(4,128)S(1)} %get-tuple-element.60), channel_id=1, source_target_pairs={{0,2},{2,0},{4,6},{6,4},{8,10},{10,8},{12,14},{14,12},{16,18},{18,... | collective-permute-start | bytes 6152 | tf_op jit(solution)/shard_map/ppermute | solution.py:444
  9.6 3.6 %collective-permute-start.1 = (f32[4,128]{1,0:T(4,128)S(1)}, f32[4,128]{1,0:T(4,128)S(1)}, u32[]{:S(2)}, u32[]{:S(2)}) collective-permute-start(f32[4,128]{1,0:T(4,128)S(1)} %get-tuple-element.61), channel_id=1, source_target_pairs={{0,4},{2,6},{4,0},{6,2},{8,12},{10,14},{12,8},{14,10},{16,20},{18,... | collective-permute-start | bytes 6152 | tf_op jit(solution)/shard_map/ppermute | solution.py:444
  13.4 1.2 %collective-permute-start.7 = (f32[12,128]{1,0:T(8,128)S(1)}, f32[12,128]{1,0:T(8,128)S(1)}, u32[]{:S(2)}, u32[]{:S(2)}) collective-permute-start(f32[12,128]{1,0:T(8,128)S(1)} %get-tuple-element.69), channel_id=1, source_target_pairs={{0,1},{1,0},{2,3},{3,2},{4,5},{5,4},{6,7},{7,6},{8,9},{9,8},{10,11... | collective-permute-start | bytes 18440 | tf_op jit(solution)/shard_map/ppermute | solution.py:449
  14.7 3.6 %collective-permute-start.8 = (f32[8,128]{1,0:T(8,128)S(1)}, f32[8,128]{1,0:T(8,128)S(1)}, u32[]{:S(2)}, u32[]{:S(2)}) collective-permute-start(f32[8,128]{1,0:T(8,128)S(1)} %slice_dynamic-update-slice_fusion.4), channel_id=1, source_target_pairs={{0,8},{1,17},{2,10},{3,19},{4,12},{5,21},{6,14},{7,23},{8,0},{9,25... | collective-permute-start | bytes 12296 | tf_op jit(solution)/shard_map/ppermute | solution.py:457
  18.3 4.3 %collective-permute-start.9 = (f32[8,128]{1,0:T(8,128)S(1)}, f32[8,128]{1,0:T(8,128)S(1)}, u32[]{:S(2)}, u32[]{:S(2)}) collective-permute-start(f32[8,128]{1,0:T(8,128)S(1)} %collective-permute-done.8.refs_7_), channel_id=1, source_target_pairs={{0,1},{1,0},{2,3},{3,2},{4,5},{5,4},{6,7},{7,6},{8,9},{9,8},{10,11... | collective-permute-start | bytes 12296 | tf_op jit(solution)/shard_map/ppermute | solution.py:458
  18.3 4.3 %collective-permute-start.5 = (f32[4,128]{1,0:T(4,128)S(1)}, f32[4,128]{1,0:T(4,128)S(1)}, u32[]{:S(2)}, u32[]{:S(2)}) collective-permute-start(f32[4,128]{1,0:T(4,128)S(1)} %get-tuple-element.67), channel_id=1, source_target_pairs={{0,2},{2,0},{4,6},{6,4},{8,10},{10,8},{12,14},{14,12},{16,18},{18,... | collective-permute-start | bytes 6152 | tf_op jit(solution)/shard_map/ppermute | solution.py:444
  18.7 3.9 %collective-permute-start.6 = (f32[4,128]{1,0:T(4,128)S(1)}, f32[4,128]{1,0:T(4,128)S(1)}, u32[]{:S(2)}, u32[]{:S(2)}) collective-permute-start(f32[4,128]{1,0:T(4,128)S(1)} %get-tuple-element.68), channel_id=1, source_target_pairs={{0,4},{2,6},{4,0},{6,2},{8,12},{10,14},{12,8},{14,10},{16,20},{18,... | collective-permute-start | bytes 6152 | tf_op jit(solution)/shard_map/ppermute | solution.py:444
  22.8 1.2 %collective-permute-start.12 = (f32[12,128]{1,0:T(8,128)S(1)}, f32[12,128]{1,0:T(8,128)S(1)}, u32[]{:S(2)}, u32[]{:S(2)}) collective-permute-start(f32[12,128]{1,0:T(8,128)S(1)} %get-tuple-element.77), channel_id=1, source_target_pairs={{0,1},{1,0},{2,3},{3,2},{4,5},{5,4},{6,7},{7,6},{8,9},{9,8},{10,11... | collective-permute-start | bytes 18440 | tf_op jit(solution)/shard_map/ppermute | solution.py:449
  24.1 3.6 %collective-permute-start.13 = (f32[8,128]{1,0:T(8,128)S(1)}, f32[8,128]{1,0:T(8,128)S(1)}, u32[]{:S(2)}, u32[]{:S(2)}) collective-permute-start(f32[8,128]{1,0:T(8,128)S(1)} %slice_dynamic-update-slice_fusion.3), channel_id=1, source_target_pairs={{0,8},{1,17},{2,10},{3,19},{4,12},{5,21},{6,14},{7,23},{8,0},{9,25... | collective-permute-start | bytes 12296 | tf_op jit(solution)/shard_map/ppermute | solution.py:457
  27.7 5.1 %collective-permute-start.14 = (f32[8,128]{1,0:T(8,128)S(1)}, f32[8,128]{1,0:T(8,128)S(1)}, u32[]{:S(2)}, u32[]{:S(2)}) collective-permute-start(f32[8,128]{1,0:T(8,128)S(1)} %collective-permute-done.13.refs_7_), channel_id=1, source_target_pairs={{0,1},{1,0},{2,3},{3,2},{4,5},{5,4},{6,7},{7,6},{8,9},{9,8},{10,11... | collective-permute-start | bytes 12296 | tf_op jit(solution)/shard_map/ppermute | solution.py:458
  27.7 4.9 %collective-permute-start.10 = (f32[4,128]{1,0:T(4,128)S(1)}, f32[4,128]{1,0:T(4,128)S(1)}, u32[]{:S(2)}, u32[]{:S(2)}) collective-permute-start(f32[4,128]{1,0:T(4,128)S(1)} %get-tuple-element.75), channel_id=1, source_target_pairs={{0,2},{2,0},{4,6},{6,4},{8,10},{10,8},{12,14},{14,12},{16,18},{18,... | collective-permute-start | bytes 6152 | tf_op jit(solution)/shard_map/ppermute | solution.py:444
  29.2 3.6 %collective-permute-start.11 = (f32[4,128]{1,0:T(4,128)S(1)}, f32[4,128]{1,0:T(4,128)S(1)}, u32[]{:S(2)}, u32[]{:S(2)}) collective-permute-start(f32[4,128]{1,0:T(4,128)S(1)} %get-tuple-element.76), channel_id=1, source_target_pairs={{0,4},{2,6},{4,0},{6,2},{8,12},{10,14},{12,8},{14,10},{16,20},{18,... | collective-permute-start | bytes 6152 | tf_op jit(solution)/shard_map/ppermute | solution.py:444
  33.0 1.2 %collective-permute-start.17 = (f32[12,128]{1,0:T(8,128)S(1)}, f32[12,128]{1,0:T(8,128)S(1)}, u32[]{:S(2)}, u32[]{:S(2)}) collective-permute-start(f32[12,128]{1,0:T(8,128)S(1)} %get-tuple-element.85), channel_id=1, source_target_pairs={{0,1},{1,0},{2,3},{3,2},{4,5},{5,4},{6,7},{7,6},{8,9},{9,8},{10,11... | collective-permute-start | bytes 18440 | tf_op jit(solution)/shard_map/ppermute | solution.py:449
  34.2 3.6 %collective-permute-start.18 = (f32[8,128]{1,0:T(8,128)S(1)}, f32[8,128]{1,0:T(8,128)S(1)}, u32[]{:S(2)}, u32[]{:S(2)}) collective-permute-start(f32[8,128]{1,0:T(8,128)S(1)} %slice_dynamic-update-slice_fusion.2), channel_id=1, source_target_pairs={{0,8},{1,17},{2,10},{3,19},{4,12},{5,21},{6,14},{7,23},{8,0},{9,25... | collective-permute-start | bytes 12296 | tf_op jit(solution)/shard_map/ppermute | solution.py:457
  37.8 4.1 %collective-permute-start.19 = (f32[8,128]{1,0:T(8,128)S(1)}, f32[8,128]{1,0:T(8,128)S(1)}, u32[]{:S(2)}, u32[]{:S(2)}) collective-permute-start(f32[8,128]{1,0:T(8,128)S(1)} %collective-permute-done.18.refs_7_), channel_id=1, source_target_pairs={{0,1},{1,0},{2,3},{3,2},{4,5},{5,4},{6,7},{7,6},{8,9},{9,8},{10,11... | collective-permute-start | bytes 12296 | tf_op jit(solution)/shard_map/ppermute | solution.py:458
  37.8 4.0 %collective-permute-start.15 = (f32[4,128]{1,0:T(4,128)S(1)}, f32[4,128]{1,0:T(4,128)S(1)}, u32[]{:S(2)}, u32[]{:S(2)}) collective-permute-start(f32[4,128]{1,0:T(4,128)S(1)} %get-tuple-element.83), channel_id=1, source_target_pairs={{0,2},{2,0},{4,6},{6,4},{8,10},{10,8},{12,14},{14,12},{16,18},{18,... | collective-permute-start | bytes 6152 | tf_op jit(solution)/shard_map/ppermute | solution.py:444
  38.3 3.6 %collective-permute-start.16 = (f32[4,128]{1,0:T(4,128)S(1)}, f32[4,128]{1,0:T(4,128)S(1)}, u32[]{:S(2)}, u32[]{:S(2)}) collective-permute-start(f32[4,128]{1,0:T(4,128)S(1)} %get-tuple-element.84), channel_id=1, source_target_pairs={{0,4},{2,6},{4,0},{6,2},{8,12},{10,14},{12,8},{14,10},{16,20},{18,... | collective-permute-start | bytes 6152 | tf_op jit(solution)/shard_map/ppermute | solution.py:444
  42.1 1.2 %collective-permute-start.22 = (f32[12,128]{1,0:T(8,128)S(1)}, f32[12,128]{1,0:T(8,128)S(1)}, u32[]{:S(2)}, u32[]{:S(2)}) collective-permute-start(f32[12,128]{1,0:T(8,128)S(1)} %get-tuple-element.93), channel_id=1, source_target_pairs={{0,1},{1,0},{2,3},{3,2},{4,5},{5,4},{6,7},{7,6},{8,9},{9,8},{10,11... | collective-permute-start | bytes 18440 | tf_op jit(solution)/shard_map/ppermute | solution.py:449
  43.4 3.6 %collective-permute-start.23 = (f32[8,128]{1,0:T(8,128)S(1)}, f32[8,128]{1,0:T(8,128)S(1)}, u32[]{:S(2)}, u32[]{:S(2)}) collective-permute-start(f32[8,128]{1,0:T(8,128)S(1)} %slice_dynamic-update-slice_fusion.1), channel_id=1, source_target_pairs={{0,8},{1,17},{2,10},{3,19},{4,12},{5,21},{6,14},{7,23},{8,0},{9,25... | collective-permute-start | bytes 12296 | tf_op jit(solution)/shard_map/ppermute | solution.py:457
  47.0 5.1 %collective-permute-start.24 = (f32[8,128]{1,0:T(8,128)S(1)}, f32[8,128]{1,0:T(8,128)S(1)}, u32[]{:S(2)}, u32[]{:S(2)}) collective-permute-start(f32[8,128]{1,0:T(8,128)S(1)} %collective-permute-done.23.refs_7_), channel_id=1, source_target_pairs={{0,1},{1,0},{2,3},{3,2},{4,5},{5,4},{6,7},{7,6},{8,9},{9,8},{10,11... | collective-permute-start | bytes 12296 | tf_op jit(solution)/shard_map/ppermute | solution.py:458
  47.0 5.0 %collective-permute-start.20 = (f32[4,128]{1,0:T(4,128)S(1)}, f32[4,128]{1,0:T(4,128)S(1)}, u32[]{:S(2)}, u32[]{:S(2)}) collective-permute-start(f32[4,128]{1,0:T(4,128)S(1)} %get-tuple-element.91), channel_id=1, source_target_pairs={{0,2},{2,0},{4,6},{6,4},{8,10},{10,8},{12,14},{14,12},{16,18},{18,... | collective-permute-start | bytes 6152 | tf_op jit(solution)/shard_map/ppermute | solution.py:444
  48.5 3.6 %collective-permute-start.21 = (f32[4,128]{1,0:T(4,128)S(1)}, f32[4,128]{1,0:T(4,128)S(1)}, u32[]{:S(2)}, u32[]{:S(2)}) collective-permute-start(f32[4,128]{1,0:T(4,128)S(1)} %get-tuple-element.92), channel_id=1, source_target_pairs={{0,4},{2,6},{4,0},{6,2},{8,12},{10,14},{12,8},{14,10},{16,20},{18,... | collective-permute-start | bytes 6152 | tf_op jit(solution)/shard_map/ppermute | solution.py:444
  52.3 1.2 %collective-permute-start.27 = (f32[12,128]{1,0:T(8,128)S(1)}, f32[12,128]{1,0:T(8,128)S(1)}, u32[]{:S(2)}, u32[]{:S(2)}) collective-permute-start(f32[12,128]{1,0:T(8,128)S(1)} %get-tuple-element.99), channel_id=1, source_target_pairs={{0,1},{1,0},{2,3},{3,2},{4,5},{5,4},{6,7},{7,6},{8,9},{9,8},{10,11... | collective-permute-start | bytes 18440 | tf_op jit(solution)/shard_map/ppermute | solution.py:449
  53.5 3.6 %collective-permute-start.28 = (f32[8,128]{1,0:T(8,128)S(1)}, f32[8,128]{1,0:T(8,128)S(1)}, u32[]{:S(2)}, u32[]{:S(2)}) collective-permute-start(f32[8,128]{1,0:T(8,128)S(1)} %slice_dynamic-update-slice_fusion), channel_id=1, source_target_pairs={{0,8},{1,17},{2,10},{3,19},{4,12},{5,21},{6,14},{7,23},{8,0},{9,25... | collective-permute-start | bytes 12296 | tf_op jit(solution)/shard_map/ppermute | solution.py:457
  57.1 4.1 %collective-permute-start.29 = (f32[8,128]{1,0:T(8,128)S(1)}, f32[8,128]{1,0:T(8,128)S(1)}, u32[]{:S(2)}, u32[]{:S(2)}) collective-permute-start(f32[8,128]{1,0:T(8,128)S(1)} %collective-permute-done.28.refs_15_), channel_id=1, source_target_pairs={{0,1},{1,0},{2,3},{3,2},{4,5},{5,4},{6,7},{7,6},{8,9},{9,8},{10,11... | collective-permute-start | bytes 12296 | tf_op jit(solution)/shard_map/ppermute | solution.py:458
  57.1 4.0 %collective-permute-start.25 = (f32[4,128]{1,0:T(4,128)S(1)}, f32[4,128]{1,0:T(4,128)S(1)}, u32[]{:S(2)}, u32[]{:S(2)}) collective-permute-start(f32[4,128]{1,0:T(4,128)S(1)} %get-tuple-element.97), channel_id=1, source_target_pairs={{0,2},{2,0},{4,6},{6,4},{8,10},{10,8},{12,14},{14,12},{16,18},{18,... | collective-permute-start | bytes 6152 | tf_op jit(solution)/shard_map/ppermute | solution.py:444
  57.7 3.6 %collective-permute-start.26 = (f32[4,128]{1,0:T(4,128)S(1)}, f32[4,128]{1,0:T(4,128)S(1)}, u32[]{:S(2)}, u32[]{:S(2)}) collective-permute-start(f32[4,128]{1,0:T(4,128)S(1)} %get-tuple-element.98), channel_id=1, source_target_pairs={{0,4},{2,6},{4,0},{6,2},{8,12},{10,14},{12,8},{14,10},{16,20},{18,... | collective-permute-start | bytes 6152 | tf_op jit(solution)/shard_map/ppermute | solution.py:444
  (5 other events, 31.4 us)
